TPU v7x, 128 devices: a whole 4x4x4 slice. The times are simulated.
128 devices in a mesh: img: 4 (over y_hi, core), gz: 32 (over x, y_lo, z).
Axes of the slice: x: 4, y: 4 (y_hi: 2, y_lo: 2; y = y_hi * 2 + y_lo), z: 4, core: 2. Of those that a mesh axis runs over, the one named last changes fastest.
Arguments:
- images: float32 [16, 5, 64, 128, 128], P('img', None, 'gz'), may hold values from -12 to 12
- centre: int32 [16], P('img'), may hold values from 1 to 14, as said below
- positions: float32 [16], P('img'), may hold values from 0 to 1
Outputs:
- path: float32 [16, 5, 64, 128, 128], P('img', None, 'gz')
Inputs may be any that keep to these rules, and one draw needn't show every extreme that they name: `centre`: centre_m lies within m - 1 to m + 1, clipped to 1 to 14; at the first target of each aligned block of 4 it is m - 1 and at the last m + 1, before clipping.
All inputs are finite; a program needn't handle non-finite values.
Results may differ from a plain program's by a relative error of at most 0.0003.
Values sent between devices are 32-bit elements; how exact they have to be, the bound alone decides.
No kernel may reach another device: no remote copies, remote signals or barrier semaphores. Data moves between devices by JAX's collectives and lax.ppermute only.
A program may use at most 64 MiB of HBM per device.

v0:
```python
import functools

import jax
import jax.numpy as jnp
import numpy as np
from jax import lax
from jax.experimental import pallas as pl
from jax.experimental.pallas import tpu as pltpu
from jax.sharding import PartitionSpec as P

NX = 128
NY = 128
NZ = 64
GROUPS = 32
IMAGES = 16
LOCAL = 4
CELLS = 5.0 * NZ * NX * NY
SMOOTH = 64.0
EPS = 1e-6
KEEP = 1.0 - 1.0 / SMOOTH
F32 = jnp.float32
BF16 = jnp.bfloat16


def real_basis(length):
    k = np.arange(length)[:, None]
    x = np.arange(length)[None, :]
    angle = 2.0 * np.pi * ((k * x) % length) / length
    table = np.where(k <= length // 2, np.cos(angle), np.sin(angle)) * np.sqrt(2.0 / length)
    table[0] = 1.0 / np.sqrt(length)
    table[length // 2] = np.cos(np.pi * np.arange(length)) / np.sqrt(length)
    return table


def split_np(table):
    import ml_dtypes

    high = table.astype(ml_dtypes.bfloat16)
    low = (table - high.astype(np.float64)).astype(ml_dtypes.bfloat16)
    return high, low


def right_table(table):
    high, low = split_np(table)
    row = np.concatenate([high, low], axis=1)
    return np.concatenate([row, row], axis=0)


def left_table(table):
    high, low = split_np(table)
    return np.concatenate([high, high, low], axis=1)


@functools.cache
def tables():
    basis_x = real_basis(NX)
    basis_y = real_basis(NY)
    swap = np.arange(NX).reshape(-1, 2, 4)[:, ::-1].reshape(-1)
    forward_y = right_table(basis_y.T)
    inverse_y = right_table(basis_y)
    forward_x = np.stack([left_table(basis_x), left_table(basis_x[swap])])
    inverse_x = np.stack([left_table(basis_x.T), left_table(basis_x[swap].T)])
    device = np.arange(GROUPS)[:, None]
    row = np.arange(8)[None, :] % 4
    wave_x = 8 * (device % 16) + 4 * (device // 16) + row
    lam_x = 2.0 - 2.0 * np.cos(2.0 * np.pi * wave_x / NX)
    lam_y = 2.0 - 2.0 * np.cos(2.0 * np.pi * np.arange(NY) / NY)
    lam = lam_x[:, :, None] + lam_y[None, None, :]
    excess = 0.5 / SMOOTH + 0.5 * lam
    rho = 1.0 / (1.0 + excess + np.sqrt(excess * (excess + 2.0)))
    return forward_y, inverse_y, forward_x, inverse_x, rho.astype(np.float32)


def split(value):
    high = value.astype(BF16)
    low = (value - high.astype(F32)).astype(BF16)
    return high, low


def times_right(value, table):
    high, low = split(value)
    both = jnp.dot(jnp.concatenate([high, low], axis=1), table, preferred_element_type=F32)
    return both[:, :128] + both[:, 128:]


def drive_planes(q, dz):
    q1, q2, q3, q4, q5 = q
    z12, z11m22, z23, z13 = dz

    def dx(f):
        return (pltpu.roll(f, NX - 1, 0) - pltpu.roll(f, 1, 0)) * 0.5

    def dy(f):
        return (pltpu.roll(f, NY - 1, 1) - pltpu.roll(f, 1, 1)) * 0.5

    qz = -(q1 + q4)
    s11 = q1 * q1 + q2 * q2 + q3 * q3
    s12 = q1 * q2 + q2 * q4 + q3 * q5
    s13 = q1 * q3 + q2 * q5 + q3 * qz
    s22 = q2 * q2 + q4 * q4 + q5 * q5
    s23 = q2 * q3 + q4 * q5 + q5 * qz
    s33 = q3 * q3 + q5 * q5 + qz * qz
    trace = s11 + s22 + s33
    scale = (0.2 + 1.0 / SMOOTH) - 0.1 * trace
    third = trace * (1.0 / 3.0)
    f1 = scale * q1 + 0.5 * (s11 - third) - dy(q3) + z12
    f2 = scale * q2 + 0.5 * s12 - 0.5 * (dy(q5) - dx(q3) + z11m22)
    f3 = scale * q3 + 0.5 * s13 - 0.5 * (dx(q2) + dy(qz - q1) - z23)
    f4 = scale * q4 + 0.5 * (s22 - third) - z12 + dx(q5)
    f5 = scale * q5 + 0.5 * s23 - 0.5 * (z13 + dx(q4 - qz) - dy(q2))
    return f1, f2, f3, f4, f5


def forward_kernel(img, low, high, ty, tx, out, stack, spectrum):
    for i in range(2):
        for zz in range(2):
            q = [img[i, c, zz] for c in range(5)]
            o = [img[i, c, 1 - zz] for c in range(5)]
            own = (o[1], o[0] - o[3], o[4], o[2])
            if zz == 0:
                dz = [(own[r] - low[i, r]) * 0.5 for r in range(4)]
            else:
                dz = [(high[i, r] - own[r]) * 0.5 for r in range(4)]
            for c, f in enumerate(drive_planes(q, dz)):
                h, l = split(times_right(f, ty[...]))
                cols = slice(zz * 128, zz * 128 + 128)
                stack[c, 0:128, cols] = h
                stack[c, 128:256, cols] = l
                stack[c, 256:384, cols] = h
        for c in range(5):
            spectrum[i, c] = jnp.dot(tx[i], stack[c], preferred_element_type=F32)
    first = lax.broadcasted_iota(jnp.int32, (16, 8, 128), 1) < 4
    for c in range(5):
        for zz in range(2):
            cols = slice(zz * 128, zz * 128 + 128)
            a = spectrum[0, c, :, cols].reshape(16, 8, 128)
            b = spectrum[1, c, :, cols].reshape(16, 8, 128)
            out[0:16, zz, 0, c] = jnp.where(first, a, b)
            out[16:32, zz, 0, c] = jnp.where(first, b, a)


def solve_kernel(where, f, rho_ref, out0, out1, work):
    del where
    rho = rho_ref[0]
    power = rho
    for _ in range(6):
        power = power * power
    closing = 1.0 / (1.0 - power)
    shape = (2, 5, 8, 128)
    zero = jnp.zeros(shape, F32)
    rb = jnp.broadcast_to(rho, shape)
    cb = jnp.broadcast_to(closing, shape)

    def ends(s, carry):
        v, u = carry
        for zz in range(2):
            v = f[s, zz] + rb * v
            u = f[GROUPS - 1 - s, 1 - zz] + rb * u
        return v, u

    v, u = lax.fori_loop(0, GROUPS, ends, (zero, zero))

    def up(s, v):
        for zz in range(2):
            v = f[s, zz] + rb * v
            work[s, zz] = v
        return v

    lax.fori_loop(0, GROUPS, up, v * cb)
    gain = rho * (1.0 / SMOOTH) / (1.0 - rho * rho)
    gb = jnp.broadcast_to(gain, shape)

    def down(n, u):
        s = GROUPS - 1 - n
        for zz in (1, 0):
            value = rb * u
            u = f[s, zz] + value
            result = gb * (work[s, zz] + value)
            out0[s, zz] = result[0]
            out1[s, zz] = result[1]
        return u

    lax.fori_loop(0, GROUPS, down, u * cb)


def inverse_kernel(spec, img, ty, tx, out, stack):
    first = lax.broadcasted_iota(jnp.int32, (16, 8, 128), 1) < 4
    for i in range(2):
        for c in range(5):
            for zz in range(2):
                even = spec[0:16, zz, c]
                odd = spec[16:32, zz, c]
                mine = jnp.where(first, even, odd) if i == 0 else jnp.where(first, odd, even)
                h, l = split(mine.reshape(128, 128))
                cols = slice(zz * 128, zz * 128 + 128)
                stack[c, 0:128, cols] = h
                stack[c, 128:256, cols] = l
                stack[c, 256:384, cols] = h
            both = jnp.dot(tx[i], stack[c], preferred_element_type=F32)
            for zz in range(2):
                update = times_right(both[:, zz * 128 : zz * 128 + 128], ty[...])
                out[i, c, zz] = KEEP * img[i, c, zz] + update


def gap_kernel(lower, upper, beyond, out):
    @pl.when(pl.program_id(0) == 0)
    def _():
        out[...] = jnp.zeros_like(out)

    def total(a, b):
        d = a - b
        d = (d * d).reshape(2 * 16, 8, 128)
        return jnp.sum(d, axis=0)

    chain = [lower[0, 0], lower[1, 0], upper[0, 0], upper[1, 0], beyond[0, 0]]
    for g in range(4):
        out[g] += total(chain[g + 1], chain[g])


def final_kernel(centre, positions, where, sums, below, lower, upper, above, out, weights):
    @pl.when(pl.program_id(0) == 0)
    def _():
        arc = [jnp.zeros((8, 128), F32)]
        for k in range(LOCAL):
            block = jnp.sum(sums[k * GROUPS : (k + 1) * GROUPS], axis=0)
            dist = jnp.sqrt(block * (1.0 / CELLS) + EPS)
            for g in range(4):
                if k * 4 + g < IMAGES - 1:
                    row = jnp.broadcast_to(dist[g : g + 1], (8, 128))
                    arc.append(arc[-1] + row)
        base = where[0] * LOCAL - 2
        for m in range(LOCAL):
            c = centre[m]
            tau = positions[m] * arc[-1]

            def pick(index):
                value = arc[0]
                for j in range(1, IMAGES):
                    value = jnp.where(index == j, arc[j], value)
                return value

            a, b, d = pick(c - 1), pick(c), pick(c + 1)
            w = (
                (tau - b) * (tau - d) / ((a - b) * (a - d)),
                (tau - a) * (tau - d) / ((b - a) * (b - d)),
                (tau - a) * (tau - b) / ((d - a) * (d - b)),
            )
            for r in range(5):
                spot = base + m + r
                value = jnp.zeros((8, 128), F32)
                for n in range(3):
                    value = jnp.where(c - 1 + n == spot, w[n], value)
                weights[m, r] = value

    pieces = [below[0], below[1], lower[0], lower[1], upper[0], upper[1], above[0], above[1]]
    pieces = [p.reshape(32, 8, 128) for p in pieces]
    for m in range(LOCAL):
        acc = pieces[m] * weights[m, 0][None]
        for r in range(1, 5):
            acc = acc + pieces[m + r] * weights[m, r][None]
        out[m, 0] = acc.reshape(2, 128, 128)


def whole(shape):
    return pl.BlockSpec(shape, lambda *_: (0,) * len(shape))


SMEM = pl.BlockSpec(memory_space=pltpu.SMEM)


def params(mib):
    return pltpu.CompilerParams(
        dimension_semantics=("arbitrary",), vmem_limit_bytes=mib * 1024 * 1024
    )


def forward(images, low, high, ty, tx):
    return pl.pallas_call(
        forward_kernel,
        out_shape=jax.ShapeDtypeStruct((GROUPS, 2, 2, 5, 8, 128), F32),
        grid=(2,),
        in_specs=[
            pl.BlockSpec((2, 5, 2, 128, 128), lambda p: (p, 0, 0, 0, 0)),
            pl.BlockSpec((2, 4, 128, 128), lambda p: (p, 0, 0, 0)),
            pl.BlockSpec((2, 4, 128, 128), lambda p: (p, 0, 0, 0)),
            whole((256, 256)),
            whole((2, 128, 384)),
        ],
        out_specs=pl.BlockSpec((GROUPS, 2, 1, 5, 8, 128), lambda p: (0, 0, p, 0, 0, 0)),
        scratch_shapes=[
            pltpu.VMEM((5, 384, 256), BF16),
            pltpu.VMEM((2, 5, 128, 256), F32),
        ],
        compiler_params=params(32),
        name="forward",
    )(images, low, high, ty, tx)


def solve(f, rho):
    half = jax.ShapeDtypeStruct((GROUPS, 2, 5, 8, 128), F32)
    where = lax.axis_index("gz").astype(jnp.int32).reshape(1)
    return pl.pallas_call(
        solve_kernel,
        out_shape=(half, half),
        grid_spec=pltpu.PrefetchScalarGridSpec(
            num_scalar_prefetch=1,
            grid=(1,),
            in_specs=[
                whole((GROUPS, 2, 2, 5, 8, 128)),
                pl.BlockSpec((1, 8, 128), lambda i, w: (w[0], 0, 0)),
            ],
            out_specs=(whole((GROUPS, 2, 5, 8, 128)), whole((GROUPS, 2, 5, 8, 128))),
            scratch_shapes=[pltpu.VMEM((GROUPS, 2, 2, 5, 8, 128), F32)],
        ),
        compiler_params=params(32),
        name="solve",
    )(where, f, rho)


def inverse(spec, images, pair, ty, tx):
    return pl.pallas_call(
        inverse_kernel,
        out_shape=jax.ShapeDtypeStruct((2, 5, 2, 128, 128), F32),
        grid=(1,),
        in_specs=[
            whole((GROUPS, 2, 5, 8, 128)),
            pl.BlockSpec((2, 5, 2, 128, 128), lambda p: (pair, 0, 0, 0, 0)),
            whole((256, 256)),
            whole((2, 128, 384)),
        ],
        out_specs=whole((2, 5, 2, 128, 128)),
        scratch_shapes=[pltpu.VMEM((5, 384, 256), BF16)],
        compiler_params=params(32),
        name="inverse",
    )(spec, images, ty, tx)


def gaps(lower, upper, beyond):
    pair = pl.BlockSpec((2, 1, 2, 128, 128), lambda c: (0, c, 0, 0, 0))
    one = pl.BlockSpec((1, 1, 2, 128, 128), lambda c: (0, c, 0, 0, 0))
    return pl.pallas_call(
        gap_kernel,
        out_shape=jax.ShapeDtypeStruct((4, 8, 128), F32),
        grid=(5,),
        in_specs=[pair, pair, one],
        out_specs=whole((4, 8, 128)),
        compiler_params=params(16),
        name="gaps",
    )(lower, upper, beyond)


def final(centre, positions, sums, below, lower, upper, above):
    pair = pl.BlockSpec((2, 1, 2, 128, 128), lambda c: (0, c, 0, 0, 0))
    where = lax.axis_index("img").astype(jnp.int32).reshape(1)
    return pl.pallas_call(
        final_kernel,
        out_shape=jax.ShapeDtypeStruct((4, 5, 2, 128, 128), F32),
        grid=(5,),
        in_specs=[SMEM, SMEM, SMEM, whole((128, 8, 128)), pair, pair, pair, pair],
        out_specs=pl.BlockSpec((4, 1, 2, 128, 128), lambda c: (0, c, 0, 0, 0)),
        scratch_shapes=[pltpu.VMEM((4, 5, 8, 128), F32)],
        compiler_params=params(32),
        name="final",
    )(centre, positions, where, sums, below, lower, upper, above)


def local(images, centre, positions):
    forward_y, inverse_y, forward_x, inverse_x, rho = (jnp.asarray(t) for t in tables())
    ring = [(i, (i + 1) % GROUPS) for i in range(GROUPS)]
    back = [(b, a) for a, b in ring]
    rows = [(i, i + 1) for i in range(LOCAL - 1)]
    rows_back = [(b, a) for a, b in rows]

    def rotated(plane):
        q = images[:, :, plane]
        return jnp.stack([q[:, 1], q[:, 0] - q[:, 3], q[:, 4], q[:, 2]], axis=1)

    low = lax.ppermute(rotated(1), "gz", ring)
    high = lax.ppermute(rotated(0), "gz", back)
    f = forward(images, low, high, forward_y, forward_x)
    f = lax.all_to_all(f, "gz", 0, 0, tiled=True)
    u0, u1 = solve(f, rho)
    u0 = lax.all_to_all(u0, "gz", 0, 0, tiled=True)
    u1 = lax.all_to_all(u1, "gz", 0, 0, tiled=True)
    lower = inverse(u0, images, 0, inverse_y, inverse_x)
    above = lax.ppermute(lower, "img", rows_back)
    upper = inverse(u1, images, 1, inverse_y, inverse_x)
    below = lax.ppermute(upper, "img", rows)
    part = gaps(lower, upper, above)
    part = jnp.sum(part, axis=(1, 2))
    part = jnp.pad(part, (0, 4))
    part = jnp.broadcast_to(part[None, :, None], (128, 8, 128))
    sums = lax.all_to_all(part, ("img", "gz"), 0, 0, tiled=True)
    return final(centre, positions, sums, below, lower, upper, above)


def solution(mesh):
    in_specs = (P("img", None, "gz", None, None), P("img"), P("img"))
    out_specs = P("img", None, "gz", None, None)
    return jax.shard_map(local, mesh=mesh, in_specs=in_specs, out_specs=out_specs, check_vma=False)
```

profile of v0, /device:TPU:1, one launch (start us, length us, event | category | flops | bytes accessed | tf_op | source)
XLA Modules:
  0.0 173.7 jit_solution(11116187787024755488)
XLA Ops:
  0.0 1.9 %slice_bitcast_fusion = (f32[4,5,128,128]{3,2,1,0:T(8,128)S(1)}, f32[4,5,128,128]{3,2,1,0:T(8,128)S(1)}) fusion(f32[4,5,2,128,128]{4,3,2,1,0:T(8,128)} %img.5), kind=kLoop, calls=%fused_computation | loop fusion | bytes 5242880 | tf_op jit(solution)/shard_map/squeeze | solution.py:375
  2.2 2.5 %collective-permute-start = (f32[4,4,128,128]{3,2,1,0:T(8,128)S(1)}, f32[4,4,128,128]{3,2,1,0:T(8,128)S(1)}, u32[]{:S(2)}, u32[]{:S(2)}) collective-permute-start(f32[4,4,128,128]{3,2,1,0:T(8,128)S(1)} %pad_maximum_fusion), channel_id=1, source_target_pairs={{0,1},{1,2},{2,3},{3,4},{4,5},{5,6},{6,7},{7,8},{8,9},{9,10},{10,1... | collective-permute-start | bytes 3145736 | tf_op jit(solution)/shard_map/ppermute | solution.py:378
  4.8 5.4 %collective-permute-start.1 = (f32[4,4,128,128]{3,2,1,0:T(8,128)S(1)}, f32[4,4,128,128]{3,2,1,0:T(8,128)S(1)}, u32[]{:S(2)}, u32[]{:S(2)}) collective-permute-start(f32[4,4,128,128]{3,2,1,0:T(8,128)S(1)} %pad_maximum_fusion.1), channel_id=1, source_target_pairs={{1,0},{2,1},{3,2},{4,3},{5,4},{6,5},{7,6},{8,7},{9,8},{10,9},{11,1... | collective-permute-start | bytes 3145736 | tf_op jit(solution)/shard_map/ppermute | solution.py:379
  10.2 22.7 %collective-permute-done.low = f32[4,4,128,128]{3,2,1,0:T(8,128)S(1)} collective-permute-done((f32[4,4,128,128]{3,2,1,0:T(8,128)S(1)}, f32[4,4,128,128]{3,2,1,0:T(8,128)S(1)}, u32[]{:S(2)}, u32[]{:S(2)}) %collective-permute-start) | collective-permute-done | bytes 1048608 | tf_op jit(solution)/shard_map/ppermute | solution.py:378
  33.0 3.7 %forward.1 = f32[32,2,2,5,8,128]{5,4,3,2,1,0:T(8,128)S(1)} custom-call(f32[4,5,2,128,128]{4,3,2,1,0:T(8,128)S(1)} %copy-done, f32[4,4,128,128]{3,2,1,0:T(8,128)S(1)} %collective-permute-done.low, f32[4,4,128,128]{3,2,1,0:T(8,128)S(1)} %collective-permute-done.1.high, bf16[256,256]{1,0:T(8,128)(2,1)S(1)} %copy-done.8, bf16[2,128,384]{2,1,0:T(8,128)(2,1)S(1)} %copy-done.6), custom_call_target="tpu_custom_call" | custom-call | tf_op jit(solution)/shard_map/forward/pallas_call | solution.py:278
  36.6 1.5 copy-done.1
  38.1 7.5 %all-to-all-start = ((f32[32,2,2,5,8,128]{5,4,3,2,1,0:T(8,128)}), f32[32,2,2,5,8,128]{5,4,3,2,1,0:T(8,128)}, u32[]{:S(2)}, u32[]{:S(2)}) async-start(f32[32,2,2,5,8,128]{5,4,3,2,1,0:T(8,128)} %copy-done.1), calls=%async_computation | async-start | bytes 5242880 | tf_op jit(solution)/shard_map/all_to_all | solution.py:381
  45.6 32.8 %all-to-all-done.f = f32[32,2,2,5,8,128]{5,4,3,2,1,0:T(8,128)} async-done(((f32[32,2,2,5,8,128]{5,4,3,2,1,0:T(8,128)}), f32[32,2,2,5,8,128]{5,4,3,2,1,0:T(8,128)}, u32[]{:S(2)}, u32[]{:S(2)}) %all-to-all-start) | async-done | bytes 2621472 | tf_op jit(solution)/shard_map/all_to_all | solution.py:381
  78.5 3.0 %solve.1 = (f32[32,2,5,8,128]{4,3,2,1,0:T(8,128)S(1)}, f32[32,2,5,8,128]{4,3,2,1,0:T(8,128)S(1)}) custom-call(s32[1]{0:T(128)} %bitcast.1.where, f32[32,2,2,5,8,128]{5,4,3,2,1,0:T(8,128)} %all-to-all-done.f, f32[32,8,128]{2,1,0:T(8,128)S(1)} %copy-done.7), custom_call_target="tpu_custom_call" | custom-call | tf_op jit(solution)/shard_map/solve/pallas_call | solution.py:302
  81.5 24.8 %all_to_all.20.spec = f32[32,2,5,8,128]{4,3,2,1,0:T(8,128)} all-to-all(f32[32,2,5,8,128]{4,3,2,1,0:T(8,128)S(1)} %get-tuple-element.7), channel_id=1, replica_groups=mesh['img'=4,'gz'=32] {'gz'}, dimensions={0} | all-to-all | bytes 2621440 | tf_op jit(solution)/shard_map/all_to_all | solution.py:383
  106.4 4.8 %all-to-all-start.2 = ((f32[32,2,5,8,128]{4,3,2,1,0:T(8,128)}), f32[32,2,5,8,128]{4,3,2,1,0:T(8,128)}, u32[]{:S(2)}, u32[]{:S(2)}) async-start(f32[32,2,5,8,128]{4,3,2,1,0:T(8,128)} %copy-done.3), calls=%async_computation.2 | async-start | bytes 2621440 | tf_op jit(solution)/shard_map/all_to_all | solution.py:384
  111.2 1.3 copy-done.2
  112.5 2.3 %inverse.2.lower = f32[2,5,2,128,128]{4,3,2,1,0:T(8,128)} custom-call(f32[32,2,5,8,128]{4,3,2,1,0:T(8,128)S(1)} %copy-done.2, f32[4,5,2,128,128]{4,3,2,1,0:T(8,128)S(1)} %copy-done, bf16[256,256]{1,0:T(8,128)(2,1)S(1)} %copy-done.5, bf16[2,128,384]{2,1,0:T(8,128)(2,1)S(1)} %copy-done.4), custom_call_target="tpu_custom_call" | custom-call | tf_op jit(solution)/shard_map/inverse/pallas_call | solution.py:321
  114.8 4.5 %collective-permute-start.2 = (f32[2,5,2,128,128]{4,3,2,1,0:T(8,128)}, f32[2,5,2,128,128]{4,3,2,1,0:T(8,128)}, u32[]{:S(2)}, u32[]{:S(2)}) collective-permute-start(f32[2,5,2,128,128]{4,3,2,1,0:T(8,128)} %inverse.2.lower), channel_id=1, source_target_pairs={{32,0},{64,32},{96,64},{33,1},{65,33},{97,65},{34,2},{66,34},{98,6... | collective-permute-start | bytes 3932168 | tf_op jit(solution)/shard_map/ppermute | solution.py:386
  119.3 8.7 %all-to-all-done.2.spec = f32[32,2,5,8,128]{4,3,2,1,0:T(8,128)} async-done(((f32[32,2,5,8,128]{4,3,2,1,0:T(8,128)}), f32[32,2,5,8,128]{4,3,2,1,0:T(8,128)}, u32[]{:S(2)}, u32[]{:S(2)}) %all-to-all-start.2) | async-done | bytes 1310752 | tf_op jit(solution)/shard_map/all_to_all | solution.py:384
  128.0 3.6 %inverse.3.upper = f32[2,5,2,128,128]{4,3,2,1,0:T(8,128)} custom-call(f32[32,2,5,8,128]{4,3,2,1,0:T(8,128)} %all-to-all-done.2.spec, f32[4,5,2,128,128]{4,3,2,1,0:T(8,128)S(1)} %copy-done, bf16[256,256]{1,0:T(8,128)(2,1)S(1)} %copy-done.5, bf16[2,128,384]{2,1,0:T(8,128)(2,1)S(1)} %copy-done.4), custom_call_target="tpu_custom_call" | custom-call | tf_op jit(solution)/shard_map/inverse/pallas_call | solution.py:321
  131.7 8.1 %collective-permute-start.3 = (f32[2,5,2,128,128]{4,3,2,1,0:T(8,128)}, f32[2,5,2,128,128]{4,3,2,1,0:T(8,128)S(1)}, u32[]{:S(2)}, u32[]{:S(2)}) collective-permute-start(f32[2,5,2,128,128]{4,3,2,1,0:T(8,128)} %inverse.3.upper), channel_id=1, source_target_pairs={{0,32},{32,64},{64,96},{1,33},{33,65},{65,97},{2,34},{34,66},{66,9... | collective-permute-start | bytes 3932168 | tf_op jit(solution)/shard_map/ppermute | solution.py:388
  139.8 3.6 %collective-permute-done.2.beyond.above = f32[2,5,2,128,128]{4,3,2,1,0:T(8,128)} collective-permute-done((f32[2,5,2,128,128]{4,3,2,1,0:T(8,128)}, f32[2,5,2,128,128]{4,3,2,1,0:T(8,128)}, u32[]{:S(2)}, u32[]{:S(2)}) %collective-permute-start.2) | collective-permute-done | bytes 1310752 | tf_op jit(solution)/shard_map/ppermute | solution.py:386
  143.4 3.5 %gaps.1 = f32[4,8,128]{2,1,0:T(8,128)S(1)} custom-call(f32[2,5,2,128,128]{4,3,2,1,0:T(8,128)} %inverse.2.lower, f32[2,5,2,128,128]{4,3,2,1,0:T(8,128)} %inverse.3.upper, f32[2,5,2,128,128]{4,3,2,1,0:T(8,128)} %collective-permute-done.2.beyond.above), custom_call_target="tpu_custom_call" | custom-call | tf_op jit(solution)/shard_map/gaps/pallas_call | solution.py:341
  147.0 0.9 broadcast_in_dim.2
  147.9 6.4 %all-to-all-start.3 = ((f32[128,8,128]{2,1,0:T(8,128)}), f32[128,8,128]{2,1,0:T(8,128)S(1)}, u32[]{:S(2)}, u32[]{:S(2)}) async-start(f32[128,8,128]{2,1,0:T(8,128)} %broadcast_in_dim.2), calls=%async_computation.3 | async-start | bytes 1048576 | tf_op jit(solution)/shard_map/all_to_all | solution.py:393
  154.3 0.3 collective-permute-done.3.below
  154.6 13.4 %all-to-all-done.3.sums = f32[128,8,128]{2,1,0:T(8,128)S(1)} async-done(((f32[128,8,128]{2,1,0:T(8,128)}), f32[128,8,128]{2,1,0:T(8,128)S(1)}, u32[]{:S(2)}, u32[]{:S(2)}) %all-to-all-start.3) | async-done | bytes 524320 | tf_op jit(solution)/shard_map/all_to_all | solution.py:393
  168.0 5.7 %final.1 = f32[4,5,2,128,128]{4,3,2,1,0:T(8,128)} custom-call(s32[4]{0:T(128)S(1)} %copy-done.9, f32[4]{0:T(128)S(1)} %copy-done.10, s32[1]{0:T(128)} %bitcast.where, f32[128,8,128]{2,1,0:T(8,128)S(1)} %all-to-all-done.3.sums, f32[2,5,2,128,128]{4,3,2,1,0:T(8,128)S(1)} %collective-permute-done.3.below, f32[2,5,2,128,128]{4,3,2,1,0:T(8,128)} %inverse.2.lower, ...), custom_call_target="tpu_custom_call" | custom-call | tf_op jit(solution)/shard_map/final/pallas_call | solution.py:355
  (26 shorter events, 0.5 us)
Async XLA Ops:
  2.1 30.9 %copy-start = (f32[4,5,2,128,128]{4,3,2,1,0:T(8,128)S(1)}, f32[4,5,2,128,128]{4,3,2,1,0:T(8,128)}, u32[]{:S(2)}) copy-start(f32[4,5,2,128,128]{4,3,2,1,0:T(8,128)} %img.5) | copy-start | bytes 7864324
  2.2 30.7 %copy-start.6 = (bf16[2,128,384]{2,1,0:T(8,128)(2,1)S(1)}, bf16[2,128,384]{2,1,0:T(8,128)(2,1)}, u32[]{:S(2)}) copy-start(bf16[2,128,384]{2,1,0:T(8,128)(2,1)} %constant.25.clone.tx) | copy-start | bytes 589828
  2.2 30.7 %copy-start.8 = (bf16[256,256]{1,0:T(8,128)(2,1)S(1)}, bf16[256,256]{1,0:T(8,128)(2,1)}, u32[]{:S(2)}) copy-start(bf16[256,256]{1,0:T(8,128)(2,1)} %constant.23.clone.ty) | copy-start | bytes 393220
  2.2 30.7 %collective-permute-start = (f32[4,4,128,128]{3,2,1,0:T(8,128)S(1)}, f32[4,4,128,128]{3,2,1,0:T(8,128)S(1)}, u32[]{:S(2)}, u32[]{:S(2)}) collective-permute-start(f32[4,4,128,128]{3,2,1,0:T(8,128)S(1)} %pad_maximum_fusion), channel_id=1, source_target_pairs={{0,1},{1,2},{2,3},{3,4},{4,5},{5,6},{6,7},{7,8},{8,9},{9,10},{10,1... | collective-permute-start | bytes 3145736 | tf_op jit(solution)/shard_map/ppermute | solution.py:378
  4.8 28.1 %collective-permute-start.1 = (f32[4,4,128,128]{3,2,1,0:T(8,128)S(1)}, f32[4,4,128,128]{3,2,1,0:T(8,128)S(1)}, u32[]{:S(2)}, u32[]{:S(2)}) collective-permute-start(f32[4,4,128,128]{3,2,1,0:T(8,128)S(1)} %pad_maximum_fusion.1), channel_id=1, source_target_pairs={{1,0},{2,1},{3,2},{4,3},{5,4},{6,5},{7,6},{8,7},{9,8},{10,9},{11,1... | collective-permute-start | bytes 3145736 | tf_op jit(solution)/shard_map/ppermute | solution.py:379
  36.6 1.5 copy-start.1
  38.1 40.3 %copy-start.7 = (f32[32,8,128]{2,1,0:T(8,128)S(1)}, f32[32,8,128]{2,1,0:T(8,128)}, u32[]{:S(2)}) copy-start(f32[32,8,128]{2,1,0:T(8,128)} %constant.27.clone.rho_ref) | copy-start | bytes 393220
  38.1 40.3 %all-to-all-start = ((f32[32,2,2,5,8,128]{5,4,3,2,1,0:T(8,128)}), f32[32,2,2,5,8,128]{5,4,3,2,1,0:T(8,128)}, u32[]{:S(2)}, u32[]{:S(2)}) async-start(f32[32,2,2,5,8,128]{5,4,3,2,1,0:T(8,128)} %copy-done.1), calls=%async_computation | async-start | bytes 5242880 | tf_op jit(solution)/shard_map/all_to_all | solution.py:381
  81.5 24.9 %copy-start.3 = (f32[32,2,5,8,128]{4,3,2,1,0:T(8,128)}, f32[32,2,5,8,128]{4,3,2,1,0:T(8,128)S(1)}, u32[]{:S(2)}) copy-start(f32[32,2,5,8,128]{4,3,2,1,0:T(8,128)S(1)} %get-tuple-element.8) | copy-start | bytes 3932164
  106.4 4.8 %copy-start.4 = (bf16[2,128,384]{2,1,0:T(8,128)(2,1)S(1)}, bf16[2,128,384]{2,1,0:T(8,128)(2,1)}, u32[]{:S(2)}) copy-start(bf16[2,128,384]{2,1,0:T(8,128)(2,1)} %constant.26.clone.tx) | copy-start | bytes 589828
  106.4 4.8 %copy-start.5 = (bf16[256,256]{1,0:T(8,128)(2,1)S(1)}, bf16[256,256]{1,0:T(8,128)(2,1)}, u32[]{:S(2)}) copy-start(bf16[256,256]{1,0:T(8,128)(2,1)} %constant.24.clone.ty) | copy-start | bytes 393220
  106.4 21.7 %all-to-all-start.2 = ((f32[32,2,5,8,128]{4,3,2,1,0:T(8,128)}), f32[32,2,5,8,128]{4,3,2,1,0:T(8,128)}, u32[]{:S(2)}, u32[]{:S(2)}) async-start(f32[32,2,5,8,128]{4,3,2,1,0:T(8,128)} %copy-done.3), calls=%async_computation.2 | async-start | bytes 2621440 | tf_op jit(solution)/shard_map/all_to_all | solution.py:384
  111.2 1.3 copy-start.2
  114.8 28.6 %collective-permute-start.2 = (f32[2,5,2,128,128]{4,3,2,1,0:T(8,128)}, f32[2,5,2,128,128]{4,3,2,1,0:T(8,128)}, u32[]{:S(2)}, u32[]{:S(2)}) collective-permute-start(f32[2,5,2,128,128]{4,3,2,1,0:T(8,128)} %inverse.2.lower), channel_id=1, source_target_pairs={{32,0},{64,32},{96,64},{33,1},{65,33},{97,65},{34,2},{66,34},{98,6... | collective-permute-start | bytes 3932168 | tf_op jit(solution)/shard_map/ppermute | solution.py:386
  131.7 22.9 %collective-permute-start.3 = (f32[2,5,2,128,128]{4,3,2,1,0:T(8,128)}, f32[2,5,2,128,128]{4,3,2,1,0:T(8,128)S(1)}, u32[]{:S(2)}, u32[]{:S(2)}) collective-permute-start(f32[2,5,2,128,128]{4,3,2,1,0:T(8,128)} %inverse.3.upper), channel_id=1, source_target_pairs={{0,32},{32,64},{64,96},{1,33},{33,65},{65,97},{2,34},{34,66},{66,9... | collective-permute-start | bytes 3932168 | tf_op jit(solution)/shard_map/ppermute | solution.py:388
  146.9 21.1 %copy-start.9 = (s32[4]{0:T(128)S(1)}, s32[4]{0:T(128)}, u32[]{:S(2)}) copy-start(s32[4]{0:T(128)} %centre.1) | copy-start | bytes 52
  146.9 21.1 %copy-start.10 = (f32[4]{0:T(128)S(1)}, f32[4]{0:T(128)}, u32[]{:S(2)}) copy-start(f32[4]{0:T(128)} %positions.1) | copy-start | bytes 52
  147.9 20.1 %all-to-all-start.3 = ((f32[128,8,128]{2,1,0:T(8,128)}), f32[128,8,128]{2,1,0:T(8,128)S(1)}, u32[]{:S(2)}, u32[]{:S(2)}) async-start(f32[128,8,128]{2,1,0:T(8,128)} %broadcast_in_dim.2), calls=%async_computation.3 | async-start | bytes 1048576 | tf_op jit(solution)/shard_map/all_to_all | solution.py:393
where the time goes:
time: 174 us
  waiting for transfers between devices  81.5 us (47%)
  starting transfers between devices  39.2 us (23%)
  blocking collectives  24.8 us (14%)
  Pallas kernels  21.8 us (13%)
  local copies, waits for them, and re-layouts  5.64 us (3%)
    all_to_all x1, waiting for transfers between devices, local(): f = lax.all_to_all(f, 'gz', 0, 0, tiled=True)  32.8 us
    all_to_all x1, blocking collectives, local(): u0 = lax.all_to_all(u0, 'gz', 0, 0, tiled=True)  24.8 us
    ppermute x1, waiting for transfers between devices, local(): low = lax.ppermute(rotated(1), 'gz', ring)  22.7 us
    all_to_all x1, waiting for transfers between devices, local(): sums = lax.all_to_all(part, ('img', 'gz'), 0, 0, tiled=True)  13.4 us
    all_to_all x1, waiting for transfers between devices, local(): u1 = lax.all_to_all(u1, 'gz', 0, 0, tiled=True)  8.67 us
    ppermute x1, starting transfers between devices, local(): below = lax.ppermute(upper, 'img', rows)  8.08 us
    all_to_all x1, starting transfers between devices, local(): f = lax.all_to_all(f, 'gz', 0, 0, tiled=True)  7.46 us
    all_to_all x1, starting transfers between devices, local(): sums = lax.all_to_all(part, ('img', 'gz'), 0, 0, tiled=True)  6.4 us
  transfers between devices with their start and end apart: 7, of which 6 were waited for; matrix products, arithmetic and copies ran while one was open for 1% of the time, Pallas kernels for 5%

commit v1 on v0

v1 whole, which is shorter than its diff:
```python
import functools

import jax
import jax.numpy as jnp
import numpy as np
from jax import lax
from jax.experimental import pallas as pl
from jax.experimental.pallas import tpu as pltpu
from jax.sharding import PartitionSpec as P

NX = 128
NY = 128
NZ = 64
GROUPS = 32
IMAGES = 16
LOCAL = 4
CELLS = 5.0 * NZ * NX * NY
SMOOTH = 64.0
EPS = 1e-6
KEEP = 1.0 - 1.0 / SMOOTH
F32 = jnp.float32
BF16 = jnp.bfloat16


def real_basis(length):
    k = np.arange(length)[:, None]
    x = np.arange(length)[None, :]
    angle = 2.0 * np.pi * ((k * x) % length) / length
    table = np.where(k <= length // 2, np.cos(angle), np.sin(angle)) * np.sqrt(2.0 / length)
    table[0] = 1.0 / np.sqrt(length)
    table[length // 2] = np.cos(np.pi * np.arange(length)) / np.sqrt(length)
    return table


def split_np(table):
    import ml_dtypes

    high = table.astype(ml_dtypes.bfloat16)
    low = (table - high.astype(np.float64)).astype(ml_dtypes.bfloat16)
    return high, low


def right_table(table):
    high, low = split_np(table)
    row = np.concatenate([high, low], axis=1)
    return np.concatenate([row, row], axis=0)


def left_table(table):
    high, low = split_np(table)
    return np.concatenate([high, high, low], axis=1)


@functools.cache
def tables():
    basis_x = real_basis(NX)
    basis_y = real_basis(NY)
    swap = np.arange(NX).reshape(-1, 2, 4)[:, ::-1].reshape(-1)
    forward_y = right_table(basis_y.T)
    inverse_y = right_table(basis_y)
    forward_x = np.stack([left_table(basis_x), left_table(basis_x[swap])])
    inverse_x = np.stack([left_table(basis_x.T), left_table(basis_x[swap].T)])
    device = np.arange(GROUPS)[:, None]
    row = np.arange(8)[None, :] % 4
    wave_x = 8 * (device % 16) + 4 * (device // 16) + row
    lam_x = 2.0 - 2.0 * np.cos(2.0 * np.pi * wave_x / NX)
    lam_y = 2.0 - 2.0 * np.cos(2.0 * np.pi * np.arange(NY) / NY)
    lam = lam_x[:, :, None] + lam_y[None, None, :]
    excess = 0.5 / SMOOTH + 0.5 * lam
    rho = 1.0 / (1.0 + excess + np.sqrt(excess * (excess + 2.0)))
    return forward_y, inverse_y, forward_x, inverse_x, rho.astype(np.float32)


def split(value):
    high = value.astype(BF16)
    low = (value - high.astype(F32)).astype(BF16)
    return high, low


def times_right(value, table):
    high, low = split(value)
    both = jnp.dot(jnp.concatenate([high, low], axis=1), table, preferred_element_type=F32)
    return both[:, :128] + both[:, 128:]


def dx(f):
    return (pltpu.roll(f, NX - 1, 0) - pltpu.roll(f, 1, 0)) * 0.5


def dy(f):
    return (pltpu.roll(f, NY - 1, 1) - pltpu.roll(f, 1, 1)) * 0.5


def local_drive(q):
    q1, q2, q3, q4, q5 = q
    qz = -(q1 + q4)
    s11 = q1 * q1 + q2 * q2 + q3 * q3
    s12 = q1 * q2 + q2 * q4 + q3 * q5
    s13 = q1 * q3 + q2 * q5 + q3 * qz
    s22 = q2 * q2 + q4 * q4 + q5 * q5
    s23 = q2 * q3 + q4 * q5 + q5 * qz
    s33 = q3 * q3 + q5 * q5 + qz * qz
    trace = s11 + s22 + s33
    scale = (0.2 + 1.0 / SMOOTH) - 0.1 * trace
    third = trace * (1.0 / 3.0)
    f1 = scale * q1 + 0.5 * (s11 - third) - dy(q3)
    f2 = scale * q2 + 0.5 * s12 - 0.5 * (dy(q5) - dx(q3))
    f3 = scale * q3 + 0.5 * s13 - 0.5 * (dx(q2) + dy(qz - q1))
    f4 = scale * q4 + 0.5 * (s22 - third) + dx(q5)
    f5 = scale * q5 + 0.5 * s23 - 0.5 * (dx(q4 - qz) - dy(q2))
    return f1, f2, f3, f4, f5


def mixed(q):
    return q[1], q[0] - q[3], q[4], q[2]


def spread(r):
    return 0.5 * r[0], -0.25 * r[1], 0.25 * r[2], -0.5 * r[0], -0.25 * r[3]


def along_plane(f):
    around = pltpu.roll(f, NX - 1, 0) + pltpu.roll(f, 1, 0)
    around = around + pltpu.roll(f, NY - 1, 1) + pltpu.roll(f, 1, 1)
    return (6.0 + 1.0 / SMOOTH) * f - around


def push(stack, slot, half, value):
    h, l = split(value)
    cols = slice(half * 128, half * 128 + 128)
    stack[slot, 0:128, cols] = h
    stack[slot, 128:256, cols] = l
    stack[slot, 256:384, cols] = h


def forward_kernel(img, ty, tx, rho_ref, out, keep, stack, spectrum):
    for i in range(2):
        qe = [img[i, c, 0] for c in range(5)]
        qo = [img[i, c, 1] for c in range(5)]
        re = mixed(qe)
        ro = mixed(qo)
        for c, (f, g) in enumerate(zip(local_drive(qe), spread(ro))):
            push(stack, c, 0, times_right(f + 2.0 * g, ty[...]))
        bo = spread([along_plane(r) for r in ro])
        for c, (f, g, b) in enumerate(zip(local_drive(qo), spread(re), bo)):
            push(stack, c, 1, times_right(f - g - b, ty[...]))
        for r in range(4):
            push(stack, 5 + r // 2, r % 2, times_right(re[r], ty[...]))
        for n in range(7):
            spectrum[i, n] = jnp.dot(tx[i], stack[n], preferred_element_type=F32)
    first = lax.broadcasted_iota(jnp.int32, (16, 8, 128), 1) < 4
    for part in range(2):
        rows = slice(part * 16, part * 16 + 16)
        rho = rho_ref[rows]
        beta = rho + 1.0 / rho
        back = (1.0 / SMOOTH) / beta

        def tile(n, half):
            cols = slice(half * 128, half * 128 + 128)
            a = spectrum[0, n, :, cols].reshape(16, 8, 128)
            b = spectrum[1, n, :, cols].reshape(16, 8, 128)
            return jnp.where(first, a, b) if part == 0 else jnp.where(first, b, a)

        g = spread([beta * tile(5 + r // 2, r % 2) for r in range(4)])
        for c in range(5):
            y = tile(c, 0)
            out[rows, 0, 0, c] = beta * tile(c, 1) + y
            out[rows, 1, 0, c] = y + g[c]
            keep[rows, 0, c] = back * y


def solve_kernel(where, f, rho_ref, out0, out1, right, work):
    del where
    rho = rho_ref[0]
    sigma = rho * rho
    power = sigma
    for _ in range(5):
        power = power * power
    closing = 1.0 / (1.0 - power)
    shape = (2, 5, 8, 128)
    zero = jnp.zeros(shape, F32)
    sb = jnp.broadcast_to(sigma, shape)
    cb = jnp.broadcast_to(closing, shape)

    def ends(s, carry):
        v, u, p = carry
        r = f[s, 0] + f[lax.rem(s + 1, GROUPS), 1]
        right[s] = r
        return r + sb * v, u + p[None, None] * r, p * sigma

    v, u, _ = lax.fori_loop(0, GROUPS, ends, (zero, zero, jnp.ones((8, 128), F32)))
    u_last = u * cb

    def up(s, v):
        v = right[s] + sb * v
        work[s] = v
        return v

    lax.fori_loop(0, GROUPS, up, v * cb)
    gain = jnp.broadcast_to(sigma / (1.0 - sigma * sigma), shape)
    back = jnp.broadcast_to((1.0 / SMOOTH) / (rho + 1.0 / rho), shape)

    def put(s, slot, value):
        out0[s, slot] = value[0]
        out1[s, slot] = value[1]

    def down(n, carry):
        u, after = carry
        s = GROUPS - 1 - n
        value = sb * u
        p = gain * (work[s] + value)
        put(s, 0, p)
        put(s + 1, 1, back * (p + after))
        return right[s] + value, p

    value = sb * u_last
    last = gain * (work[GROUPS - 1] + value)
    put(GROUPS - 1, 0, last)
    _, head = lax.fori_loop(1, GROUPS, down, (right[GROUPS - 1] + value, last))
    put(0, 1, back * (head + last))


def fold(value):
    return jnp.sum((value * value).reshape(16, 8, 128), axis=0)


def inverse_kernel(*refs, pair):
    if pair == 0:
        spec, keep, img, ty, tx, out, sums, stack = refs
    else:
        spec, keep, img, ty, tx, lower, out, sums, stack = refs
    first = lax.broadcasted_iota(jnp.int32, (16, 8, 128), 1) < 4
    inner = jnp.zeros((8, 128), F32)
    cross = jnp.zeros((8, 128), F32)
    for i in range(2):
        qo = [img[i, c, 1] for c in range(5)]
        go = spread(mixed(qo))
        for c in range(5):
            p_even, p_odd = spec[0:16, 0, c], spec[16:32, 0, c]
            w_even = spec[0:16, 1, c] + keep[0:16, 0, c]
            w_odd = spec[16:32, 1, c] + keep[16:32, 0, c]
            if i == 1:
                p_even, p_odd, w_even, w_odd = p_odd, p_even, w_odd, w_even
            push(stack, c, 0, jnp.where(first, w_even, w_odd).reshape(128, 128))
            push(stack, c, 1, jnp.where(first, p_even, p_odd).reshape(128, 128))
            both = jnp.dot(tx[i], stack[c], preferred_element_type=F32)
            even = KEEP * img[i, c, 0] + times_right(both[:, :128], ty[...])
            odd = times_right(both[:, 128:], ty[...])
            odd = KEEP * qo[c] + (odd + go[c]) * (1.0 / SMOOTH)
            out[i, c, 0] = even
            out[i, c, 1] = odd
            if i == 1:
                inner = inner + fold(even - out[0, c, 0]) + fold(odd - out[0, c, 1])
            elif pair == 1:
                cross = cross + fold(even - lower[0, c, 0]) + fold(odd - lower[0, c, 1])
    sums[0] = inner
    if pair == 1:
        sums[1] = cross


def edge_kernel(first_sums, second_sums, upper, above, out):
    edge = jnp.zeros((8, 128), F32)
    for c in range(5):
        for zz in range(2):
            edge = edge + fold(above[0, c, zz] - upper[0, c, zz])
    rows = [first_sums[0], second_sums[1], second_sums[0], edge]
    index = lax.broadcasted_iota(jnp.int32, (8, 128), 0)
    total = jnp.zeros((8, 128), F32)
    for g, row in enumerate(rows):
        total = jnp.where(index == g, jnp.sum(row), total)
    out[...] = jnp.broadcast_to(total, (128, 8, 128))


def final_kernel(centre, positions, where, sums, below, lower, upper, above, out, weights):
    @pl.when(pl.program_id(0) == 0)
    def _():
        arc = [jnp.zeros((8, 128), F32)]
        for k in range(LOCAL):
            block = jnp.sum(sums[k * GROUPS : (k + 1) * GROUPS], axis=0)
            dist = jnp.sqrt(block * (1.0 / CELLS) + EPS)
            for g in range(4):
                if k * 4 + g < IMAGES - 1:
                    row = jnp.broadcast_to(dist[g : g + 1], (8, 128))
                    arc.append(arc[-1] + row)
        base = where[0] * LOCAL - 2
        for m in range(LOCAL):
            c = centre[m]
            tau = positions[m] * arc[-1]

            def pick(index):
                value = arc[0]
                for j in range(1, IMAGES):
                    value = jnp.where(index == j, arc[j], value)
                return value

            a, b, d = pick(c - 1), pick(c), pick(c + 1)
            w = (
                (tau - b) * (tau - d) / ((a - b) * (a - d)),
                (tau - a) * (tau - d) / ((b - a) * (b - d)),
                (tau - a) * (tau - b) / ((d - a) * (d - b)),
            )
            for r in range(5):
                spot = base + m + r
                value = jnp.zeros((8, 128), F32)
                for n in range(3):
                    value = jnp.where(c - 1 + n == spot, w[n], value)
                weights[m, r] = value

    pieces = [below[0], below[1], lower[0], lower[1], upper[0], upper[1], above[0], above[1]]
    pieces = [p.reshape(32, 8, 128) for p in pieces]
    for m in range(LOCAL):
        acc = pieces[m] * weights[m, 0][None]
        for r in range(1, 5):
            acc = acc + pieces[m + r] * weights[m, r][None]
        out[m, 0] = acc.reshape(2, 128, 128)


def whole(shape):
    return pl.BlockSpec(shape, lambda *_: (0,) * len(shape))


SMEM = pl.BlockSpec(memory_space=pltpu.SMEM)


def params(mib):
    return pltpu.CompilerParams(
        dimension_semantics=("arbitrary",), vmem_limit_bytes=mib * 1024 * 1024
    )


def forward(images, ty, tx, rho):
    return pl.pallas_call(
        forward_kernel,
        out_shape=(
            jax.ShapeDtypeStruct((GROUPS, 2, 2, 5, 8, 128), F32),
            jax.ShapeDtypeStruct((GROUPS, 2, 5, 8, 128), F32),
        ),
        grid=(2,),
        in_specs=[
            pl.BlockSpec((2, 5, 2, 128, 128), lambda p: (p, 0, 0, 0, 0)),
            whole((256, 256)),
            whole((2, 128, 384)),
            whole((GROUPS, 8, 128)),
        ],
        out_specs=(
            pl.BlockSpec((GROUPS, 2, 1, 5, 8, 128), lambda p: (0, 0, p, 0, 0, 0)),
            pl.BlockSpec((GROUPS, 1, 5, 8, 128), lambda p: (0, p, 0, 0, 0)),
        ),
        scratch_shapes=[
            pltpu.VMEM((7, 384, 256), BF16),
            pltpu.VMEM((2, 7, 128, 256), F32),
        ],
        compiler_params=params(32),
        name="forward",
    )(images, ty, tx, rho)


def solve(f, rho):
    half = jax.ShapeDtypeStruct((GROUPS, 2, 5, 8, 128), F32)
    where = lax.axis_index("gz").astype(jnp.int32).reshape(1)
    return pl.pallas_call(
        solve_kernel,
        out_shape=(half, half),
        grid_spec=pltpu.PrefetchScalarGridSpec(
            num_scalar_prefetch=1,
            grid=(1,),
            in_specs=[
                whole((GROUPS, 2, 2, 5, 8, 128)),
                pl.BlockSpec((1, 8, 128), lambda i, w: (w[0], 0, 0)),
            ],
            out_specs=(whole((GROUPS, 2, 5, 8, 128)), whole((GROUPS, 2, 5, 8, 128))),
            scratch_shapes=[
                pltpu.VMEM((GROUPS, 2, 5, 8, 128), F32),
                pltpu.VMEM((GROUPS, 2, 5, 8, 128), F32),
            ],
        ),
        compiler_params=params(32),
        name="solve",
    )(where, f, rho)


def inverse(spec, keep, images, pair, ty, tx, *lower):
    specs = [
        whole((GROUPS, 2, 5, 8, 128)),
        pl.BlockSpec((GROUPS, 1, 5, 8, 128), lambda p: (0, pair, 0, 0, 0)),
        pl.BlockSpec((2, 5, 2, 128, 128), lambda p: (pair, 0, 0, 0, 0)),
        whole((256, 256)),
        whole((2, 128, 384)),
    ]
    if pair == 1:
        specs.append(pl.BlockSpec((1, 5, 2, 128, 128), lambda p: (1, 0, 0, 0, 0)))
    return pl.pallas_call(
        functools.partial(inverse_kernel, pair=pair),
        out_shape=(
            jax.ShapeDtypeStruct((2, 5, 2, 128, 128), F32),
            jax.ShapeDtypeStruct((2, 8, 128), F32),
        ),
        grid=(1,),
        in_specs=specs,
        out_specs=(whole((2, 5, 2, 128, 128)), whole((2, 8, 128))),
        scratch_shapes=[pltpu.VMEM((5, 384, 256), BF16)],
        compiler_params=params(32),
        name="inverse",
    )(spec, keep, images, ty, tx, *lower)


def edge(first_sums, second_sums, upper, above):
    return pl.pallas_call(
        edge_kernel,
        out_shape=jax.ShapeDtypeStruct((128, 8, 128), F32),
        grid=(1,),
        in_specs=[
            whole((2, 8, 128)),
            whole((2, 8, 128)),
            pl.BlockSpec((1, 5, 2, 128, 128), lambda p: (1, 0, 0, 0, 0)),
            pl.BlockSpec((1, 5, 2, 128, 128), lambda p: (0, 0, 0, 0, 0)),
        ],
        out_specs=whole((128, 8, 128)),
        compiler_params=params(16),
        name="edge",
    )(first_sums, second_sums, upper, above)


def final(centre, positions, sums, below, lower, upper, above):
    pair = pl.BlockSpec((2, 1, 2, 128, 128), lambda c: (0, c, 0, 0, 0))
    where = lax.axis_index("img").astype(jnp.int32).reshape(1)
    return pl.pallas_call(
        final_kernel,
        out_shape=jax.ShapeDtypeStruct((4, 5, 2, 128, 128), F32),
        grid=(5,),
        in_specs=[SMEM, SMEM, SMEM, whole((128, 8, 128)), pair, pair, pair, pair],
        out_specs=pl.BlockSpec((4, 1, 2, 128, 128), lambda c: (0, c, 0, 0, 0)),
        scratch_shapes=[pltpu.VMEM((4, 5, 8, 128), F32)],
        compiler_params=params(32),
        name="final",
    )(centre, positions, where, sums, below, lower, upper, above)


def local(images, centre, positions):
    forward_y, inverse_y, forward_x, inverse_x, rho = (jnp.asarray(t) for t in tables())
    rows = [(i, i + 1) for i in range(LOCAL - 1)]
    rows_back = [(b, a) for a, b in rows]
    f, keep = forward(images, forward_y, forward_x, rho)
    f = lax.all_to_all(f, "gz", 0, 0, tiled=True)
    u0, u1 = solve(f, rho)
    u0 = lax.all_to_all(u0, "gz", 0, 0, tiled=True)
    u1 = lax.all_to_all(u1, "gz", 0, 0, tiled=True)
    lower, first_sums = inverse(u0, keep, images, 0, inverse_y, inverse_x)
    above = lax.ppermute(lower, "img", rows_back)
    upper, second_sums = inverse(u1, keep, images, 1, inverse_y, inverse_x, lower)
    below = lax.ppermute(upper, "img", rows)
    part = edge(first_sums, second_sums, upper, above)
    sums = lax.all_to_all(part, ("img", "gz"), 0, 0, tiled=True)
    return final(centre, positions, sums, below, lower, upper, above)


def solution(mesh):
    in_specs = (P("img", None, "gz", None, None), P("img"), P("img"))
    out_specs = P("img", None, "gz", None, None)
    return jax.shard_map(local, mesh=mesh, in_specs=in_specs, out_specs=out_specs, check_vma=False)
```

time: 174 us -> 147 us (0.84)
  waiting for transfers between devices: 81.5 us -> 57.9 us
  starting transfers between devices: 39.2 us -> 33.7 us
  local copies, waits for them, and re-layouts: 5.64 us -> 11 us
  Pallas kernels: 21.8 us -> 19.8 us
    ppermute x2 -> x0, waiting for transfers between devices: 22.7 us -> none  [the longest x1 22.7 us: local(): low = lax.ppermute(rotated(1), 'gz', ring)]
    all_to_all x1, waiting for transfers between devices: 13.4 us -> 4.81 us  [local(): sums = lax.all_to_all(part, ('img', 'gz'), 0, 0, tiled=True)]
    ppermute x1, waiting for transfers between devices: 0.26 us -> 8.84 us  [local(): below = lax.ppermute(upper, 'img', rows)]
    unnamed x22 -> x32, local copies, waits for them, and re-layouts: 2.84 us -> 11 us
    ppermute x2 -> x0, starting transfers between devices: 7.94 us -> none  [the longest x1 5.41 us: local(): high = lax.ppermute(rotated(0), 'gz', back)]
    all_to_all x1, starting transfers between devices: 7.46 us -> 9.85 us  [local(): f = lax.all_to_all(f, 'gz', 0, 0, tiled=True)]
    pallas_call x1, Pallas kernels: 3.03 us -> 1.11 us  [solve(): pl.pallas_call(solve_kernel, out_shape=(half, half), grid_spec=pltpu.Pref...]
    squeeze x1 -> x0, local copies, waits for them, and re-layouts: 1.89 us -> none  [rotated(): q = images[:, :, plane]]
  transfers between devices with their start and end apart: 7 -> 5, of which waited for: 6 -> 5; matrix products, arithmetic and copies ran while one was open for 1% -> 0% of each run, Pallas kernels for 5% -> 6%
where the time goes in v1:
time: 147 us
  waiting for transfers between devices  57.9 us (39%)
  starting transfers between devices  33.7 us (23%)
  blocking collectives  24 us (16%)
  Pallas kernels  19.8 us (13%)
  local copies, waits for them, and re-layouts  11 us (7%)
    all_to_all x1, waiting for transfers between devices, local(): f = lax.all_to_all(f, 'gz', 0, 0, tiled=True)  34.7 us
    all_to_all x1, blocking collectives, local(): u0 = lax.all_to_all(u0, 'gz', 0, 0, tiled=True)  24 us
    unnamed x32, local copies, waits for them, and re-layouts  11 us
    all_to_all x1, starting transfers between devices, local(): f = lax.all_to_all(f, 'gz', 0, 0, tiled=True)  9.85 us
    ppermute x1, waiting for transfers between devices, local(): below = lax.ppermute(upper, 'img', rows)  8.84 us
    ppermute x1, starting transfers between devices, local(): below = lax.ppermute(upper, 'img', rows)  8.04 us
    all_to_all x1, waiting for transfers between devices, local(): u1 = lax.all_to_all(u1, 'gz', 0, 0, tiled=True)  7.35 us
    all_to_all x1, starting transfers between devices, local(): sums = lax.all_to_all(part, ('img', 'gz'), 0, 0, tiled=True)  6.39 us
  transfers between devices with their start and end apart: 5, of which 5 were waited for; matrix products, arithmetic and copies ran while one was open for 0% of the time, Pallas kernels for 6%

profile of v1, /device:TPU:1, one launch (start us, length us, event | category | flops | bytes accessed | tf_op | source)
XLA Modules:
  0.0 146.5 jit_solution(13841773061250641289)
XLA Ops:
  0.0 1.7 %copy-done = f32[4,5,2,128,128]{4,3,2,1,0:T(8,128)S(1)} copy-done((f32[4,5,2,128,128]{4,3,2,1,0:T(8,128)S(1)}, f32[4,5,2,128,128]{4,3,2,1,0:T(8,128)}, u32[]{:S(2)}) %copy-start) | copy-done | bytes 2621464
  2.6 0.9 copy-done.12
  4.5 4.5 %forward.1 = (f32[32,2,2,5,8,128]{5,4,3,2,1,0:T(8,128)S(1)}, f32[32,2,5,8,128]{4,3,2,1,0:T(8,128)S(1)}) custom-call(f32[4,5,2,128,128]{4,3,2,1,0:T(8,128)S(1)} %copy-done, bf16[256,256]{1,0:T(8,128)(2,1)S(1)} %copy-done.13, bf16[2,128,384]{2,1,0:T(8,128)(2,1)S(1)} %copy-done.12, f32[32,8,128]{2,1,0:T(8,128)S(1)} %copy-done.9), custom_call_target="tpu_custom_call" | custom-call | tf_op jit(solution)/shard_map/forward/pallas_call | solution.py:332
  9.0 1.1 copy-done.3
  10.0 1.5 %copy-done.6 = f32[32,2,2,5,8,128]{5,4,3,2,1,0:T(8,128)} copy-done((f32[32,2,2,5,8,128]{5,4,3,2,1,0:T(8,128)}, f32[32,2,2,5,8,128]{5,4,3,2,1,0:T(8,128)S(1)}, u32[]{:S(2)}) %copy-start.6) | copy-done | bytes 2621464
  11.5 9.8 %all-to-all-start = ((f32[32,2,2,5,8,128]{5,4,3,2,1,0:T(8,128)}), f32[32,2,2,5,8,128]{5,4,3,2,1,0:T(8,128)S(1)}, u32[]{:S(2)}, u32[]{:S(2)}) async-start(f32[32,2,2,5,8,128]{5,4,3,2,1,0:T(8,128)} %copy-done.6), calls=%async_computation | async-start | bytes 5242880 | tf_op jit(solution)/shard_map/all_to_all | solution.py:444
  21.4 34.7 %all-to-all-done.f = f32[32,2,2,5,8,128]{5,4,3,2,1,0:T(8,128)S(1)} async-done(((f32[32,2,2,5,8,128]{5,4,3,2,1,0:T(8,128)}), f32[32,2,2,5,8,128]{5,4,3,2,1,0:T(8,128)S(1)}, u32[]{:S(2)}, u32[]{:S(2)}) %all-to-all-start) | async-done | bytes 2621472 | tf_op jit(solution)/shard_map/all_to_all | solution.py:444
  56.1 1.1 solve.1
  57.3 24.0 %all_to_all.20.refs_0_ = f32[32,2,5,8,128]{4,3,2,1,0:T(8,128)} all-to-all(f32[32,2,5,8,128]{4,3,2,1,0:T(8,128)S(1)} %get-tuple-element.14), channel_id=1, replica_groups=mesh['img'=4,'gz'=32] {'gz'}, dimensions={0} | all-to-all | bytes 2621440 | tf_op jit(solution)/shard_map/all_to_all | solution.py:446
  81.3 5.0 %all-to-all-start.2 = ((f32[32,2,5,8,128]{4,3,2,1,0:T(8,128)}), f32[32,2,5,8,128]{4,3,2,1,0:T(8,128)}, u32[]{:S(2)}, u32[]{:S(2)}) async-start(f32[32,2,5,8,128]{4,3,2,1,0:T(8,128)} %copy-done.7), calls=%async_computation.2 | async-start | bytes 2621440 | tf_op jit(solution)/shard_map/all_to_all | solution.py:447
  86.3 1.3 copy-done.2
  87.6 1.3 copy-done.4
  88.9 2.3 %inverse.2 = (f32[2,5,2,128,128]{4,3,2,1,0:T(8,128)}, f32[2,8,128]{2,1,0:T(8,128)S(1)}) custom-call(f32[32,2,5,8,128]{4,3,2,1,0:T(8,128)S(1)} %copy-done.2, f32[32,2,5,8,128]{4,3,2,1,0:T(8,128)S(1)} %copy-done.4, f32[4,5,2,128,128]{4,3,2,1,0:T(8,128)S(1)} %copy-done.1, bf16[256,256]{1,0:T(8,128)(2,1)S(1)} %copy-done.11, bf16[2,128,384]{2,1,0:T(8,128)(2,1)S(1)} %copy-done.8), custom_call_target="tpu_custom_call" | custom-call | tf_op jit(solution)/shard_map/inverse/pallas_call | solution.py:392
  91.3 4.5 %collective-permute-start = (f32[2,5,2,128,128]{4,3,2,1,0:T(8,128)}, f32[2,5,2,128,128]{4,3,2,1,0:T(8,128)}, u32[]{:S(2)}, u32[]{:S(2)}) collective-permute-start(f32[2,5,2,128,128]{4,3,2,1,0:T(8,128)} %get-tuple-element.18.refs_5_.lower), channel_id=1, source_target_pairs={{32,0},{64,32},{96,64},{33,1},{65,33},{97,65},{34,2},{66,34},{98,6... | collective-permute-start | bytes 3932168 | tf_op jit(solution)/shard_map/ppermute | solution.py:449
  95.7 7.3 %all-to-all-done.2.refs_0_ = f32[32,2,5,8,128]{4,3,2,1,0:T(8,128)} async-done(((f32[32,2,5,8,128]{4,3,2,1,0:T(8,128)}), f32[32,2,5,8,128]{4,3,2,1,0:T(8,128)}, u32[]{:S(2)}, u32[]{:S(2)}) %all-to-all-start.2) | async-done | bytes 1310752 | tf_op jit(solution)/shard_map/all_to_all | solution.py:447
  103.1 1.3 copy-done.5
  104.4 3.8 %inverse.3 = (f32[2,5,2,128,128]{4,3,2,1,0:T(8,128)}, f32[2,8,128]{2,1,0:T(8,128)S(1)}) custom-call(f32[32,2,5,8,128]{4,3,2,1,0:T(8,128)} %all-to-all-done.2.refs_0_, f32[32,2,5,8,128]{4,3,2,1,0:T(8,128)S(1)} %copy-done.5, f32[4,5,2,128,128]{4,3,2,1,0:T(8,128)S(1)} %copy-done.1, bf16[256,256]{1,0:T(8,128)(2,1)S(1)} %copy-done.11, ...), custom_call_target="tpu_custom_call" | custom-call | tf_op jit(solution)/shard_map/inverse/pallas_call | solution.py:392
  108.2 8.0 %collective-permute-start.1 = (f32[2,5,2,128,128]{4,3,2,1,0:T(8,128)}, f32[2,5,2,128,128]{4,3,2,1,0:T(8,128)S(1)}, u32[]{:S(2)}, u32[]{:S(2)}) collective-permute-start(f32[2,5,2,128,128]{4,3,2,1,0:T(8,128)} %get-tuple-element.20.upper), channel_id=1, source_target_pairs={{0,32},{32,64},{64,96},{1,33},{33,65},{65,97},{2,34},{34,66},{66,9... | collective-permute-start | bytes 3932168 | tf_op jit(solution)/shard_map/ppermute | solution.py:451
  116.3 2.2 %collective-permute-done.above = f32[2,5,2,128,128]{4,3,2,1,0:T(8,128)} collective-permute-done((f32[2,5,2,128,128]{4,3,2,1,0:T(8,128)}, f32[2,5,2,128,128]{4,3,2,1,0:T(8,128)}, u32[]{:S(2)}, u32[]{:S(2)}) %collective-permute-start) | collective-permute-done | bytes 1310752 | tf_op jit(solution)/shard_map/ppermute | solution.py:449
  118.5 2.3 %edge.1 = f32[128,8,128]{2,1,0:T(8,128)} custom-call(f32[2,8,128]{2,1,0:T(8,128)S(1)} %get-tuple-element.16.first_sums, f32[2,8,128]{2,1,0:T(8,128)S(1)} %get-tuple-element.19.second_sums, f32[2,5,2,128,128]{4,3,2,1,0:T(8,128)} %get-tuple-element.20.upper, f32[2,5,2,128,128]{4,3,2,1,0:T(8,128)} %collective-permute-done.above), custom_call_target="tpu_custom_call" | custom-call | tf_op jit(solution)/shard_map/edge/pallas_call | solution.py:408
  120.8 6.4 %all-to-all-start.3 = ((f32[128,8,128]{2,1,0:T(8,128)}), f32[128,8,128]{2,1,0:T(8,128)S(1)}, u32[]{:S(2)}, u32[]{:S(2)}) async-start(f32[128,8,128]{2,1,0:T(8,128)} %edge.1), calls=%async_computation.3 | async-start | bytes 1048576 | tf_op jit(solution)/shard_map/all_to_all | solution.py:453
  127.2 8.8 %collective-permute-done.1.below = f32[2,5,2,128,128]{4,3,2,1,0:T(8,128)S(1)} collective-permute-done((f32[2,5,2,128,128]{4,3,2,1,0:T(8,128)}, f32[2,5,2,128,128]{4,3,2,1,0:T(8,128)S(1)}, u32[]{:S(2)}, u32[]{:S(2)}) %collective-permute-start.1) | collective-permute-done | bytes 1310752 | tf_op jit(solution)/shard_map/ppermute | solution.py:451
  136.0 4.8 %all-to-all-done.3.sums = f32[128,8,128]{2,1,0:T(8,128)S(1)} async-done(((f32[128,8,128]{2,1,0:T(8,128)}), f32[128,8,128]{2,1,0:T(8,128)S(1)}, u32[]{:S(2)}, u32[]{:S(2)}) %all-to-all-start.3) | async-done | bytes 524320 | tf_op jit(solution)/shard_map/all_to_all | solution.py:453
  140.8 5.7 %final.1 = f32[4,5,2,128,128]{4,3,2,1,0:T(8,128)} custom-call(s32[4]{0:T(128)S(1)} %copy-done.14, f32[4]{0:T(128)S(1)} %copy-done.15, s32[1]{0:T(128)} %bitcast.where, f32[128,8,128]{2,1,0:T(8,128)S(1)} %all-to-all-done.3.sums, f32[2,5,2,128,128]{4,3,2,1,0:T(8,128)S(1)} %collective-permute-done.1.below, ...), custom_call_target="tpu_custom_call" | custom-call | tf_op jit(solution)/shard_map/final/pallas_call | solution.py:427
  (25 shorter events, 1.9 us)
Async XLA Ops:
  0.0 1.7 %copy-start = (f32[4,5,2,128,128]{4,3,2,1,0:T(8,128)S(1)}, f32[4,5,2,128,128]{4,3,2,1,0:T(8,128)}, u32[]{:S(2)}) copy-start(f32[4,5,2,128,128]{4,3,2,1,0:T(8,128)} %refs_2_.3) | copy-start | bytes 7864324
  1.7 0.9 copy-start.9
  2.6 0.9 copy-start.12
  3.6 0.9 copy-start.13
  9.0 1.1 copy-start.3
  10.0 1.5 %copy-start.6 = (f32[32,2,2,5,8,128]{5,4,3,2,1,0:T(8,128)}, f32[32,2,2,5,8,128]{5,4,3,2,1,0:T(8,128)S(1)}, u32[]{:S(2)}) copy-start(f32[32,2,2,5,8,128]{5,4,3,2,1,0:T(8,128)S(1)} %get-tuple-element.13) | copy-start | bytes 7864324
  11.5 44.6 %copy-start.10 = (f32[32,8,128]{2,1,0:T(8,128)S(1)}, f32[32,8,128]{2,1,0:T(8,128)}, u32[]{:S(2)}) copy-start(f32[32,8,128]{2,1,0:T(8,128)} %constant.23.clone.rho_ref) | copy-start | bytes 393220
  11.5 44.6 %all-to-all-start = ((f32[32,2,2,5,8,128]{5,4,3,2,1,0:T(8,128)}), f32[32,2,2,5,8,128]{5,4,3,2,1,0:T(8,128)S(1)}, u32[]{:S(2)}, u32[]{:S(2)}) async-start(f32[32,2,2,5,8,128]{5,4,3,2,1,0:T(8,128)} %copy-done.6), calls=%async_computation | async-start | bytes 5242880 | tf_op jit(solution)/shard_map/all_to_all | solution.py:444
  57.2 24.1 %copy-start.7 = (f32[32,2,5,8,128]{4,3,2,1,0:T(8,128)}, f32[32,2,5,8,128]{4,3,2,1,0:T(8,128)S(1)}, u32[]{:S(2)}) copy-start(f32[32,2,5,8,128]{4,3,2,1,0:T(8,128)S(1)} %get-tuple-element.17) | copy-start | bytes 3932164
  57.2 29.0 %copy-start.8 = (bf16[2,128,384]{2,1,0:T(8,128)(2,1)S(1)}, bf16[2,128,384]{2,1,0:T(8,128)(2,1)}, u32[]{:S(2)}) copy-start(bf16[2,128,384]{2,1,0:T(8,128)(2,1)} %constant.22.clone.refs_4_) | copy-start | bytes 589828
  57.3 29.0 %copy-start.11 = (bf16[256,256]{1,0:T(8,128)(2,1)S(1)}, bf16[256,256]{1,0:T(8,128)(2,1)}, u32[]{:S(2)}) copy-start(bf16[256,256]{1,0:T(8,128)(2,1)} %constant.20.clone.refs_3_) | copy-start | bytes 393220
  81.3 5.0 %copy-start.1 = (f32[4,5,2,128,128]{4,3,2,1,0:T(8,128)S(1)}, f32[4,5,2,128,128]{4,3,2,1,0:T(8,128)}, u32[]{:S(2)}) copy-start(f32[4,5,2,128,128]{4,3,2,1,0:T(8,128)} %refs_2_.3) | copy-start | bytes 7864324
  81.3 21.8 %all-to-all-start.2 = ((f32[32,2,5,8,128]{4,3,2,1,0:T(8,128)}), f32[32,2,5,8,128]{4,3,2,1,0:T(8,128)}, u32[]{:S(2)}, u32[]{:S(2)}) async-start(f32[32,2,5,8,128]{4,3,2,1,0:T(8,128)} %copy-done.7), calls=%async_computation.2 | async-start | bytes 2621440 | tf_op jit(solution)/shard_map/all_to_all | solution.py:447
  86.3 1.3 copy-start.2
  87.6 1.3 copy-start.4
  91.3 27.2 %collective-permute-start = (f32[2,5,2,128,128]{4,3,2,1,0:T(8,128)}, f32[2,5,2,128,128]{4,3,2,1,0:T(8,128)}, u32[]{:S(2)}, u32[]{:S(2)}) collective-permute-start(f32[2,5,2,128,128]{4,3,2,1,0:T(8,128)} %get-tuple-element.18.refs_5_.lower), channel_id=1, source_target_pairs={{32,0},{64,32},{96,64},{33,1},{65,33},{97,65},{34,2},{66,34},{98,6... | collective-permute-start | bytes 3932168 | tf_op jit(solution)/shard_map/ppermute | solution.py:449
  103.1 1.3 copy-start.5
  108.2 27.8 %collective-permute-start.1 = (f32[2,5,2,128,128]{4,3,2,1,0:T(8,128)}, f32[2,5,2,128,128]{4,3,2,1,0:T(8,128)S(1)}, u32[]{:S(2)}, u32[]{:S(2)}) collective-permute-start(f32[2,5,2,128,128]{4,3,2,1,0:T(8,128)} %get-tuple-element.20.upper), channel_id=1, source_target_pairs={{0,32},{32,64},{64,96},{1,33},{33,65},{65,97},{2,34},{34,66},{66,9... | collective-permute-start | bytes 3932168 | tf_op jit(solution)/shard_map/ppermute | solution.py:451
  118.4 22.4 %copy-start.14 = (s32[4]{0:T(128)S(1)}, s32[4]{0:T(128)}, u32[]{:S(2)}) copy-start(s32[4]{0:T(128)} %centre.1) | copy-start | bytes 52
  118.4 22.4 %copy-start.15 = (f32[4]{0:T(128)S(1)}, f32[4]{0:T(128)}, u32[]{:S(2)}) copy-start(f32[4]{0:T(128)} %positions.1) | copy-start | bytes 52
  120.8 20.1 %all-to-all-start.3 = ((f32[128,8,128]{2,1,0:T(8,128)}), f32[128,8,128]{2,1,0:T(8,128)S(1)}, u32[]{:S(2)}, u32[]{:S(2)}) async-start(f32[128,8,128]{2,1,0:T(8,128)} %edge.1), calls=%async_computation.3 | async-start | bytes 1048576 | tf_op jit(solution)/shard_map/all_to_all | solution.py:453

commit v2 on v1

--- a/solution.py
+++ b/solution.py
@@ -18,6 +18,11 @@
 SMOOTH = 64.0
 EPS = 1e-6
 KEEP = 1.0 - 1.0 / SMOOTH
+FORWARD_MIB = 60
+SOLVE_MIB = 32
+INVERSE_MIB = 64
+EDGE_MIB = 64
+FINAL_MIB = 64
 F32 = jnp.float32
 BF16 = jnp.bfloat16
 
@@ -169,7 +174,7 @@
             keep[rows, 0, c] = back * y
 
 
-def solve_kernel(where, f, rho_ref, out0, out1, right, work):
+def solve_kernel(where, f, rho_ref, out, right, work):
     del where
     rho = rho_ref[0]
     sigma = rho * rho
@@ -201,8 +206,7 @@
     back = jnp.broadcast_to((1.0 / SMOOTH) / (rho + 1.0 / rho), shape)
 
     def put(s, slot, value):
-        out0[s, slot] = value[0]
-        out1[s, slot] = value[1]
+        out[s, slot] = value
 
     def down(n, carry):
         u, after = carry
@@ -225,63 +229,72 @@
 
 
 def inverse_kernel(*refs, pair):
+    spec, keep, img, mix, minus, ty, tx = refs[:7]
+    stack = refs[-1]
     if pair == 0:
-        spec, keep, img, ty, tx, out, sums, stack = refs
+        out, sums = refs[7:9], refs[9]
     else:
-        spec, keep, img, ty, tx, lower, out, sums, stack = refs
+        lower, upper, sums = refs[7:10]
+        out = [upper.at[0], upper.at[1]]
+    c = pl.program_id(0)
+    weight = jnp.where(c == 0, 0.5, jnp.where(c == 3, -0.5, jnp.where(c == 2, 0.25, -0.25)))
+    weight = weight * (1.0 / SMOOTH)
+    other = jnp.where(c == 1, 0.25 / SMOOTH, 0.0)
     first = lax.broadcasted_iota(jnp.int32, (16, 8, 128), 1) < 4
-    inner = jnp.zeros((8, 128), F32)
-    cross = jnp.zeros((8, 128), F32)
+
+    @pl.when(c == 0)
+    def _():
+        sums[...] = jnp.zeros_like(sums)
+
+    planes = []
     for i in range(2):
-        qo = [img[i, c, 1] for c in range(5)]
-        go = spread(mixed(qo))
-        for c in range(5):
-            p_even, p_odd = spec[0:16, 0, c], spec[16:32, 0, c]
-            w_even = spec[0:16, 1, c] + keep[0:16, 0, c]
-            w_odd = spec[16:32, 1, c] + keep[16:32, 0, c]
-            if i == 1:
-                p_even, p_odd, w_even, w_odd = p_odd, p_even, w_odd, w_even
-            push(stack, c, 0, jnp.where(first, w_even, w_odd).reshape(128, 128))
-            push(stack, c, 1, jnp.where(first, p_even, p_odd).reshape(128, 128))
-            both = jnp.dot(tx[i], stack[c], preferred_element_type=F32)
-            even = KEEP * img[i, c, 0] + times_right(both[:, :128], ty[...])
-            odd = times_right(both[:, 128:], ty[...])
-            odd = KEEP * qo[c] + (odd + go[c]) * (1.0 / SMOOTH)
-            out[i, c, 0] = even
-            out[i, c, 1] = odd
-            if i == 1:
-                inner = inner + fold(even - out[0, c, 0]) + fold(odd - out[0, c, 1])
-            elif pair == 1:
-                cross = cross + fold(even - lower[0, c, 0]) + fold(odd - lower[0, c, 1])
-    sums[0] = inner
+        p_even, p_odd = spec[0:16, 0, 0, 0], spec[16:32, 0, 0, 0]
+        w_even = spec[0:16, 1, 0, 0] + keep[0:16, 0, 0]
+        w_odd = spec[16:32, 1, 0, 0] + keep[16:32, 0, 0]
+        if i == 1:
+            p_even, p_odd, w_even, w_odd = p_odd, p_even, w_odd, w_even
+        push(stack, i, 0, jnp.where(first, w_even, w_odd).reshape(128, 128))
+        push(stack, i, 1, jnp.where(first, p_even, p_odd).reshape(128, 128))
+        both = jnp.dot(tx[i], stack[i], preferred_element_type=F32)
+        even = KEEP * img[i, 0, 0] + times_right(both[:, :128], ty[...])
+        odd = times_right(both[:, 128:], ty[...])
+        odd = KEEP * img[i, 0, 1] + odd * (1.0 / SMOOTH)
+        odd = odd + (weight * mix[i, 0, 0] + other * minus[i, 0, 0])
+        out[i][0, 0] = even
+        out[i][0, 1] = odd
+        planes.append((even, odd))
+    sums[0] += fold(planes[1][0] - planes[0][0]) + fold(planes[1][1] - planes[0][1])
     if pair == 1:
-        sums[1] = cross
+        sums[1] += fold(planes[0][0] - lower[0, 0]) + fold(planes[0][1] - lower[0, 1])
 
 
 def edge_kernel(first_sums, second_sums, upper, above, out):
     edge = jnp.zeros((8, 128), F32)
     for c in range(5):
         for zz in range(2):
-            edge = edge + fold(above[0, c, zz] - upper[0, c, zz])
+            edge = edge + fold(above[c, zz] - upper[0, c, zz])
     rows = [first_sums[0], second_sums[1], second_sums[0], edge]
-    index = lax.broadcasted_iota(jnp.int32, (8, 128), 0)
-    total = jnp.zeros((8, 128), F32)
+    index = lax.broadcasted_iota(jnp.int32, (1, 128), 1)
+    total = jnp.zeros((1, 128), F32)
     for g, row in enumerate(rows):
         total = jnp.where(index == g, jnp.sum(row), total)
-    out[...] = jnp.broadcast_to(total, (128, 8, 128))
-
-
-def final_kernel(centre, positions, where, sums, below, lower, upper, above, out, weights):
+    out[...] = jnp.broadcast_to(total, (128, 1, 128))
+
+
+def final_kernel(
+    centre, positions, where, sums, below, s0, s1, upper, a0, a1, out, weights
+):
     @pl.when(pl.program_id(0) == 0)
     def _():
         arc = [jnp.zeros((8, 128), F32)]
+        lane = lax.broadcasted_iota(jnp.int32, (1, 128), 1)
         for k in range(LOCAL):
             block = jnp.sum(sums[k * GROUPS : (k + 1) * GROUPS], axis=0)
             dist = jnp.sqrt(block * (1.0 / CELLS) + EPS)
             for g in range(4):
                 if k * 4 + g < IMAGES - 1:
-                    row = jnp.broadcast_to(dist[g : g + 1], (8, 128))
-                    arc.append(arc[-1] + row)
+                    value = jnp.sum(jnp.where(lane == g, dist, 0.0), axis=1, keepdims=True)
+                    arc.append(arc[-1] + jnp.broadcast_to(value, (8, 128)))
         base = where[0] * LOCAL - 2
         for m in range(LOCAL):
             c = centre[m]
@@ -306,8 +319,8 @@
                     value = jnp.where(c - 1 + n == spot, w[n], value)
                 weights[m, r] = value
 
-    pieces = [below[0], below[1], lower[0], lower[1], upper[0], upper[1], above[0], above[1]]
-    pieces = [p.reshape(32, 8, 128) for p in pieces]
+    pieces = [below[0], below[1], s0, s1, upper[0], upper[1], a0, a1]
+    pieces = [p[...].reshape(32, 8, 128) for p in pieces]
     for m in range(LOCAL):
         acc = pieces[m] * weights[m, 0][None]
         for r in range(1, 5):
@@ -324,8 +337,12 @@
 
 def params(mib):
     return pltpu.CompilerParams(
-        dimension_semantics=("arbitrary",), vmem_limit_bytes=mib * 1024 * 1024
+        dimension_semantics=("arbitrary",), vmem_limit_bytes=min(int(mib * 1024 * 1024), 67_043_328)
     )
+
+
+def cost(flops, moved):
+    return pl.CostEstimate(flops=flops, bytes_accessed=moved, transcendentals=0)
 
 
 def forward(images, ty, tx, rho):
@@ -350,90 +367,110 @@
             pltpu.VMEM((7, 384, 256), BF16),
             pltpu.VMEM((2, 7, 128, 256), F32),
         ],
-        compiler_params=params(32),
+        compiler_params=params(FORWARD_MIB),
+        cost_estimate=cost(3000000000, 9000000),
         name="forward",
     )(images, ty, tx, rho)
 
 
 def solve(f, rho):
-    half = jax.ShapeDtypeStruct((GROUPS, 2, 5, 8, 128), F32)
     where = lax.axis_index("gz").astype(jnp.int32).reshape(1)
+    shape = (GROUPS, 2, 2, 5, 8, 128)
     return pl.pallas_call(
         solve_kernel,
-        out_shape=(half, half),
+        out_shape=jax.ShapeDtypeStruct(shape, F32),
         grid_spec=pltpu.PrefetchScalarGridSpec(
             num_scalar_prefetch=1,
             grid=(1,),
             in_specs=[
-                whole((GROUPS, 2, 2, 5, 8, 128)),
+                whole(shape),
                 pl.BlockSpec((1, 8, 128), lambda i, w: (w[0], 0, 0)),
             ],
-            out_specs=(whole((GROUPS, 2, 5, 8, 128)), whole((GROUPS, 2, 5, 8, 128))),
+            out_specs=whole(shape),
             scratch_shapes=[
                 pltpu.VMEM((GROUPS, 2, 5, 8, 128), F32),
                 pltpu.VMEM((GROUPS, 2, 5, 8, 128), F32),
             ],
         ),
-        compiler_params=params(32),
+        compiler_params=params(SOLVE_MIB),
+        cost_estimate=cost(20000000, 6000000),
         name="solve",
     )(where, f, rho)
 
 
+def mix_index(pair):
+    def index(c):
+        source = jnp.where(c == 1, 0, jnp.where(c == 2, 4, jnp.where(c == 4, 2, 1)))
+        return pair, source, 1, 0, 0
+
+    return index
+
+
 def inverse(spec, keep, images, pair, ty, tx, *lower):
+    single = pl.BlockSpec((None, 2, 128, 128), lambda c: (c, 0, 0, 0))
+    flat = jax.ShapeDtypeStruct((5, 2, 128, 128), F32)
     specs = [
-        whole((GROUPS, 2, 5, 8, 128)),
-        pl.BlockSpec((GROUPS, 1, 5, 8, 128), lambda p: (0, pair, 0, 0, 0)),
-        pl.BlockSpec((2, 5, 2, 128, 128), lambda p: (pair, 0, 0, 0, 0)),
+        pl.BlockSpec((GROUPS, 2, 1, 1, 8, 128), lambda c: (0, 0, pair, c, 0, 0)),
+        pl.BlockSpec((GROUPS, 1, 1, 8, 128), lambda c: (0, pair, c, 0, 0)),
+        pl.BlockSpec((2, 1, 2, 128, 128), lambda c: (pair, c, 0, 0, 0)),
+        pl.BlockSpec((2, 1, 1, 128, 128), mix_index(pair)),
+        pl.BlockSpec((2, 1, 1, 128, 128), lambda c: (pair, 3, 1, 0, 0)),
         whole((256, 256)),
         whole((2, 128, 384)),
     ]
     if pair == 1:
-        specs.append(pl.BlockSpec((1, 5, 2, 128, 128), lambda p: (1, 0, 0, 0, 0)))
+        specs.append(pl.BlockSpec((1, 2, 128, 128), lambda c: (c, 0, 0, 0)))
+        out_shape = (jax.ShapeDtypeStruct((2, 5, 2, 128, 128), F32),)
+        out_specs = (pl.BlockSpec((2, 1, 2, 128, 128), lambda c: (0, c, 0, 0, 0)),)
+    else:
+        out_shape = (flat, flat)
+        out_specs = (pl.BlockSpec((1, 2, 128, 128), lambda c: (c, 0, 0, 0)),) * 2
     return pl.pallas_call(
         functools.partial(inverse_kernel, pair=pair),
-        out_shape=(
-            jax.ShapeDtypeStruct((2, 5, 2, 128, 128), F32),
-            jax.ShapeDtypeStruct((2, 8, 128), F32),
-        ),
-        grid=(1,),
+        out_shape=(*out_shape, jax.ShapeDtypeStruct((2, 8, 128), F32)),
+        grid=(5,),
         in_specs=specs,
-        out_specs=(whole((2, 5, 2, 128, 128)), whole((2, 8, 128))),
-        scratch_shapes=[pltpu.VMEM((5, 384, 256), BF16)],
-        compiler_params=params(32),
+        out_specs=(*out_specs, whole((2, 8, 128))),
+        scratch_shapes=[pltpu.VMEM((2, 384, 256), BF16)],
+        compiler_params=params(INVERSE_MIB),
+        cost_estimate=cost(2000000000, 6000000),
         name="inverse",
-    )(spec, keep, images, ty, tx, *lower)
+    )(spec, keep, images, images, images, ty, tx, *lower)
 
 
 def edge(first_sums, second_sums, upper, above):
     return pl.pallas_call(
         edge_kernel,
-        out_shape=jax.ShapeDtypeStruct((128, 8, 128), F32),
+        out_shape=jax.ShapeDtypeStruct((128, 1, 128), F32),
         grid=(1,),
         in_specs=[
             whole((2, 8, 128)),
             whole((2, 8, 128)),
             pl.BlockSpec((1, 5, 2, 128, 128), lambda p: (1, 0, 0, 0, 0)),
-            pl.BlockSpec((1, 5, 2, 128, 128), lambda p: (0, 0, 0, 0, 0)),
+            whole((5, 2, 128, 128)),
         ],
-        out_specs=whole((128, 8, 128)),
-        compiler_params=params(16),
+        out_specs=whole((128, 1, 128)),
+        compiler_params=params(EDGE_MIB),
+        cost_estimate=cost(2000000, 1300000),
         name="edge",
     )(first_sums, second_sums, upper, above)
 
 
-def final(centre, positions, sums, below, lower, upper, above):
+def final(centre, positions, sums, below, s0, s1, upper, a0, a1):
     pair = pl.BlockSpec((2, 1, 2, 128, 128), lambda c: (0, c, 0, 0, 0))
+    one = pl.BlockSpec((1, 2, 128, 128), lambda c: (c, 0, 0, 0))
     where = lax.axis_index("img").astype(jnp.int32).reshape(1)
     return pl.pallas_call(
         final_kernel,
         out_shape=jax.ShapeDtypeStruct((4, 5, 2, 128, 128), F32),
         grid=(5,),
-        in_specs=[SMEM, SMEM, SMEM, whole((128, 8, 128)), pair, pair, pair, pair],
+        in_specs=[SMEM, SMEM, SMEM, whole((128, 1, 128)), pair, one, one, pair, one, one],
         out_specs=pl.BlockSpec((4, 1, 2, 128, 128), lambda c: (0, c, 0, 0, 0)),
         scratch_shapes=[pltpu.VMEM((4, 5, 8, 128), F32)],
-        compiler_params=params(32),
+        compiler_params=params(FINAL_MIB),
+        cost_estimate=cost(30000000, 8000000),
         name="final",
-    )(centre, positions, where, sums, below, lower, upper, above)
+    )(centre, positions, where, sums, below, s0, s1, upper, a0, a1)
 
 
 def local(images, centre, positions):
@@ -442,19 +479,21 @@
     rows_back = [(b, a) for a, b in rows]
     f, keep = forward(images, forward_y, forward_x, rho)
     f = lax.all_to_all(f, "gz", 0, 0, tiled=True)
-    u0, u1 = solve(f, rho)
-    u0 = lax.all_to_all(u0, "gz", 0, 0, tiled=True)
-    u1 = lax.all_to_all(u1, "gz", 0, 0, tiled=True)
-    lower, first_sums = inverse(u0, keep, images, 0, inverse_y, inverse_x)
-    above = lax.ppermute(lower, "img", rows_back)
-    upper, second_sums = inverse(u1, keep, images, 1, inverse_y, inverse_x, lower)
+    u = solve(f, rho)
+    u = lax.all_to_all(u, "gz", 0, 0, tiled=True)
+    s0, s1, first_sums = inverse(u, keep, images, 0, inverse_y, inverse_x)
+    a0 = lax.ppermute(s0, "img", rows_back)
+    a1 = lax.ppermute(s1, "img", rows_back)
+    upper, second_sums = inverse(u, keep, images, 1, inverse_y, inverse_x, s1)
     below = lax.ppermute(upper, "img", rows)
-    part = edge(first_sums, second_sums, upper, above)
+    part = edge(first_sums, second_sums, upper, a0)
     sums = lax.all_to_all(part, ("img", "gz"), 0, 0, tiled=True)
-    return final(centre, positions, sums, below, lower, upper, above)
+    return final(centre, positions, sums, below, s0, s1, upper, a0, a1)
 
 
 def solution(mesh):
     in_specs = (P("img", None, "gz", None, None), P("img"), P("img"))
     out_specs = P("img", None, "gz", None, None)
-    return jax.shard_map(local, mesh=mesh, in_specs=in_specs, out_specs=out_specs, check_vma=False)
+    return jax.shard_map(
+        local, mesh=mesh, in_specs=in_specs, out_specs=out_specs, check_vma=False
+    )

time: 147 us -> 145 us (0.986)
  blocking collectives: 24 us -> 37.3 us
  local copies, waits for them, and re-layouts: 11 us -> 0.01 us
  Pallas kernels: 19.8 us -> 28.3 us
  starting transfers between devices: 33.7 us -> 25.5 us
  waiting for transfers between devices: 57.9 us -> 52.9 us
    all_to_all x1, blocking collectives: 24 us -> 37.3 us  [local(): u = lax.all_to_all(u, 'gz', 0, 0, tiled=True)]
    unnamed x32 -> x2, local copies, waits for them, and re-layouts: 11 us -> 0.01 us
    ppermute x1, waiting for transfers between devices: 8.84 us -> 0.01 us  [local(): below = lax.ppermute(upper, 'img', rows)]
    ppermute x1 -> x2, waiting for transfers between devices: 2.18 us -> 10.1 us  [the longest x1 9.87 us: local(): a0 = lax.ppermute(s0, 'img', rows_back)]
    all_to_all x1 -> x0, waiting for transfers between devices: 7.35 us -> none  [local(): u1 = lax.all_to_all(u1, 'gz', 0, 0, tiled=True)]
    pallas_call x4, Pallas kernels: 9.6 us -> 15.1 us  [the longest x2 11.8 us: inverse(): pl.pallas_call(functools.partial(inverse_kernel, pair=pair), out_shape=(*...]
    all_to_all x1 -> x0, starting transfers between devices: 4.95 us -> none  [local(): u1 = lax.all_to_all(u1, 'gz', 0, 0, tiled=True)]
    all_to_all x1, waiting for transfers between devices: 4.81 us -> 8.08 us  [local(): sums = lax.all_to_all(part, ('img', 'gz'), 0, 0, tiled=True)]
  transfers between devices with their start and end apart: 5 -> 5, of which waited for: 5 -> 4; matrix products, arithmetic and copies ran while one was open for 0% -> 0% of each run, Pallas kernels for 6% -> 2%
where the time goes in v2:
time: 145 us; the launch traced here: 144 us
  waiting for transfers between devices  52.9 us (36%)
  blocking collectives  37.3 us (26%)
  Pallas kernels  28.3 us (20%)
  starting transfers between devices  25.5 us (18%)
    all_to_all x1, blocking collectives, local(): u = lax.all_to_all(u, 'gz', 0, 0, tiled=True)  37.3 us
    all_to_all x1, waiting for transfers between devices, local(): f = lax.all_to_all(f, 'gz', 0, 0, tiled=True)  34.7 us
    pallas_call x2, Pallas kernels, inverse(): pl.pallas_call(functools.partial(inverse_kernel, pair=pair), out_shape=(*...  11.8 us
    ppermute x1, waiting for transfers between devices, local(): a0 = lax.ppermute(s0, 'img', rows_back)  9.87 us
    all_to_all x1, starting transfers between devices, local(): f = lax.all_to_all(f, 'gz', 0, 0, tiled=True)  9.84 us
    all_to_all x1, waiting for transfers between devices, local(): sums = lax.all_to_all(part, ('img', 'gz'), 0, 0, tiled=True)  8.08 us
    ppermute x1, starting transfers between devices, local(): below = lax.ppermute(upper, 'img', rows)  7.18 us
    pallas_call x1, Pallas kernels, forward(): pl.pallas_call(forward_kernel, out_shape=(jax.ShapeDtypeStruct((GROUPS, 2...  6.94 us
  transfers between devices with their start and end apart: 5, of which 4 were waited for; matrix products, arithmetic and copies ran while one was open for 0% of the time, Pallas kernels for 2%

profile of v2, /device:TPU:1, one launch (start us, length us, event | category | flops | bytes accessed | tf_op | source)
XLA Modules:
  0.0 144.0 jit_solution(17692406673294107495)
XLA Ops:
  0.0 6.9 %forward.1 = (f32[32,2,2,5,8,128]{5,4,3,2,1,0:T(8,128)}, f32[32,2,5,8,128]{4,3,2,1,0:T(8,128)}) custom-call(f32[4,5,2,128,128]{4,3,2,1,0:T(8,128)} %refs_4_.3, bf16[256,256]{1,0:T(8,128)(2,1)} %constant.19.clone.ty, bf16[2,128,384]{2,1,0:T(8,128)(2,1)} %constant.21.clone.tx, f32[32,8,128]{2,1,0:T(8,128)} %constant.23.clone.rho_ref), custom_call_target="tpu_custom_call" | custom-call | flops 3000000000 | bytes 9000000 | tf_op jit(solution)/shard_map/forward/pallas_call | solution.py:349
  6.9 0.0 copy-start
  6.9 9.8 %all-to-all-start = ((f32[32,2,2,5,8,128]{5,4,3,2,1,0:T(8,128)}), f32[32,2,2,5,8,128]{5,4,3,2,1,0:T(8,128)S(1)}, u32[]{:S(2)}, u32[]{:S(2)}) async-start(f32[32,2,2,5,8,128]{5,4,3,2,1,0:T(8,128)} %get-tuple-element.12), calls=%async_computation | async-start | bytes 5242880 | tf_op jit(solution)/shard_map/all_to_all | solution.py:481
  16.8 34.7 %all-to-all-done.f = f32[32,2,2,5,8,128]{5,4,3,2,1,0:T(8,128)S(1)} async-done(((f32[32,2,2,5,8,128]{5,4,3,2,1,0:T(8,128)}), f32[32,2,2,5,8,128]{5,4,3,2,1,0:T(8,128)S(1)}, u32[]{:S(2)}, u32[]{:S(2)}) %all-to-all-start) | async-done | bytes 2621472 | tf_op jit(solution)/shard_map/all_to_all | solution.py:481
  51.5 0.0 copy-done
  51.5 1.1 solve.1
  52.6 37.3 %all_to_all.15.refs_0_ = f32[32,2,2,5,8,128]{5,4,3,2,1,0:T(8,128)} all-to-all(f32[32,2,2,5,8,128]{5,4,3,2,1,0:T(8,128)S(1)} %solve.1), channel_id=1, replica_groups=mesh['img'=4,'gz'=32] {'gz'}, dimensions={0} | all-to-all | bytes 5242880 | tf_op jit(solution)/shard_map/all_to_all | solution.py:483
  89.9 5.8 %inverse.2 = (f32[5,2,128,128]{3,2,1,0:T(8,128)}, f32[5,2,128,128]{3,2,1,0:T(8,128)}, f32[2,8,128]{2,1,0:T(8,128)}) custom-call(f32[32,2,2,5,8,128]{5,4,3,2,1,0:T(8,128)} %all_to_all.15.refs_0_, f32[32,2,5,8,128]{4,3,2,1,0:T(8,128)} %get-tuple-element.13.refs_1_, f32[4,5,2,128,128]{4,3,2,1,0:T(8,128)} %refs_4_.3, f32[4,5,2,128,128]{4,3,2,1,0:T(8,128)} %refs_4_.3, ...), custom_call_target="tpu_custom_call" | custom-call | flops 2000000000 | bytes 6000000 | tf_op jit(solution)/shard_map/inverse/pallas_call | solution.py:428
  95.7 6.1 %inverse.3 = (f32[2,5,2,128,128]{4,3,2,1,0:T(8,128)}, f32[2,8,128]{2,1,0:T(8,128)}) custom-call(f32[32,2,2,5,8,128]{5,4,3,2,1,0:T(8,128)} %all_to_all.15.refs_0_, f32[32,2,5,8,128]{4,3,2,1,0:T(8,128)} %get-tuple-element.13.refs_1_, f32[4,5,2,128,128]{4,3,2,1,0:T(8,128)} %refs_4_.3, f32[4,5,2,128,128]{4,3,2,1,0:T(8,128)} %refs_4_.3, ...), custom_call_target="tpu_custom_call" | custom-call | flops 2000000000 | bytes 6000000 | tf_op jit(solution)/shard_map/inverse/pallas_call | solution.py:428
  101.8 7.2 %collective-permute-start.1 = (f32[2,5,2,128,128]{4,3,2,1,0:T(8,128)}, f32[2,5,2,128,128]{4,3,2,1,0:T(8,128)}, u32[]{:S(2)}, u32[]{:S(2)}) collective-permute-start(f32[2,5,2,128,128]{4,3,2,1,0:T(8,128)} %get-tuple-element.17.upper), channel_id=1, source_target_pairs={{0,32},{32,64},{64,96},{1,33},{33,65},{65,97},{2,34},{34,66},{66,9... | collective-permute-start | bytes 3932168 | tf_op jit(solution)/shard_map/ppermute | solution.py:488
  109.0 1.9 %collective-permute-start = (f32[5,2,128,128]{3,2,1,0:T(8,128)}, f32[5,2,128,128]{3,2,1,0:T(8,128)}, u32[]{:S(2)}, u32[]{:S(2)}) collective-permute-start(f32[5,2,128,128]{3,2,1,0:T(8,128)} %get-tuple-element.18.s0), channel_id=1, source_target_pairs={{32,0},{64,32},{96,64},{33,1},{65,33},{97,65},{34,2},{66,34},{98,6... | collective-permute-start | bytes 1966088 | tf_op jit(solution)/shard_map/ppermute | solution.py:485
  110.9 1.9 %collective-permute-start.2 = (f32[5,2,128,128]{3,2,1,0:T(8,128)}, f32[5,2,128,128]{3,2,1,0:T(8,128)}, u32[]{:S(2)}, u32[]{:S(2)}) collective-permute-start(f32[5,2,128,128]{3,2,1,0:T(8,128)} %get-tuple-element.15.refs_7_.s1), channel_id=1, source_target_pairs={{32,0},{64,32},{96,64},{33,1},{65,33},{97,65},{34,2},{66,34},{98,6... | collective-permute-start | bytes 1966088 | tf_op jit(solution)/shard_map/ppermute | solution.py:486
  112.8 9.9 %collective-permute-done.above.a0 = f32[5,2,128,128]{3,2,1,0:T(8,128)} collective-permute-done((f32[5,2,128,128]{3,2,1,0:T(8,128)}, f32[5,2,128,128]{3,2,1,0:T(8,128)}, u32[]{:S(2)}, u32[]{:S(2)}) %collective-permute-start) | collective-permute-done | bytes 655392 | tf_op jit(solution)/shard_map/ppermute | solution.py:485
  122.7 2.2 %edge.1 = f32[128,1,128]{2,1,0:T(1,128)} custom-call(f32[2,8,128]{2,1,0:T(8,128)} %get-tuple-element.14.first_sums, f32[2,8,128]{2,1,0:T(8,128)} %get-tuple-element.16.second_sums, f32[2,5,2,128,128]{4,3,2,1,0:T(8,128)} %get-tuple-element.17.upper, f32[5,2,128,128]{3,2,1,0:T(8,128)} %collective-permute-done.above.a0), custom_call_target="tpu_custom_call" | custom-call | flops 2000000 | bytes 1300000 | tf_op jit(solution)/shard_map/edge/pallas_call | solution.py:442
  124.9 4.6 %all-to-all-start.2 = ((f32[128,1,128]{2,1,0:T(1,128)}), f32[128,1,128]{2,1,0:T(1,128)}, u32[]{:S(2)}, u32[]{:S(2)}) async-start(f32[128,1,128]{2,1,0:T(1,128)} %edge.1), calls=%async_computation.2 | async-start | bytes 131072 | tf_op jit(solution)/shard_map/all_to_all | solution.py:490
  129.5 0.2 collective-permute-done.2.a1
  129.7 8.1 %all-to-all-done.2.sums = f32[128,1,128]{2,1,0:T(1,128)} async-done(((f32[128,1,128]{2,1,0:T(1,128)}), f32[128,1,128]{2,1,0:T(1,128)}, u32[]{:S(2)}, u32[]{:S(2)}) %all-to-all-start.2) | async-done | bytes 65568 | tf_op jit(solution)/shard_map/all_to_all | solution.py:490
  137.8 0.0 collective-permute-done.1.below
  137.8 6.2 %final.1 = f32[4,5,2,128,128]{4,3,2,1,0:T(8,128)} custom-call(s32[4]{0:T(128)} %centre.1, f32[4]{0:T(128)} %positions.1, s32[1]{0:T(128)} %bitcast.where, f32[128,1,128]{2,1,0:T(1,128)} %all-to-all-done.2.sums, f32[2,5,2,128,128]{4,3,2,1,0:T(8,128)} %collective-permute-done.1.below, f32[5,2,128,128]{3,2,1,0:T(8,128)} %get-tuple-element.18.s0, ...), custom_call_target="tpu_custom_call" | custom-call | flops 30000000 | bytes 8000000 | tf_op jit(solution)/shard_map/final/pallas_call | solution.py:463
Async XLA Ops:
  6.9 44.6 %copy-start = (f32[32,8,128]{2,1,0:T(8,128)S(1)}, f32[32,8,128]{2,1,0:T(8,128)}, u32[]{:S(2)}) copy-start(f32[32,8,128]{2,1,0:T(8,128)} %constant.23.clone.rho_ref) | copy-start | bytes 393220
  6.9 44.6 %all-to-all-start = ((f32[32,2,2,5,8,128]{5,4,3,2,1,0:T(8,128)}), f32[32,2,2,5,8,128]{5,4,3,2,1,0:T(8,128)S(1)}, u32[]{:S(2)}, u32[]{:S(2)}) async-start(f32[32,2,2,5,8,128]{5,4,3,2,1,0:T(8,128)} %get-tuple-element.12), calls=%async_computation | async-start | bytes 5242880 | tf_op jit(solution)/shard_map/all_to_all | solution.py:481
  101.8 36.0 %collective-permute-start.1 = (f32[2,5,2,128,128]{4,3,2,1,0:T(8,128)}, f32[2,5,2,128,128]{4,3,2,1,0:T(8,128)}, u32[]{:S(2)}, u32[]{:S(2)}) collective-permute-start(f32[2,5,2,128,128]{4,3,2,1,0:T(8,128)} %get-tuple-element.17.upper), channel_id=1, source_target_pairs={{0,32},{32,64},{64,96},{1,33},{33,65},{65,97},{2,34},{34,66},{66,9... | collective-permute-start | bytes 3932168 | tf_op jit(solution)/shard_map/ppermute | solution.py:488
  109.0 13.7 %collective-permute-start = (f32[5,2,128,128]{3,2,1,0:T(8,128)}, f32[5,2,128,128]{3,2,1,0:T(8,128)}, u32[]{:S(2)}, u32[]{:S(2)}) collective-permute-start(f32[5,2,128,128]{3,2,1,0:T(8,128)} %get-tuple-element.18.s0), channel_id=1, source_target_pairs={{32,0},{64,32},{96,64},{33,1},{65,33},{97,65},{34,2},{66,34},{98,6... | collective-permute-start | bytes 1966088 | tf_op jit(solution)/shard_map/ppermute | solution.py:485
  110.9 18.8 %collective-permute-start.2 = (f32[5,2,128,128]{3,2,1,0:T(8,128)}, f32[5,2,128,128]{3,2,1,0:T(8,128)}, u32[]{:S(2)}, u32[]{:S(2)}) collective-permute-start(f32[5,2,128,128]{3,2,1,0:T(8,128)} %get-tuple-element.15.refs_7_.s1), channel_id=1, source_target_pairs={{32,0},{64,32},{96,64},{33,1},{65,33},{97,65},{34,2},{66,34},{98,6... | collective-permute-start | bytes 1966088 | tf_op jit(solution)/shard_map/ppermute | solution.py:486
  124.9 12.9 %all-to-all-start.2 = ((f32[128,1,128]{2,1,0:T(1,128)}), f32[128,1,128]{2,1,0:T(1,128)}, u32[]{:S(2)}, u32[]{:S(2)}) async-start(f32[128,1,128]{2,1,0:T(1,128)} %edge.1), calls=%async_computation.2 | async-start | bytes 131072 | tf_op jit(solution)/shard_map/all_to_all | solution.py:490

commit v3 on v2

--- a/solution.py
+++ b/solution.py
@@ -19,10 +19,10 @@
 EPS = 1e-6
 KEEP = 1.0 - 1.0 / SMOOTH
 FORWARD_MIB = 60
-SOLVE_MIB = 32
-INVERSE_MIB = 64
-EDGE_MIB = 64
-FINAL_MIB = 64
+SOLVE_MIB = 16
+INVERSE_MIB = 8
+EDGE_MIB = 4
+FINAL_MIB = 16
 F32 = jnp.float32
 BF16 = jnp.bfloat16
 
@@ -171,7 +171,7 @@
             y = tile(c, 0)
             out[rows, 0, 0, c] = beta * tile(c, 1) + y
             out[rows, 1, 0, c] = y + g[c]
-            keep[rows, 0, c] = back * y
+            keep[0, c, rows] = back * y
 
 
 def solve_kernel(where, f, rho_ref, out, right, work):
@@ -206,7 +206,7 @@
     back = jnp.broadcast_to((1.0 / SMOOTH) / (rho + 1.0 / rho), shape)
 
     def put(s, slot, value):
-        out[s, slot] = value
+        out[s, :, :, slot] = value
 
     def down(n, carry):
         u, after = carry
@@ -229,50 +229,50 @@
 
 
 def inverse_kernel(*refs, pair):
-    spec, keep, img, mix, minus, ty, tx = refs[:7]
+    spec, keep, img, ty, tx = refs[:5]
     stack = refs[-1]
     if pair == 0:
-        out, sums = refs[7:9], refs[9]
+        out, sums = refs[5:7], refs[7]
     else:
-        lower, upper, sums = refs[7:10]
+        lower, upper, sums = refs[5:8]
         out = [upper.at[0], upper.at[1]]
-    c = pl.program_id(0)
-    weight = jnp.where(c == 0, 0.5, jnp.where(c == 3, -0.5, jnp.where(c == 2, 0.25, -0.25)))
-    weight = weight * (1.0 / SMOOTH)
-    other = jnp.where(c == 1, 0.25 / SMOOTH, 0.0)
     first = lax.broadcasted_iota(jnp.int32, (16, 8, 128), 1) < 4
-
-    @pl.when(c == 0)
-    def _():
-        sums[...] = jnp.zeros_like(sums)
-
-    planes = []
-    for i in range(2):
-        p_even, p_odd = spec[0:16, 0, 0, 0], spec[16:32, 0, 0, 0]
-        w_even = spec[0:16, 1, 0, 0] + keep[0:16, 0, 0]
-        w_odd = spec[16:32, 1, 0, 0] + keep[16:32, 0, 0]
-        if i == 1:
-            p_even, p_odd, w_even, w_odd = p_odd, p_even, w_odd, w_even
-        push(stack, i, 0, jnp.where(first, w_even, w_odd).reshape(128, 128))
-        push(stack, i, 1, jnp.where(first, p_even, p_odd).reshape(128, 128))
-        both = jnp.dot(tx[i], stack[i], preferred_element_type=F32)
-        even = KEEP * img[i, 0, 0] + times_right(both[:, :128], ty[...])
-        odd = times_right(both[:, 128:], ty[...])
-        odd = KEEP * img[i, 0, 1] + odd * (1.0 / SMOOTH)
-        odd = odd + (weight * mix[i, 0, 0] + other * minus[i, 0, 0])
-        out[i][0, 0] = even
-        out[i][0, 1] = odd
-        planes.append((even, odd))
-    sums[0] += fold(planes[1][0] - planes[0][0]) + fold(planes[1][1] - planes[0][1])
-    if pair == 1:
-        sums[1] += fold(planes[0][0] - lower[0, 0]) + fold(planes[0][1] - lower[0, 1])
+    sums[...] = jnp.zeros_like(sums)
+
+    @pl.loop(0, 5)
+    def _(c):
+        weight = jnp.where(c == 0, 0.5, jnp.where(c == 3, -0.5, jnp.where(c == 2, 0.25, -0.25)))
+        weight = weight * (1.0 / SMOOTH)
+        other = jnp.where(c == 1, 0.25 / SMOOTH, 0.0)
+        source = jnp.where(c == 1, 0, jnp.where(c == 2, 4, jnp.where(c == 4, 2, 1)))
+        planes = []
+        for i in range(2):
+            image = 2 * pair + i
+            p_even, p_odd = spec[0:16, pair, c, 0], spec[16:32, pair, c, 0]
+            w_even = spec[0:16, pair, c, 1] + keep[pair, c, 0:16]
+            w_odd = spec[16:32, pair, c, 1] + keep[pair, c, 16:32]
+            if i == 1:
+                p_even, p_odd, w_even, w_odd = p_odd, p_even, w_odd, w_even
+            push(stack, i, 0, jnp.where(first, w_even, w_odd).reshape(128, 128))
+            push(stack, i, 1, jnp.where(first, p_even, p_odd).reshape(128, 128))
+            both = jnp.dot(tx[i], stack[i], preferred_element_type=F32)
+            even = KEEP * img[image, c, 0] + times_right(both[:, :128], ty[...])
+            odd = times_right(both[:, 128:], ty[...])
+            odd = KEEP * img[image, c, 1] + odd * (1.0 / SMOOTH)
+            odd = odd + (weight * img[image, source, 1] + other * img[image, 3, 1])
+            out[i][c, 0] = even
+            out[i][c, 1] = odd
+            planes.append((even, odd))
+        sums[0] += fold(planes[1][0] - planes[0][0]) + fold(planes[1][1] - planes[0][1])
+        if pair == 1:
+            sums[1] += fold(planes[0][0] - lower[c, 0]) + fold(planes[0][1] - lower[c, 1])
 
 
 def edge_kernel(first_sums, second_sums, upper, above, out):
     edge = jnp.zeros((8, 128), F32)
     for c in range(5):
         for zz in range(2):
-            edge = edge + fold(above[c, zz] - upper[0, c, zz])
+            edge = edge + fold(above[c, zz] - upper[1, c, zz])
     rows = [first_sums[0], second_sums[1], second_sums[0], edge]
     index = lax.broadcasted_iota(jnp.int32, (1, 128), 1)
     total = jnp.zeros((1, 128), F32)
@@ -319,8 +319,9 @@
                     value = jnp.where(c - 1 + n == spot, w[n], value)
                 weights[m, r] = value
 
-    pieces = [below[0], below[1], s0, s1, upper[0], upper[1], a0, a1]
-    pieces = [p[...].reshape(32, 8, 128) for p in pieces]
+    c = pl.program_id(0)
+    pieces = [below[0, 0], below[1, 0], s0[c], s1[c], upper[0, c], upper[1, c], a0[c], a1[0]]
+    pieces = [p.reshape(32, 8, 128) for p in pieces]
     for m in range(LOCAL):
         acc = pieces[m] * weights[m, 0][None]
         for r in range(1, 5):
@@ -333,6 +334,11 @@
 
 
 SMEM = pl.BlockSpec(memory_space=pltpu.SMEM)
+VMEM = pl.BlockSpec(memory_space=pltpu.VMEM)
+
+
+def plain(mib):
+    return pltpu.CompilerParams(vmem_limit_bytes=mib * 1024 * 1024)
 
 
 def params(mib):
@@ -350,7 +356,7 @@
         forward_kernel,
         out_shape=(
             jax.ShapeDtypeStruct((GROUPS, 2, 2, 5, 8, 128), F32),
-            jax.ShapeDtypeStruct((GROUPS, 2, 5, 8, 128), F32),
+            jax.ShapeDtypeStruct((2, 5, GROUPS, 8, 128), F32),
         ),
         grid=(2,),
         in_specs=[
@@ -361,7 +367,7 @@
         ],
         out_specs=(
             pl.BlockSpec((GROUPS, 2, 1, 5, 8, 128), lambda p: (0, 0, p, 0, 0, 0)),
-            pl.BlockSpec((GROUPS, 1, 5, 8, 128), lambda p: (0, p, 0, 0, 0)),
+            pl.BlockSpec((1, 5, GROUPS, 8, 128), lambda p: (p, 0, 0, 0, 0)),
         ),
         scratch_shapes=[
             pltpu.VMEM((7, 384, 256), BF16),
@@ -375,18 +381,18 @@
 
 def solve(f, rho):
     where = lax.axis_index("gz").astype(jnp.int32).reshape(1)
-    shape = (GROUPS, 2, 2, 5, 8, 128)
+    result = (GROUPS, 2, 5, 2, 8, 128)
     return pl.pallas_call(
         solve_kernel,
-        out_shape=jax.ShapeDtypeStruct(shape, F32),
+        out_shape=pltpu.VMEM(result, F32),
         grid_spec=pltpu.PrefetchScalarGridSpec(
             num_scalar_prefetch=1,
             grid=(1,),
             in_specs=[
-                whole(shape),
+                VMEM,
                 pl.BlockSpec((1, 8, 128), lambda i, w: (w[0], 0, 0)),
             ],
-            out_specs=whole(shape),
+            out_specs=VMEM,
             scratch_shapes=[
                 pltpu.VMEM((GROUPS, 2, 5, 8, 128), F32),
                 pltpu.VMEM((GROUPS, 2, 5, 8, 128), F32),
@@ -398,60 +404,33 @@
     )(where, f, rho)
 
 
-def mix_index(pair):
-    def index(c):
-        source = jnp.where(c == 1, 0, jnp.where(c == 2, 4, jnp.where(c == 4, 2, 1)))
-        return pair, source, 1, 0, 0
-
-    return index
-
-
 def inverse(spec, keep, images, pair, ty, tx, *lower):
-    single = pl.BlockSpec((None, 2, 128, 128), lambda c: (c, 0, 0, 0))
-    flat = jax.ShapeDtypeStruct((5, 2, 128, 128), F32)
-    specs = [
-        pl.BlockSpec((GROUPS, 2, 1, 1, 8, 128), lambda c: (0, 0, pair, c, 0, 0)),
-        pl.BlockSpec((GROUPS, 1, 1, 8, 128), lambda c: (0, pair, c, 0, 0)),
-        pl.BlockSpec((2, 1, 2, 128, 128), lambda c: (pair, c, 0, 0, 0)),
-        pl.BlockSpec((2, 1, 1, 128, 128), mix_index(pair)),
-        pl.BlockSpec((2, 1, 1, 128, 128), lambda c: (pair, 3, 1, 0, 0)),
-        whole((256, 256)),
-        whole((2, 128, 384)),
-    ]
     if pair == 1:
-        specs.append(pl.BlockSpec((1, 2, 128, 128), lambda c: (c, 0, 0, 0)))
-        out_shape = (jax.ShapeDtypeStruct((2, 5, 2, 128, 128), F32),)
-        out_specs = (pl.BlockSpec((2, 1, 2, 128, 128), lambda c: (0, c, 0, 0, 0)),)
+        out_shape = (pltpu.VMEM((2, 5, 2, 128, 128), F32),)
     else:
-        out_shape = (flat, flat)
-        out_specs = (pl.BlockSpec((1, 2, 128, 128), lambda c: (c, 0, 0, 0)),) * 2
+        out_shape = (pltpu.VMEM((5, 2, 128, 128), F32),) * 2
+    out_shape = (*out_shape, pltpu.VMEM((2, 8, 128), F32))
+    args = (spec, keep, images, ty, tx, *lower)
     return pl.pallas_call(
         functools.partial(inverse_kernel, pair=pair),
-        out_shape=(*out_shape, jax.ShapeDtypeStruct((2, 8, 128), F32)),
-        grid=(5,),
-        in_specs=specs,
-        out_specs=(*out_specs, whole((2, 8, 128))),
+        out_shape=out_shape,
+        in_specs=[VMEM] * len(args),
+        out_specs=(VMEM,) * len(out_shape),
         scratch_shapes=[pltpu.VMEM((2, 384, 256), BF16)],
-        compiler_params=params(INVERSE_MIB),
-        cost_estimate=cost(2000000000, 6000000),
+        compiler_params=plain(INVERSE_MIB),
+        cost_estimate=cost(2_000_000_000, 6_000_000),
         name="inverse",
-    )(spec, keep, images, images, images, ty, tx, *lower)
+    )(*args)
 
 
 def edge(first_sums, second_sums, upper, above):
     return pl.pallas_call(
         edge_kernel,
         out_shape=jax.ShapeDtypeStruct((128, 1, 128), F32),
-        grid=(1,),
-        in_specs=[
-            whole((2, 8, 128)),
-            whole((2, 8, 128)),
-            pl.BlockSpec((1, 5, 2, 128, 128), lambda p: (1, 0, 0, 0, 0)),
-            whole((5, 2, 128, 128)),
-        ],
-        out_specs=whole((128, 1, 128)),
-        compiler_params=params(EDGE_MIB),
-        cost_estimate=cost(2000000, 1300000),
+        in_specs=[VMEM] * 4,
+        out_specs=VMEM,
+        compiler_params=plain(EDGE_MIB),
+        cost_estimate=cost(2_000_000, 1_300_000),
         name="edge",
     )(first_sums, second_sums, upper, above)
 
@@ -464,7 +443,7 @@
         final_kernel,
         out_shape=jax.ShapeDtypeStruct((4, 5, 2, 128, 128), F32),
         grid=(5,),
-        in_specs=[SMEM, SMEM, SMEM, whole((128, 1, 128)), pair, one, one, pair, one, one],
+        in_specs=[SMEM, SMEM, SMEM, VMEM, pair, VMEM, VMEM, VMEM, VMEM, one],
         out_specs=pl.BlockSpec((4, 1, 2, 128, 128), lambda c: (0, c, 0, 0, 0)),
         scratch_shapes=[pltpu.VMEM((4, 5, 8, 128), F32)],
         compiler_params=params(FINAL_MIB),

time: 145 us -> 135 us (0.931)
  Pallas kernels: 28.3 us -> 19.1 us
    pallas_call x3, Pallas kernels: 12.9 us -> 5.92 us  [the longest x2 4.81 us: inverse(): pl.pallas_call(functools.partial(inverse_kernel, pair=pair), out_shape=ou...]
    ppermute x1, waiting for transfers between devices: 0.23 us -> 2.82 us  [local(): a1 = lax.ppermute(s1, 'img', rows_back)]
    all_to_all x1, waiting for transfers between devices: 8.08 us -> 6.26 us  [local(): sums = lax.all_to_all(part, ('img', 'gz'), 0, 0, tiled=True)]
  transfers between devices with their start and end apart: 5 -> 5, of which waited for: 4 -> 4; matrix products, arithmetic and copies ran while one was open for 0% -> 0% of each run, Pallas kernels for 2% -> 1%
where the time goes in v3:
time: 135 us; the launch traced here: 134 us
  waiting for transfers between devices  53.4 us (40%)
  blocking collectives  37.5 us (28%)
  starting transfers between devices  24.4 us (18%)
  Pallas kernels  19.1 us (14%)
    all_to_all x1, blocking collectives, local(): u = lax.all_to_all(u, 'gz', 0, 0, tiled=True)  37.5 us
    all_to_all x1, waiting for transfers between devices, local(): f = lax.all_to_all(f, 'gz', 0, 0, tiled=True)  34.7 us
    all_to_all x1, starting transfers between devices, local(): f = lax.all_to_all(f, 'gz', 0, 0, tiled=True)  9.85 us
    ppermute x1, waiting for transfers between devices, local(): a0 = lax.ppermute(s0, 'img', rows_back)  9.55 us
    ppermute x1, starting transfers between devices, local(): below = lax.ppermute(upper, 'img', rows)  7.18 us
    pallas_call x1, Pallas kernels, forward(): pl.pallas_call(forward_kernel, out_shape=(jax.ShapeDtypeStruct((GROUPS, 2...  6.94 us
    all_to_all x1, waiting for transfers between devices, local(): sums = lax.all_to_all(part, ('img', 'gz'), 0, 0, tiled=True)  6.26 us
    pallas_call x1, Pallas kernels, final(): pl.pallas_call(final_kernel, out_shape=jax.ShapeDtypeStruct((4, 5, 2, 128...  5.33 us
  transfers between devices with their start and end apart: 5, of which 4 were waited for; matrix products, arithmetic and copies ran while one was open for 0% of the time, Pallas kernels for 1%

profile of v3, /device:TPU:1, one launch (start us, length us, event | category | flops | bytes accessed | tf_op | source)
XLA Modules:
  0.0 134.5 jit_solution(1085343662095383648)
XLA Ops:
  0.0 6.9 %forward.1 = (f32[32,2,2,5,8,128]{5,4,3,2,1,0:T(8,128)}, f32[2,5,32,8,128]{4,3,2,1,0:T(8,128)}) custom-call(f32[4,5,2,128,128]{4,3,2,1,0:T(8,128)} %refs_2_.3, bf16[256,256]{1,0:T(8,128)(2,1)} %constant.19.clone.ty, bf16[2,128,384]{2,1,0:T(8,128)(2,1)} %constant.21.clone.tx, f32[32,8,128]{2,1,0:T(8,128)} %constant.23.clone.rho_ref), custom_call_target="tpu_custom_call" | custom-call | flops 3000000000 | bytes 9000000 | tf_op jit(solution)/shard_map/forward/pallas_call | solution.py:355
  6.9 9.8 %all-to-all-start = ((f32[32,2,2,5,8,128]{5,4,3,2,1,0:T(8,128)}), f32[32,2,2,5,8,128]{5,4,3,2,1,0:T(8,128)S(1)}, u32[]{:S(2)}, u32[]{:S(2)}) async-start(f32[32,2,2,5,8,128]{5,4,3,2,1,0:T(8,128)} %get-tuple-element.12), calls=%async_computation | async-start | bytes 5242880 | tf_op jit(solution)/shard_map/all_to_all | solution.py:460
  16.8 34.7 %all-to-all-done.f = f32[32,2,2,5,8,128]{5,4,3,2,1,0:T(8,128)S(1)} async-done(((f32[32,2,2,5,8,128]{5,4,3,2,1,0:T(8,128)}), f32[32,2,2,5,8,128]{5,4,3,2,1,0:T(8,128)S(1)}, u32[]{:S(2)}, u32[]{:S(2)}) %all-to-all-start) | async-done | bytes 2621472 | tf_op jit(solution)/shard_map/all_to_all | solution.py:460
  51.5 0.0 copy-done.4
  51.5 1.1 solve.1
  52.6 0.0 copy-start
  52.6 0.0 copy-start.1
  52.7 0.0 copy-start.2
  52.7 0.0 copy-start.3
  52.7 37.5 %all_to_all.15.refs_0_ = f32[32,2,5,2,8,128]{5,4,3,2,1,0:T(8,128)S(1)} all-to-all(f32[32,2,5,2,8,128]{5,4,3,2,1,0:T(8,128)S(1)} %solve.1), channel_id=1, replica_groups=mesh['img'=4,'gz'=32] {'gz'}, dimensions={0} | all-to-all | bytes 5242880 | tf_op jit(solution)/shard_map/all_to_all | solution.py:462
  90.2 2.4 %inverse.2 = (f32[5,2,128,128]{3,2,1,0:T(8,128)S(1)}, f32[5,2,128,128]{3,2,1,0:T(8,128)S(1)}, f32[2,8,128]{2,1,0:T(8,128)S(1)}) custom-call(f32[32,2,5,2,8,128]{5,4,3,2,1,0:T(8,128)S(1)} %all_to_all.15.refs_0_, f32[2,5,32,8,128]{4,3,2,1,0:T(8,128)S(1)} %copy-done.1, f32[4,5,2,128,128]{4,3,2,1,0:T(8,128)S(1)} %copy-done, bf16[256,256]{1,0:T(8,128)(2,1)S(1)} %copy-done.3, ...), custom_call_target="tpu_custom_call" | custom-call | flops 2000000000 | bytes 6000000 | tf_op jit(solution)/shard_map/inverse/pallas_call | solution.py:414
  92.6 0.0 copy-start.5
  92.6 0.0 copy-start.6
  92.6 2.4 %inverse.3 = (f32[2,5,2,128,128]{4,3,2,1,0:T(8,128)S(1)}, f32[2,8,128]{2,1,0:T(8,128)S(1)}) custom-call(f32[32,2,5,2,8,128]{5,4,3,2,1,0:T(8,128)S(1)} %all_to_all.15.refs_0_, f32[2,5,32,8,128]{4,3,2,1,0:T(8,128)S(1)} %copy-done.1, f32[4,5,2,128,128]{4,3,2,1,0:T(8,128)S(1)} %copy-done, bf16[256,256]{1,0:T(8,128)(2,1)S(1)} %copy-done.3, ...), custom_call_target="tpu_custom_call" | custom-call | flops 2000000000 | bytes 6000000 | tf_op jit(solution)/shard_map/inverse/pallas_call | solution.py:414
  95.0 7.2 %collective-permute-start.1 = (f32[2,5,2,128,128]{4,3,2,1,0:T(8,128)S(1)}, f32[2,5,2,128,128]{4,3,2,1,0:T(8,128)}, u32[]{:S(2)}, u32[]{:S(2)}) collective-permute-start(f32[2,5,2,128,128]{4,3,2,1,0:T(8,128)S(1)} %get-tuple-element.17.upper), channel_id=1, source_target_pairs={{0,32},{32,64},{64,96},{1,33},{33,65},{65,97},{2,34},{34,66},{66,9... | collective-permute-start | bytes 3932168 | tf_op jit(solution)/shard_map/ppermute | solution.py:467
  102.2 1.9 %collective-permute-start = (f32[5,2,128,128]{3,2,1,0:T(8,128)S(1)}, f32[5,2,128,128]{3,2,1,0:T(8,128)S(1)}, u32[]{:S(2)}, u32[]{:S(2)}) collective-permute-start(f32[5,2,128,128]{3,2,1,0:T(8,128)S(1)} %get-tuple-element.18.s0), channel_id=1, source_target_pairs={{32,0},{64,32},{96,64},{33,1},{65,33},{97,65},{34,2},{66,34},{98,6... | collective-permute-start | bytes 1966088 | tf_op jit(solution)/shard_map/ppermute | solution.py:464
  104.2 1.9 %collective-permute-start.2 = (f32[5,2,128,128]{3,2,1,0:T(8,128)S(1)}, f32[5,2,128,128]{3,2,1,0:T(8,128)}, u32[]{:S(2)}, u32[]{:S(2)}) collective-permute-start(f32[5,2,128,128]{3,2,1,0:T(8,128)S(1)} %get-tuple-element.15.refs_5_.s1), channel_id=1, source_target_pairs={{32,0},{64,32},{96,64},{33,1},{65,33},{97,65},{34,2},{66,34},{98,6... | collective-permute-start | bytes 1966088 | tf_op jit(solution)/shard_map/ppermute | solution.py:465
  106.1 9.6 %collective-permute-done.above.a0 = f32[5,2,128,128]{3,2,1,0:T(8,128)S(1)} collective-permute-done((f32[5,2,128,128]{3,2,1,0:T(8,128)S(1)}, f32[5,2,128,128]{3,2,1,0:T(8,128)S(1)}, u32[]{:S(2)}, u32[]{:S(2)}) %collective-permute-start) | collective-permute-done | bytes 655392 | tf_op jit(solution)/shard_map/ppermute | solution.py:464
  115.6 0.9 edge.1
  116.5 3.5 %all-to-all-start.2 = ((f32[128,1,128]{2,1,0:T(1,128)}), f32[128,1,128]{2,1,0:T(1,128)S(1)}, u32[]{:S(2)}, u32[]{:S(2)}) async-start(f32[128,1,128]{2,1,0:T(1,128)} %edge.1), calls=%async_computation.2 | async-start | bytes 131072 | tf_op jit(solution)/shard_map/all_to_all | solution.py:469
  120.1 2.8 %collective-permute-done.2.a1 = f32[5,2,128,128]{3,2,1,0:T(8,128)} collective-permute-done((f32[5,2,128,128]{3,2,1,0:T(8,128)S(1)}, f32[5,2,128,128]{3,2,1,0:T(8,128)}, u32[]{:S(2)}, u32[]{:S(2)}) %collective-permute-start.2) | collective-permute-done | bytes 655392 | tf_op jit(solution)/shard_map/ppermute | solution.py:465
  122.9 6.3 %all-to-all-done.2.sums = f32[128,1,128]{2,1,0:T(1,128)S(1)} async-done(((f32[128,1,128]{2,1,0:T(1,128)}), f32[128,1,128]{2,1,0:T(1,128)S(1)}, u32[]{:S(2)}, u32[]{:S(2)}) %all-to-all-start.2) | async-done | bytes 65568 | tf_op jit(solution)/shard_map/all_to_all | solution.py:469
  129.1 0.0 collective-permute-done.1.below
  129.2 5.3 %final.1 = f32[4,5,2,128,128]{4,3,2,1,0:T(8,128)} custom-call(s32[4]{0:T(128)S(1)} %copy-done.5, f32[4]{0:T(128)S(1)} %copy-done.6, s32[1]{0:T(128)} %bitcast.where, f32[128,1,128]{2,1,0:T(1,128)S(1)} %all-to-all-done.2.sums, f32[2,5,2,128,128]{4,3,2,1,0:T(8,128)} %collective-permute-done.1.below, f32[5,2,128,128]{3,2,1,0:T(8,128)S(1)} %get-tuple-element.18.s0, ...), custom_call_target="tpu_custom_call" | custom-call | flops 30000000 | bytes 8000000 | tf_op jit(solution)/shard_map/final/pallas_call | solution.py:442
  (7 shorter events, 0.0 us)
Async XLA Ops:
  6.9 44.6 %copy-start.4 = (f32[32,8,128]{2,1,0:T(8,128)S(1)}, f32[32,8,128]{2,1,0:T(8,128)}, u32[]{:S(2)}) copy-start(f32[32,8,128]{2,1,0:T(8,128)} %constant.23.clone.rho_ref) | copy-start | bytes 393220
  6.9 44.6 %all-to-all-start = ((f32[32,2,2,5,8,128]{5,4,3,2,1,0:T(8,128)}), f32[32,2,2,5,8,128]{5,4,3,2,1,0:T(8,128)S(1)}, u32[]{:S(2)}, u32[]{:S(2)}) async-start(f32[32,2,2,5,8,128]{5,4,3,2,1,0:T(8,128)} %get-tuple-element.12), calls=%async_computation | async-start | bytes 5242880 | tf_op jit(solution)/shard_map/all_to_all | solution.py:460
  52.6 37.5 %copy-start = (f32[4,5,2,128,128]{4,3,2,1,0:T(8,128)S(1)}, f32[4,5,2,128,128]{4,3,2,1,0:T(8,128)}, u32[]{:S(2)}) copy-start(f32[4,5,2,128,128]{4,3,2,1,0:T(8,128)} %refs_2_.3) | copy-start | bytes 7864324
  52.6 37.5 %copy-start.1 = (f32[2,5,32,8,128]{4,3,2,1,0:T(8,128)S(1)}, f32[2,5,32,8,128]{4,3,2,1,0:T(8,128)}, u32[]{:S(2)}) copy-start(f32[2,5,32,8,128]{4,3,2,1,0:T(8,128)} %get-tuple-element.13.refs_1_) | copy-start | bytes 3932164
  52.7 37.5 %copy-start.2 = (bf16[2,128,384]{2,1,0:T(8,128)(2,1)S(1)}, bf16[2,128,384]{2,1,0:T(8,128)(2,1)}, u32[]{:S(2)}) copy-start(bf16[2,128,384]{2,1,0:T(8,128)(2,1)} %constant.22.clone.refs_4_) | copy-start | bytes 589828
  52.7 37.5 %copy-start.3 = (bf16[256,256]{1,0:T(8,128)(2,1)S(1)}, bf16[256,256]{1,0:T(8,128)(2,1)}, u32[]{:S(2)}) copy-start(bf16[256,256]{1,0:T(8,128)(2,1)} %constant.20.clone.refs_3_) | copy-start | bytes 393220
  92.6 36.5 %copy-start.5 = (s32[4]{0:T(128)S(1)}, s32[4]{0:T(128)}, u32[]{:S(2)}) copy-start(s32[4]{0:T(128)} %centre.1) | copy-start | bytes 52
  92.6 36.5 %copy-start.6 = (f32[4]{0:T(128)S(1)}, f32[4]{0:T(128)}, u32[]{:S(2)}) copy-start(f32[4]{0:T(128)} %positions.1) | copy-start | bytes 52
  95.0 34.1 %collective-permute-start.1 = (f32[2,5,2,128,128]{4,3,2,1,0:T(8,128)S(1)}, f32[2,5,2,128,128]{4,3,2,1,0:T(8,128)}, u32[]{:S(2)}, u32[]{:S(2)}) collective-permute-start(f32[2,5,2,128,128]{4,3,2,1,0:T(8,128)S(1)} %get-tuple-element.17.upper), channel_id=1, source_target_pairs={{0,32},{32,64},{64,96},{1,33},{33,65},{65,97},{2,34},{34,66},{66,9... | collective-permute-start | bytes 3932168 | tf_op jit(solution)/shard_map/ppermute | solution.py:467
  102.2 13.4 %collective-permute-start = (f32[5,2,128,128]{3,2,1,0:T(8,128)S(1)}, f32[5,2,128,128]{3,2,1,0:T(8,128)S(1)}, u32[]{:S(2)}, u32[]{:S(2)}) collective-permute-start(f32[5,2,128,128]{3,2,1,0:T(8,128)S(1)} %get-tuple-element.18.s0), channel_id=1, source_target_pairs={{32,0},{64,32},{96,64},{33,1},{65,33},{97,65},{34,2},{66,34},{98,6... | collective-permute-start | bytes 1966088 | tf_op jit(solution)/shard_map/ppermute | solution.py:464
  104.2 18.7 %collective-permute-start.2 = (f32[5,2,128,128]{3,2,1,0:T(8,128)S(1)}, f32[5,2,128,128]{3,2,1,0:T(8,128)}, u32[]{:S(2)}, u32[]{:S(2)}) collective-permute-start(f32[5,2,128,128]{3,2,1,0:T(8,128)S(1)} %get-tuple-element.15.refs_5_.s1), channel_id=1, source_target_pairs={{32,0},{64,32},{96,64},{33,1},{65,33},{97,65},{34,2},{66,34},{98,6... | collective-permute-start | bytes 1966088 | tf_op jit(solution)/shard_map/ppermute | solution.py:465
  116.5 12.6 %all-to-all-start.2 = ((f32[128,1,128]{2,1,0:T(1,128)}), f32[128,1,128]{2,1,0:T(1,128)S(1)}, u32[]{:S(2)}, u32[]{:S(2)}) async-start(f32[128,1,128]{2,1,0:T(1,128)} %edge.1), calls=%async_computation.2 | async-start | bytes 131072 | tf_op jit(solution)/shard_map/all_to_all | solution.py:469

commit v4 on v3

--- a/solution.py
+++ b/solution.py
@@ -88,46 +88,59 @@
     return both[:, :128] + both[:, 128:]
 
 
-def dx(f):
-    return (pltpu.roll(f, NX - 1, 0) - pltpu.roll(f, 1, 0)) * 0.5
-
-
-def dy(f):
-    return (pltpu.roll(f, NY - 1, 1) - pltpu.roll(f, 1, 1)) * 0.5
+def shifts(f, axis):
+    size = NX if axis == 0 else NY
+    return pltpu.roll(f, size - 1, axis), pltpu.roll(f, 1, axis)
 
 
 def local_drive(q):
     q1, q2, q3, q4, q5 = q
-    qz = -(q1 + q4)
-    s11 = q1 * q1 + q2 * q2 + q3 * q3
-    s12 = q1 * q2 + q2 * q4 + q3 * q5
-    s13 = q1 * q3 + q2 * q5 + q3 * qz
-    s22 = q2 * q2 + q4 * q4 + q5 * q5
-    s23 = q2 * q3 + q4 * q5 + q5 * qz
-    s33 = q3 * q3 + q5 * q5 + qz * qz
-    trace = s11 + s22 + s33
-    scale = (0.2 + 1.0 / SMOOTH) - 0.1 * trace
-    third = trace * (1.0 / 3.0)
-    f1 = scale * q1 + 0.5 * (s11 - third) - dy(q3)
-    f2 = scale * q2 + 0.5 * s12 - 0.5 * (dy(q5) - dx(q3))
-    f3 = scale * q3 + 0.5 * s13 - 0.5 * (dx(q2) + dy(qz - q1))
-    f4 = scale * q4 + 0.5 * (s22 - third) + dx(q5)
-    f5 = scale * q5 + 0.5 * s23 - 0.5 * (dx(q4 - qz) - dy(q2))
-    return f1, f2, f3, f4, f5
+    both = q1 + q4
+    s11 = q1 * q1 + (q2 * q2 + q3 * q3)
+    d = q2 * q2
+    s22 = q4 * q4 + (d + q5 * q5)
+    half_trace = (s11 + s22) + (q1 * q4 - d)
+    scale = (0.2 + 1.0 / SMOOTH) - 0.2 * half_trace
+    third = half_trace * (1.0 / 3.0)
+    h2, h3 = 0.5 * q2, 0.5 * q3
+    rolled = {}
+    for name, f in (("2", q2), ("3", q3), ("5", q5)):
+        for axis in range(2):
+            rolled[name, axis] = shifts(f, axis)
+
+    def step(name, axis):
+        after, before = rolled[name, axis]
+        return after - before
+
+    after, before = shifts(both + q1, 1)
+    step_y = after - before
+    after, before = shifts(both + q4, 0)
+    step_x = after - before
+    f1 = scale * q1 + (0.5 * (s11 - step("3", 1)) - third)
+    f2 = q2 * (scale + 0.5 * both) + h3 * q5 + 0.25 * (step("3", 0) - step("5", 1))
+    f3 = q3 * (scale - 0.5 * q4) + h2 * q5 + 0.25 * (step_y - step("2", 0))
+    f4 = scale * q4 + (0.5 * (s22 + step("5", 0)) - third)
+    f5 = q5 * (scale - 0.5 * q1) + h2 * q3 + 0.25 * (step("2", 1) - step_x)
+    return (f1, f2, f3, f4, f5), rolled
 
 
 def mixed(q):
     return q[1], q[0] - q[3], q[4], q[2]
 
 
-def spread(r):
-    return 0.5 * r[0], -0.25 * r[1], 0.25 * r[2], -0.5 * r[0], -0.25 * r[3]
-
-
-def along_plane(f):
-    around = pltpu.roll(f, NX - 1, 0) + pltpu.roll(f, 1, 0)
-    around = around + pltpu.roll(f, NY - 1, 1) + pltpu.roll(f, 1, 1)
-    return (6.0 + 1.0 / SMOOTH) * f - around
+def add_spread(f, r, factor):
+    half = (0.5 * factor) * r[0]
+    return (
+        f[0] + half,
+        f[1] - (0.25 * factor) * r[1],
+        f[2] + (0.25 * factor) * r[2],
+        f[3] - half,
+        f[4] - (0.25 * factor) * r[3],
+    )
+
+
+def along_plane(f, x, y):
+    return (6.0 + 1.0 / SMOOTH) * f - ((x[0] + x[1]) + (y[0] + y[1]))
 
 
 def push(stack, slot, half, value):
@@ -144,11 +157,16 @@
         qo = [img[i, c, 1] for c in range(5)]
         re = mixed(qe)
         ro = mixed(qo)
-        for c, (f, g) in enumerate(zip(local_drive(qe), spread(ro))):
-            push(stack, c, 0, times_right(f + 2.0 * g, ty[...]))
-        bo = spread([along_plane(r) for r in ro])
-        for c, (f, g, b) in enumerate(zip(local_drive(qo), spread(re), bo)):
-            push(stack, c, 1, times_right(f - g - b, ty[...]))
+        f, _ = local_drive(qe)
+        for c, value in enumerate(add_spread(f, ro, 2.0)):
+            push(stack, c, 0, times_right(value, ty[...]))
+        f, rolled = local_drive(qo)
+        total = [re[1] + along_plane(ro[1], shifts(ro[1], 0), shifts(ro[1], 1))]
+        for r, name in ((0, "2"), (2, "5"), (3, "3")):
+            total.append(re[r] + along_plane(ro[r], rolled[name, 0], rolled[name, 1]))
+        total = (total[1], total[0], total[2], total[3])
+        for c, value in enumerate(add_spread(f, total, -1.0)):
+            push(stack, c, 1, times_right(value, ty[...]))
         for r in range(4):
             push(stack, 5 + r // 2, r % 2, times_right(re[r], ty[...]))
         for n in range(7):
@@ -166,11 +184,13 @@
             b = spectrum[1, n, :, cols].reshape(16, 8, 128)
             return jnp.where(first, a, b) if part == 0 else jnp.where(first, b, a)
 
-        g = spread([beta * tile(5 + r // 2, r % 2) for r in range(4)])
+        g = [beta * tile(5 + r // 2, r % 2) for r in range(4)]
+        ys = [tile(c, 0) for c in range(5)]
+        ks = add_spread(ys, g, 1.0)
         for c in range(5):
-            y = tile(c, 0)
+            y = ys[c]
             out[rows, 0, 0, c] = beta * tile(c, 1) + y
-            out[rows, 1, 0, c] = y + g[c]
+            out[rows, 1, 0, c] = ks[c]
             keep[0, c, rows] = back * y
 
 
@@ -228,16 +248,17 @@
     return jnp.sum((value * value).reshape(16, 8, 128), axis=0)
 
 
-def inverse_kernel(*refs, pair):
+def inverse_kernel(*refs, chosen):
     spec, keep, img, ty, tx = refs[:5]
     stack = refs[-1]
-    if pair == 0:
-        out, sums = refs[5:7], refs[7]
+    if chosen[0] == 0:
+        out = [refs[5]]
+        start = None
     else:
-        lower, upper, sums = refs[5:8]
-        out = [upper.at[0], upper.at[1]]
+        start, second, upper, sums = refs[5:9]
+        out = [second, upper.at[0], upper.at[1]]
+        sums[...] = jnp.zeros_like(sums)
     first = lax.broadcasted_iota(jnp.int32, (16, 8, 128), 1) < 4
-    sums[...] = jnp.zeros_like(sums)
 
     @pl.loop(0, 5)
     def _(c):
@@ -245,35 +266,35 @@
         weight = weight * (1.0 / SMOOTH)
         other = jnp.where(c == 1, 0.25 / SMOOTH, 0.0)
         source = jnp.where(c == 1, 0, jnp.where(c == 2, 4, jnp.where(c == 4, 2, 1)))
-        planes = []
-        for i in range(2):
-            image = 2 * pair + i
+        if start is not None:
+            last = (start[c, 0], start[c, 1])
+        for n, image in enumerate(chosen):
+            pair, i = image // 2, image % 2
             p_even, p_odd = spec[0:16, pair, c, 0], spec[16:32, pair, c, 0]
             w_even = spec[0:16, pair, c, 1] + keep[pair, c, 0:16]
             w_odd = spec[16:32, pair, c, 1] + keep[pair, c, 16:32]
             if i == 1:
                 p_even, p_odd, w_even, w_odd = p_odd, p_even, w_odd, w_even
-            push(stack, i, 0, jnp.where(first, w_even, w_odd).reshape(128, 128))
-            push(stack, i, 1, jnp.where(first, p_even, p_odd).reshape(128, 128))
-            both = jnp.dot(tx[i], stack[i], preferred_element_type=F32)
+            push(stack, n, 0, jnp.where(first, w_even, w_odd).reshape(128, 128))
+            push(stack, n, 1, jnp.where(first, p_even, p_odd).reshape(128, 128))
+            both = jnp.dot(tx[i], stack[n], preferred_element_type=F32)
             even = KEEP * img[image, c, 0] + times_right(both[:, :128], ty[...])
             odd = times_right(both[:, 128:], ty[...])
             odd = KEEP * img[image, c, 1] + odd * (1.0 / SMOOTH)
             odd = odd + (weight * img[image, source, 1] + other * img[image, 3, 1])
-            out[i][c, 0] = even
-            out[i][c, 1] = odd
-            planes.append((even, odd))
-        sums[0] += fold(planes[1][0] - planes[0][0]) + fold(planes[1][1] - planes[0][1])
-        if pair == 1:
-            sums[1] += fold(planes[0][0] - lower[c, 0]) + fold(planes[0][1] - lower[c, 1])
-
-
-def edge_kernel(first_sums, second_sums, upper, above, out):
+            out[n][c, 0] = even
+            out[n][c, 1] = odd
+            if start is not None:
+                sums[n] += fold(even - last[0]) + fold(odd - last[1])
+                last = (even, odd)
+
+
+def edge_kernel(sums, upper, above, out):
     edge = jnp.zeros((8, 128), F32)
     for c in range(5):
         for zz in range(2):
             edge = edge + fold(above[c, zz] - upper[1, c, zz])
-    rows = [first_sums[0], second_sums[1], second_sums[0], edge]
+    rows = [sums[0], sums[1], sums[2], edge]
     index = lax.broadcasted_iota(jnp.int32, (1, 128), 1)
     total = jnp.zeros((1, 128), F32)
     for g, row in enumerate(rows):
@@ -404,35 +425,36 @@
     )(where, f, rho)
 
 
-def inverse(spec, keep, images, pair, ty, tx, *lower):
-    if pair == 1:
-        out_shape = (pltpu.VMEM((2, 5, 2, 128, 128), F32),)
+def inverse(chosen, spec, keep, images, ty, tx, *start):
+    one = pltpu.VMEM((5, 2, 128, 128), F32)
+    if start:
+        out_shape = (one, pltpu.VMEM((2, 5, 2, 128, 128), F32), pltpu.VMEM((3, 8, 128), F32))
     else:
-        out_shape = (pltpu.VMEM((5, 2, 128, 128), F32),) * 2
-    out_shape = (*out_shape, pltpu.VMEM((2, 8, 128), F32))
-    args = (spec, keep, images, ty, tx, *lower)
+        out_shape = (one,)
+    args = (spec, keep, images, ty, tx, *start)
+    count = len(chosen)
     return pl.pallas_call(
-        functools.partial(inverse_kernel, pair=pair),
+        functools.partial(inverse_kernel, chosen=chosen),
         out_shape=out_shape,
         in_specs=[VMEM] * len(args),
         out_specs=(VMEM,) * len(out_shape),
-        scratch_shapes=[pltpu.VMEM((2, 384, 256), BF16)],
+        scratch_shapes=[pltpu.VMEM((count, 384, 256), BF16)],
         compiler_params=plain(INVERSE_MIB),
-        cost_estimate=cost(2_000_000_000, 6_000_000),
+        cost_estimate=cost(1_000_000_000 * count, 3_000_000 * count),
         name="inverse",
     )(*args)
 
 
-def edge(first_sums, second_sums, upper, above):
+def edge(sums, upper, above):
     return pl.pallas_call(
         edge_kernel,
         out_shape=jax.ShapeDtypeStruct((128, 1, 128), F32),
-        in_specs=[VMEM] * 4,
+        in_specs=[VMEM] * 3,
         out_specs=VMEM,
         compiler_params=plain(EDGE_MIB),
         cost_estimate=cost(2_000_000, 1_300_000),
         name="edge",
-    )(first_sums, second_sums, upper, above)
+    )(sums, upper, above)
 
 
 def final(centre, positions, sums, below, s0, s1, upper, a0, a1):
@@ -460,12 +482,12 @@
     f = lax.all_to_all(f, "gz", 0, 0, tiled=True)
     u = solve(f, rho)
     u = lax.all_to_all(u, "gz", 0, 0, tiled=True)
-    s0, s1, first_sums = inverse(u, keep, images, 0, inverse_y, inverse_x)
+    (s0,) = inverse((0,), u, keep, images, inverse_y, inverse_x)
     a0 = lax.ppermute(s0, "img", rows_back)
+    s1, upper, sums = inverse((1, 2, 3), u, keep, images, inverse_y, inverse_x, s0)
     a1 = lax.ppermute(s1, "img", rows_back)
-    upper, second_sums = inverse(u, keep, images, 1, inverse_y, inverse_x, s1)
     below = lax.ppermute(upper, "img", rows)
-    part = edge(first_sums, second_sums, upper, a0)
+    part = edge(sums, upper, a0)
     sums = lax.all_to_all(part, ("img", "gz"), 0, 0, tiled=True)
     return final(centre, positions, sums, below, s0, s1, upper, a0, a1)
 

time: 135 us -> 135 us (level)
  no operation moved by 1% of the time
where the time goes in v4:
time: 135 us; the launch traced here: 134 us
  waiting for transfers between devices  53.4 us (40%)
  blocking collectives  37.5 us (28%)
  starting transfers between devices  24.4 us (18%)
  Pallas kernels  18.7 us (14%)
    all_to_all x1, blocking collectives, local(): u = lax.all_to_all(u, 'gz', 0, 0, tiled=True)  37.5 us
    all_to_all x1, waiting for transfers between devices, local(): f = lax.all_to_all(f, 'gz', 0, 0, tiled=True)  34.7 us
    all_to_all x1, starting transfers between devices, local(): f = lax.all_to_all(f, 'gz', 0, 0, tiled=True)  9.84 us
    ppermute x1, waiting for transfers between devices, local(): a0 = lax.ppermute(s0, 'img', rows_back)  9.55 us
    ppermute x1, starting transfers between devices, local(): below = lax.ppermute(upper, 'img', rows)  7.19 us
    pallas_call x1, Pallas kernels, forward(): pl.pallas_call(forward_kernel, out_shape=(jax.ShapeDtypeStruct((GROUPS, 2...  6.52 us
    all_to_all x1, waiting for transfers between devices, local(): sums = lax.all_to_all(part, ('img', 'gz'), 0, 0, tiled=True)  6.26 us
    pallas_call x1, Pallas kernels, final(): pl.pallas_call(final_kernel, out_shape=jax.ShapeDtypeStruct((4, 5, 2, 128...  5.33 us
  transfers between devices with their start and end apart: 5, of which 4 were waited for; matrix products, arithmetic and copies ran while one was open for 0% of the time, Pallas kernels for 1%

profile of v4, /device:TPU:1, one launch (start us, length us, event | category | flops | bytes accessed | tf_op | source)
XLA Modules:
  0.0 134.1 jit_solution(17572889856347487414)
XLA Ops:
  0.0 6.5 %forward.1 = (f32[32,2,2,5,8,128]{5,4,3,2,1,0:T(8,128)}, f32[2,5,32,8,128]{4,3,2,1,0:T(8,128)}) custom-call(f32[4,5,2,128,128]{4,3,2,1,0:T(8,128)} %refs_2_.3, bf16[256,256]{1,0:T(8,128)(2,1)} %constant.19.clone.ty, bf16[2,128,384]{2,1,0:T(8,128)(2,1)} %constant.21.clone.tx, f32[32,8,128]{2,1,0:T(8,128)} %constant.23.clone.rho_ref), custom_call_target="tpu_custom_call" | custom-call | flops 3000000000 | bytes 9000000 | tf_op jit(solution)/shard_map/forward/pallas_call | solution.py:376
  6.5 9.8 %all-to-all-start = ((f32[32,2,2,5,8,128]{5,4,3,2,1,0:T(8,128)}), f32[32,2,2,5,8,128]{5,4,3,2,1,0:T(8,128)S(1)}, u32[]{:S(2)}, u32[]{:S(2)}) async-start(f32[32,2,2,5,8,128]{5,4,3,2,1,0:T(8,128)} %get-tuple-element.10), calls=%async_computation | async-start | bytes 5242880 | tf_op jit(solution)/shard_map/all_to_all | solution.py:482
  16.4 34.7 %all-to-all-done.f = f32[32,2,2,5,8,128]{5,4,3,2,1,0:T(8,128)S(1)} async-done(((f32[32,2,2,5,8,128]{5,4,3,2,1,0:T(8,128)}), f32[32,2,2,5,8,128]{5,4,3,2,1,0:T(8,128)S(1)}, u32[]{:S(2)}, u32[]{:S(2)}) %all-to-all-start) | async-done | bytes 2621472 | tf_op jit(solution)/shard_map/all_to_all | solution.py:482
  51.1 1.1 solve.1
  52.2 0.0 copy-start
  52.2 0.0 copy-start.2
  52.3 0.0 copy-start.3
  52.3 37.5 %all_to_all.15.refs_0_ = f32[32,2,5,2,8,128]{5,4,3,2,1,0:T(8,128)S(1)} all-to-all(f32[32,2,5,2,8,128]{5,4,3,2,1,0:T(8,128)S(1)} %solve.1), channel_id=1, replica_groups=mesh['img'=4,'gz'=32] {'gz'}, dimensions={0} | all-to-all | bytes 5242880 | tf_op jit(solution)/shard_map/all_to_all | solution.py:484
  89.7 0.0 copy-done
  89.7 0.0 copy-done.2
  89.8 2.0 %inverse.2.refs_5_.s0 = f32[5,2,128,128]{3,2,1,0:T(8,128)S(1)} custom-call(f32[32,2,5,2,8,128]{5,4,3,2,1,0:T(8,128)S(1)} %all_to_all.15.refs_0_, f32[2,5,32,8,128]{4,3,2,1,0:T(8,128)S(1)} %copy-done.1, f32[4,5,2,128,128]{4,3,2,1,0:T(8,128)S(1)} %copy-done, bf16[256,256]{1,0:T(8,128)(2,1)S(1)} %copy-done.3, bf16[2,128,384]{2,1,0:T(8,128)(2,1)S(1)} %copy-done.2), custom_call_target="tpu_custom_call" | custom-call | flops 1000000000 | bytes 3000000 | tf_op jit(solution)/shard_map/inverse/pallas_call | solution.py:436
  91.8 0.0 copy-start.5
  91.8 0.0 copy-start.6
  91.8 2.8 %inverse.3 = (f32[5,2,128,128]{3,2,1,0:T(8,128)S(1)}, f32[2,5,2,128,128]{4,3,2,1,0:T(8,128)S(1)}, f32[3,8,128]{2,1,0:T(8,128)S(1)}) custom-call(f32[32,2,5,2,8,128]{5,4,3,2,1,0:T(8,128)S(1)} %all_to_all.15.refs_0_, f32[2,5,32,8,128]{4,3,2,1,0:T(8,128)S(1)} %copy-done.1, f32[4,5,2,128,128]{4,3,2,1,0:T(8,128)S(1)} %copy-done, bf16[256,256]{1,0:T(8,128)(2,1)S(1)} %copy-done.3, ...), custom_call_target="tpu_custom_call" | custom-call | flops 3000000000 | bytes 9000000 | tf_op jit(solution)/shard_map/inverse/pallas_call | solution.py:436
  94.7 7.2 %collective-permute-start.1 = (f32[2,5,2,128,128]{4,3,2,1,0:T(8,128)S(1)}, f32[2,5,2,128,128]{4,3,2,1,0:T(8,128)}, u32[]{:S(2)}, u32[]{:S(2)}) collective-permute-start(f32[2,5,2,128,128]{4,3,2,1,0:T(8,128)S(1)} %get-tuple-element.13.upper), channel_id=1, source_target_pairs={{0,32},{32,64},{64,96},{1,33},{33,65},{65,97},{2,34},{34,66},{66,9... | collective-permute-start | bytes 3932168 | tf_op jit(solution)/shard_map/ppermute | solution.py:489
  101.9 1.9 %collective-permute-start = (f32[5,2,128,128]{3,2,1,0:T(8,128)S(1)}, f32[5,2,128,128]{3,2,1,0:T(8,128)S(1)}, u32[]{:S(2)}, u32[]{:S(2)}) collective-permute-start(f32[5,2,128,128]{3,2,1,0:T(8,128)S(1)} %inverse.2.refs_5_.s0), channel_id=1, source_target_pairs={{32,0},{64,32},{96,64},{33,1},{65,33},{97,65},{34,2},{66,34},{98,6... | collective-permute-start | bytes 1966088 | tf_op jit(solution)/shard_map/ppermute | solution.py:486
  103.8 1.9 %collective-permute-start.2 = (f32[5,2,128,128]{3,2,1,0:T(8,128)S(1)}, f32[5,2,128,128]{3,2,1,0:T(8,128)}, u32[]{:S(2)}, u32[]{:S(2)}) collective-permute-start(f32[5,2,128,128]{3,2,1,0:T(8,128)S(1)} %get-tuple-element.14.s1), channel_id=1, source_target_pairs={{32,0},{64,32},{96,64},{33,1},{65,33},{97,65},{34,2},{66,34},{98,6... | collective-permute-start | bytes 1966088 | tf_op jit(solution)/shard_map/ppermute | solution.py:488
  105.7 9.6 %collective-permute-done.above.a0 = f32[5,2,128,128]{3,2,1,0:T(8,128)S(1)} collective-permute-done((f32[5,2,128,128]{3,2,1,0:T(8,128)S(1)}, f32[5,2,128,128]{3,2,1,0:T(8,128)S(1)}, u32[]{:S(2)}, u32[]{:S(2)}) %collective-permute-start) | collective-permute-done | bytes 655392 | tf_op jit(solution)/shard_map/ppermute | solution.py:486
  115.3 0.9 edge.1
  116.1 3.5 %all-to-all-start.2 = ((f32[128,1,128]{2,1,0:T(1,128)}), f32[128,1,128]{2,1,0:T(1,128)S(1)}, u32[]{:S(2)}, u32[]{:S(2)}) async-start(f32[128,1,128]{2,1,0:T(1,128)} %edge.1), calls=%async_computation.2 | async-start | bytes 131072 | tf_op jit(solution)/shard_map/all_to_all | solution.py:491
  119.7 2.8 %collective-permute-done.2.a1 = f32[5,2,128,128]{3,2,1,0:T(8,128)} collective-permute-done((f32[5,2,128,128]{3,2,1,0:T(8,128)S(1)}, f32[5,2,128,128]{3,2,1,0:T(8,128)}, u32[]{:S(2)}, u32[]{:S(2)}) %collective-permute-start.2) | collective-permute-done | bytes 655392 | tf_op jit(solution)/shard_map/ppermute | solution.py:488
  122.5 6.3 %all-to-all-done.2.sums = f32[128,1,128]{2,1,0:T(1,128)S(1)} async-done(((f32[128,1,128]{2,1,0:T(1,128)}), f32[128,1,128]{2,1,0:T(1,128)S(1)}, u32[]{:S(2)}, u32[]{:S(2)}) %all-to-all-start.2) | async-done | bytes 65568 | tf_op jit(solution)/shard_map/all_to_all | solution.py:491
  128.8 0.0 collective-permute-done.1.below
  128.8 5.3 %final.1 = f32[4,5,2,128,128]{4,3,2,1,0:T(8,128)} custom-call(s32[4]{0:T(128)S(1)} %copy-done.5, f32[4]{0:T(128)S(1)} %copy-done.6, s32[1]{0:T(128)} %bitcast.where, f32[128,1,128]{2,1,0:T(1,128)S(1)} %all-to-all-done.2.sums, f32[2,5,2,128,128]{4,3,2,1,0:T(8,128)} %collective-permute-done.1.below, f32[5,2,128,128]{3,2,1,0:T(8,128)S(1)} %inverse.2.refs_5_.s0, ...), custom_call_target="tpu_custom_call" | custom-call | flops 30000000 | bytes 8000000 | tf_op jit(solution)/shard_map/final/pallas_call | solution.py:464
  (7 shorter events, 0.0 us)
Async XLA Ops:
  6.5 44.6 %copy-start.4 = (f32[32,8,128]{2,1,0:T(8,128)S(1)}, f32[32,8,128]{2,1,0:T(8,128)}, u32[]{:S(2)}) copy-start(f32[32,8,128]{2,1,0:T(8,128)} %constant.23.clone.rho_ref) | copy-start | bytes 393220
  6.5 44.6 %all-to-all-start = ((f32[32,2,2,5,8,128]{5,4,3,2,1,0:T(8,128)}), f32[32,2,2,5,8,128]{5,4,3,2,1,0:T(8,128)S(1)}, u32[]{:S(2)}, u32[]{:S(2)}) async-start(f32[32,2,2,5,8,128]{5,4,3,2,1,0:T(8,128)} %get-tuple-element.10), calls=%async_computation | async-start | bytes 5242880 | tf_op jit(solution)/shard_map/all_to_all | solution.py:482
  52.2 37.5 %copy-start = (f32[4,5,2,128,128]{4,3,2,1,0:T(8,128)S(1)}, f32[4,5,2,128,128]{4,3,2,1,0:T(8,128)}, u32[]{:S(2)}) copy-start(f32[4,5,2,128,128]{4,3,2,1,0:T(8,128)} %refs_2_.3) | copy-start | bytes 7864324
  52.2 37.5 %copy-start.1 = (f32[2,5,32,8,128]{4,3,2,1,0:T(8,128)S(1)}, f32[2,5,32,8,128]{4,3,2,1,0:T(8,128)}, u32[]{:S(2)}) copy-start(f32[2,5,32,8,128]{4,3,2,1,0:T(8,128)} %get-tuple-element.11.refs_1_) | copy-start | bytes 3932164
  52.2 37.5 %copy-start.2 = (bf16[2,128,384]{2,1,0:T(8,128)(2,1)S(1)}, bf16[2,128,384]{2,1,0:T(8,128)(2,1)}, u32[]{:S(2)}) copy-start(bf16[2,128,384]{2,1,0:T(8,128)(2,1)} %constant.22.clone.refs_4_) | copy-start | bytes 589828
  52.3 37.5 %copy-start.3 = (bf16[256,256]{1,0:T(8,128)(2,1)S(1)}, bf16[256,256]{1,0:T(8,128)(2,1)}, u32[]{:S(2)}) copy-start(bf16[256,256]{1,0:T(8,128)(2,1)} %constant.20.clone.refs_3_) | copy-start | bytes 393220
  91.8 37.0 %copy-start.5 = (s32[4]{0:T(128)S(1)}, s32[4]{0:T(128)}, u32[]{:S(2)}) copy-start(s32[4]{0:T(128)} %centre.1) | copy-start | bytes 52
  91.8 37.0 %copy-start.6 = (f32[4]{0:T(128)S(1)}, f32[4]{0:T(128)}, u32[]{:S(2)}) copy-start(f32[4]{0:T(128)} %positions.1) | copy-start | bytes 52
  94.7 34.1 %collective-permute-start.1 = (f32[2,5,2,128,128]{4,3,2,1,0:T(8,128)S(1)}, f32[2,5,2,128,128]{4,3,2,1,0:T(8,128)}, u32[]{:S(2)}, u32[]{:S(2)}) collective-permute-start(f32[2,5,2,128,128]{4,3,2,1,0:T(8,128)S(1)} %get-tuple-element.13.upper), channel_id=1, source_target_pairs={{0,32},{32,64},{64,96},{1,33},{33,65},{65,97},{2,34},{34,66},{66,9... | collective-permute-start | bytes 3932168 | tf_op jit(solution)/shard_map/ppermute | solution.py:489
  101.9 13.4 %collective-permute-start = (f32[5,2,128,128]{3,2,1,0:T(8,128)S(1)}, f32[5,2,128,128]{3,2,1,0:T(8,128)S(1)}, u32[]{:S(2)}, u32[]{:S(2)}) collective-permute-start(f32[5,2,128,128]{3,2,1,0:T(8,128)S(1)} %inverse.2.refs_5_.s0), channel_id=1, source_target_pairs={{32,0},{64,32},{96,64},{33,1},{65,33},{97,65},{34,2},{66,34},{98,6... | collective-permute-start | bytes 1966088 | tf_op jit(solution)/shard_map/ppermute | solution.py:486
  103.8 18.7 %collective-permute-start.2 = (f32[5,2,128,128]{3,2,1,0:T(8,128)S(1)}, f32[5,2,128,128]{3,2,1,0:T(8,128)}, u32[]{:S(2)}, u32[]{:S(2)}) collective-permute-start(f32[5,2,128,128]{3,2,1,0:T(8,128)S(1)} %get-tuple-element.14.s1), channel_id=1, source_target_pairs={{32,0},{64,32},{96,64},{33,1},{65,33},{97,65},{34,2},{66,34},{98,6... | collective-permute-start | bytes 1966088 | tf_op jit(solution)/shard_map/ppermute | solution.py:488
  116.1 12.6 %all-to-all-start.2 = ((f32[128,1,128]{2,1,0:T(1,128)}), f32[128,1,128]{2,1,0:T(1,128)S(1)}, u32[]{:S(2)}, u32[]{:S(2)}) async-start(f32[128,1,128]{2,1,0:T(1,128)} %edge.1), calls=%async_computation.2 | async-start | bytes 131072 | tf_op jit(solution)/shard_map/all_to_all | solution.py:491

commit v5 on v4

--- a/solution.py
+++ b/solution.py
@@ -20,7 +20,7 @@
 KEEP = 1.0 - 1.0 / SMOOTH
 FORWARD_MIB = 60
 SOLVE_MIB = 16
-INVERSE_MIB = 8
+INVERSE_MIB = 62.3
 EDGE_MIB = 4
 FINAL_MIB = 16
 F32 = jnp.float32
@@ -194,7 +194,7 @@
             keep[0, c, rows] = back * y
 
 
-def solve_kernel(where, f, rho_ref, out, right, work):
+def solve_kernel(where, f, rho_ref, out0, out1, right, work):
     del where
     rho = rho_ref[0]
     sigma = rho * rho
@@ -226,7 +226,8 @@
     back = jnp.broadcast_to((1.0 / SMOOTH) / (rho + 1.0 / rho), shape)
 
     def put(s, slot, value):
-        out[s, :, :, slot] = value
+        out0[s, :, slot] = value[0]
+        out1[s, :, slot] = value[1]
 
     def down(n, carry):
         u, after = carry
@@ -248,53 +249,66 @@
     return jnp.sum((value * value).reshape(16, 8, 128), axis=0)
 
 
-def inverse_kernel(*refs, chosen):
-    spec, keep, img, ty, tx = refs[:5]
-    stack = refs[-1]
-    if chosen[0] == 0:
-        out = [refs[5]]
+def inverse_kernel(*refs, pair):
+    spec_hbm, keep_hbm, img_hbm, ty, tx = refs[:5]
+    spec, img, keep, spec_sem, img_sem, keep_sem, stack = refs[-7:]
+    if pair == 0:
+        out, sums = refs[5:7], refs[7]
         start = None
     else:
-        start, second, upper, sums = refs[5:9]
-        out = [second, upper.at[0], upper.at[1]]
-        sums[...] = jnp.zeros_like(sums)
+        start, upper, sums = refs[5:8]
+        out = [upper.at[0], upper.at[1]]
+
+    def fetch_keep(c):
+        return pltpu.make_async_copy(keep_hbm.at[pair, c], keep.at[c], keep_sem.at[c])
+
+    def fetch_spec(c):
+        return pltpu.make_async_copy(spec_hbm.at[:, c], spec.at[c], spec_sem.at[c])
+
+    images = pltpu.make_async_copy(img_hbm.at[pl.ds(2 * pair, 2)], img, img_sem)
+    images.start()
+    for c in range(5):
+        fetch_spec(c).start()
+        fetch_keep(c).start()
+    sums[...] = jnp.zeros_like(sums)
     first = lax.broadcasted_iota(jnp.int32, (16, 8, 128), 1) < 4
+    images.wait()
 
     @pl.loop(0, 5)
     def _(c):
+        fetch_spec(c).wait()
+        fetch_keep(c).wait()
         weight = jnp.where(c == 0, 0.5, jnp.where(c == 3, -0.5, jnp.where(c == 2, 0.25, -0.25)))
         weight = weight * (1.0 / SMOOTH)
         other = jnp.where(c == 1, 0.25 / SMOOTH, 0.0)
         source = jnp.where(c == 1, 0, jnp.where(c == 2, 4, jnp.where(c == 4, 2, 1)))
-        if start is not None:
-            last = (start[c, 0], start[c, 1])
-        for n, image in enumerate(chosen):
-            pair, i = image // 2, image % 2
-            p_even, p_odd = spec[0:16, pair, c, 0], spec[16:32, pair, c, 0]
-            w_even = spec[0:16, pair, c, 1] + keep[pair, c, 0:16]
-            w_odd = spec[16:32, pair, c, 1] + keep[pair, c, 16:32]
+        last = None if start is None else (start[c, 0], start[c, 1])
+        for i in range(2):
+            p_even, p_odd = spec[c, 0:16, 0], spec[c, 16:32, 0]
+            w_even = spec[c, 0:16, 1] + keep[c, 0:16]
+            w_odd = spec[c, 16:32, 1] + keep[c, 16:32]
             if i == 1:
                 p_even, p_odd, w_even, w_odd = p_odd, p_even, w_odd, w_even
-            push(stack, n, 0, jnp.where(first, w_even, w_odd).reshape(128, 128))
-            push(stack, n, 1, jnp.where(first, p_even, p_odd).reshape(128, 128))
-            both = jnp.dot(tx[i], stack[n], preferred_element_type=F32)
-            even = KEEP * img[image, c, 0] + times_right(both[:, :128], ty[...])
+            push(stack, i, 0, jnp.where(first, w_even, w_odd).reshape(128, 128))
+            push(stack, i, 1, jnp.where(first, p_even, p_odd).reshape(128, 128))
+            both = jnp.dot(tx[i], stack[i], preferred_element_type=F32)
+            even = KEEP * img[i, c, 0] + times_right(both[:, :128], ty[...])
             odd = times_right(both[:, 128:], ty[...])
-            odd = KEEP * img[image, c, 1] + odd * (1.0 / SMOOTH)
-            odd = odd + (weight * img[image, source, 1] + other * img[image, 3, 1])
-            out[n][c, 0] = even
-            out[n][c, 1] = odd
-            if start is not None:
-                sums[n] += fold(even - last[0]) + fold(odd - last[1])
-                last = (even, odd)
-
-
-def edge_kernel(sums, upper, above, out):
+            odd = KEEP * img[i, c, 1] + odd * (1.0 / SMOOTH)
+            odd = odd + (weight * img[i, source, 1] + other * img[i, 3, 1])
+            out[i][c, 0] = even
+            out[i][c, 1] = odd
+            if last is not None:
+                sums[i] += fold(even - last[0]) + fold(odd - last[1])
+            last = (even, odd)
+
+
+def edge_kernel(first_sums, second_sums, upper, above, out):
     edge = jnp.zeros((8, 128), F32)
     for c in range(5):
         for zz in range(2):
             edge = edge + fold(above[c, zz] - upper[1, c, zz])
-    rows = [sums[0], sums[1], sums[2], edge]
+    rows = [first_sums[1], second_sums[0], second_sums[1], edge]
     index = lax.broadcasted_iota(jnp.int32, (1, 128), 1)
     total = jnp.zeros((1, 128), F32)
     for g, row in enumerate(rows):
@@ -340,8 +354,7 @@
                     value = jnp.where(c - 1 + n == spot, w[n], value)
                 weights[m, r] = value
 
-    c = pl.program_id(0)
-    pieces = [below[0, 0], below[1, 0], s0[c], s1[c], upper[0, c], upper[1, c], a0[c], a1[0]]
+    pieces = [below[0, 0], below[1, 0], s0[0], s1[0], upper[0, 0], upper[1, 0], a0[0], a1[0]]
     pieces = [p.reshape(32, 8, 128) for p in pieces]
     for m in range(LOCAL):
         acc = pieces[m] * weights[m, 0][None]
@@ -356,10 +369,11 @@
 
 SMEM = pl.BlockSpec(memory_space=pltpu.SMEM)
 VMEM = pl.BlockSpec(memory_space=pltpu.VMEM)
+HBM = pl.BlockSpec(memory_space=pltpu.HBM)
 
 
 def plain(mib):
-    return pltpu.CompilerParams(vmem_limit_bytes=mib * 1024 * 1024)
+    return pltpu.CompilerParams(vmem_limit_bytes=min(int(mib * 1024 * 1024), 67_043_328))
 
 
 def params(mib):
@@ -402,10 +416,10 @@
 
 def solve(f, rho):
     where = lax.axis_index("gz").astype(jnp.int32).reshape(1)
-    result = (GROUPS, 2, 5, 2, 8, 128)
+    half = pltpu.VMEM((GROUPS, 5, 2, 8, 128), F32)
     return pl.pallas_call(
         solve_kernel,
-        out_shape=pltpu.VMEM(result, F32),
+        out_shape=(half, half),
         grid_spec=pltpu.PrefetchScalarGridSpec(
             num_scalar_prefetch=1,
             grid=(1,),
@@ -413,7 +427,7 @@
                 VMEM,
                 pl.BlockSpec((1, 8, 128), lambda i, w: (w[0], 0, 0)),
             ],
-            out_specs=VMEM,
+            out_specs=(VMEM, VMEM),
             scratch_shapes=[
                 pltpu.VMEM((GROUPS, 2, 5, 8, 128), F32),
                 pltpu.VMEM((GROUPS, 2, 5, 8, 128), F32),
@@ -425,36 +439,43 @@
     )(where, f, rho)
 
 
-def inverse(chosen, spec, keep, images, ty, tx, *start):
-    one = pltpu.VMEM((5, 2, 128, 128), F32)
-    if start:
-        out_shape = (one, pltpu.VMEM((2, 5, 2, 128, 128), F32), pltpu.VMEM((3, 8, 128), F32))
+def inverse(pair, spec, keep, images, ty, tx, *start):
+    if pair == 0:
+        out_shape = (pltpu.VMEM((5, 2, 128, 128), F32),) * 2
     else:
-        out_shape = (one,)
+        out_shape = (pltpu.VMEM((2, 5, 2, 128, 128), F32),)
+    out_shape = (*out_shape, pltpu.VMEM((2, 8, 128), F32))
     args = (spec, keep, images, ty, tx, *start)
-    count = len(chosen)
     return pl.pallas_call(
-        functools.partial(inverse_kernel, chosen=chosen),
+        functools.partial(inverse_kernel, pair=pair),
         out_shape=out_shape,
-        in_specs=[VMEM] * len(args),
+        in_specs=[HBM, HBM, HBM, VMEM, VMEM] + [VMEM] * len(start),
         out_specs=(VMEM,) * len(out_shape),
-        scratch_shapes=[pltpu.VMEM((count, 384, 256), BF16)],
+        scratch_shapes=[
+            pltpu.VMEM((5, GROUPS, 2, 8, 128), F32),
+            pltpu.VMEM((2, 5, 2, 128, 128), F32),
+            pltpu.VMEM((5, GROUPS, 8, 128), F32),
+            pltpu.SemaphoreType.DMA((5,)),
+            pltpu.SemaphoreType.DMA,
+            pltpu.SemaphoreType.DMA((5,)),
+            pltpu.VMEM((2, 384, 256), BF16),
+        ],
         compiler_params=plain(INVERSE_MIB),
-        cost_estimate=cost(1_000_000_000 * count, 3_000_000 * count),
+        cost_estimate=cost(2_000_000_000, 6_000_000),
         name="inverse",
     )(*args)
 
 
-def edge(sums, upper, above):
+def edge(first_sums, second_sums, upper, above):
     return pl.pallas_call(
         edge_kernel,
         out_shape=jax.ShapeDtypeStruct((128, 1, 128), F32),
-        in_specs=[VMEM] * 3,
+        in_specs=[VMEM] * 4,
         out_specs=VMEM,
         compiler_params=plain(EDGE_MIB),
         cost_estimate=cost(2_000_000, 1_300_000),
         name="edge",
-    )(sums, upper, above)
+    )(first_sums, second_sums, upper, above)
 
 
 def final(centre, positions, sums, below, s0, s1, upper, a0, a1):
@@ -465,7 +486,7 @@
         final_kernel,
         out_shape=jax.ShapeDtypeStruct((4, 5, 2, 128, 128), F32),
         grid=(5,),
-        in_specs=[SMEM, SMEM, SMEM, VMEM, pair, VMEM, VMEM, VMEM, VMEM, one],
+        in_specs=[SMEM, SMEM, SMEM, VMEM, pair, one, one, pair, one, one],
         out_specs=pl.BlockSpec((4, 1, 2, 128, 128), lambda c: (0, c, 0, 0, 0)),
         scratch_shapes=[pltpu.VMEM((4, 5, 8, 128), F32)],
         compiler_params=params(FINAL_MIB),
@@ -480,14 +501,15 @@
     rows_back = [(b, a) for a, b in rows]
     f, keep = forward(images, forward_y, forward_x, rho)
     f = lax.all_to_all(f, "gz", 0, 0, tiled=True)
-    u = solve(f, rho)
-    u = lax.all_to_all(u, "gz", 0, 0, tiled=True)
-    (s0,) = inverse((0,), u, keep, images, inverse_y, inverse_x)
+    u0, u1 = solve(f, rho)
+    u0 = lax.all_to_all(u0, "gz", 0, 0, tiled=True)
+    u1 = lax.all_to_all(u1, "gz", 0, 0, tiled=True)
+    s0, s1, first_sums = inverse(0, u0, keep, images, inverse_y, inverse_x)
     a0 = lax.ppermute(s0, "img", rows_back)
-    s1, upper, sums = inverse((1, 2, 3), u, keep, images, inverse_y, inverse_x, s0)
+    upper, second_sums = inverse(1, u1, keep, images, inverse_y, inverse_x, s1)
     a1 = lax.ppermute(s1, "img", rows_back)
     below = lax.ppermute(upper, "img", rows)
-    part = edge(sums, upper, a0)
+    part = edge(first_sums, second_sums, upper, a0)
     sums = lax.all_to_all(part, ("img", "gz"), 0, 0, tiled=True)
     return final(centre, positions, sums, below, s0, s1, upper, a0, a1)
 

time: 135 us -> 148 us (1.096)
  blocking collectives: 37.5 us -> 23.9 us
  waiting for transfers between devices: 53.4 us -> 63.2 us
  local copies, waits for them, and re-layouts: 0.04 us -> 5.78 us
  Pallas kernels: 18.7 us -> 24.4 us
  starting transfers between devices: 24.4 us -> 29.9 us
    all_to_all x1, blocking collectives: 37.5 us -> 23.9 us  [local(): u0 = lax.all_to_all(u0, 'gz', 0, 0, tiled=True)]
    all_to_all x0 -> x1, waiting for transfers between devices: none -> 9.82 us  [local(): u1 = lax.all_to_all(u1, 'gz', 0, 0, tiled=True)]
    pallas_call x3, Pallas kernels: 5.98 us -> 12 us  [the longest x2 10.9 us: inverse(): pl.pallas_call(functools.partial(inverse_kernel, pair=pair), out_shape=ou...]
    unnamed x14 -> x20, local copies, waits for them, and re-layouts: 0.04 us -> 5.78 us
    all_to_all x0 -> x1, starting transfers between devices: none -> 4.68 us  [local(): u1 = lax.all_to_all(u1, 'gz', 0, 0, tiled=True)]
  transfers between devices with their start and end apart: 5 -> 6, of which waited for: 4 -> 5; matrix products, arithmetic and copies ran while one was open for 0% -> 0% of each run, Pallas kernels for 1% -> 4%
where the time goes in v5:
time: 148 us; the launch traced here: 147 us
  waiting for transfers between devices  63.2 us (43%)
  starting transfers between devices  29.9 us (20%)
  Pallas kernels  24.4 us (16%)
  blocking collectives  23.9 us (16%)
  local copies, waits for them, and re-layouts  5.78 us (4%)
    all_to_all x1, waiting for transfers between devices, local(): f = lax.all_to_all(f, 'gz', 0, 0, tiled=True)  34.7 us
    all_to_all x1, blocking collectives, local(): u0 = lax.all_to_all(u0, 'gz', 0, 0, tiled=True)  23.9 us
    pallas_call x2, Pallas kernels, inverse(): pl.pallas_call(functools.partial(inverse_kernel, pair=pair), out_shape=ou...  10.9 us
    all_to_all x1, starting transfers between devices, local(): f = lax.all_to_all(f, 'gz', 0, 0, tiled=True)  9.84 us
    all_to_all x1, waiting for transfers between devices, local(): u1 = lax.all_to_all(u1, 'gz', 0, 0, tiled=True)  9.82 us
    ppermute x1, waiting for transfers between devices, local(): a0 = lax.ppermute(s0, 'img', rows_back)  9.76 us
    ppermute x1, starting transfers between devices, local(): below = lax.ppermute(upper, 'img', rows)  8.05 us
    pallas_call x1, Pallas kernels, forward(): pl.pallas_call(forward_kernel, out_shape=(jax.ShapeDtypeStruct((GROUPS, 2...  6.5 us
  transfers between devices with their start and end apart: 6, of which 5 were waited for; matrix products, arithmetic and copies ran while one was open for 0% of the time, Pallas kernels for 4%

profile of v5, /device:TPU:1, one launch (start us, length us, event | category | flops | bytes accessed | tf_op | source)
XLA Modules:
  0.0 147.3 jit_solution(2537862562443295177)
XLA Ops:
  0.0 6.5 %forward.1 = (f32[32,2,2,5,8,128]{5,4,3,2,1,0:T(8,128)}, f32[2,5,32,8,128]{4,3,2,1,0:T(8,128)}) custom-call(f32[4,5,2,128,128]{4,3,2,1,0:T(8,128)} %refs_2_.3, bf16[256,256]{1,0:T(8,128)(2,1)} %constant.19.clone.ty, bf16[2,128,384]{2,1,0:T(8,128)(2,1)} %constant.21.clone.tx, f32[32,8,128]{2,1,0:T(8,128)} %constant.23.clone.rho_ref), custom_call_target="tpu_custom_call" | custom-call | flops 3000000000 | bytes 9000000 | tf_op jit(solution)/shard_map/forward/pallas_call | solution.py:390
  6.5 9.8 %all-to-all-start = ((f32[32,2,2,5,8,128]{5,4,3,2,1,0:T(8,128)}), f32[32,2,2,5,8,128]{5,4,3,2,1,0:T(8,128)S(1)}, u32[]{:S(2)}, u32[]{:S(2)}) async-start(f32[32,2,2,5,8,128]{5,4,3,2,1,0:T(8,128)} %get-tuple-element.14), calls=%async_computation | async-start | bytes 5242880 | tf_op jit(solution)/shard_map/all_to_all | solution.py:503
  16.4 34.7 %all-to-all-done.f = f32[32,2,2,5,8,128]{5,4,3,2,1,0:T(8,128)S(1)} async-done(((f32[32,2,2,5,8,128]{5,4,3,2,1,0:T(8,128)}), f32[32,2,2,5,8,128]{5,4,3,2,1,0:T(8,128)S(1)}, u32[]{:S(2)}, u32[]{:S(2)}) %all-to-all-start) | async-done | bytes 2621472 | tf_op jit(solution)/shard_map/all_to_all | solution.py:503
  51.1 1.1 solve.1
  52.2 23.9 %all_to_all.20.refs_0_ = f32[32,5,2,8,128]{4,3,2,1,0:T(8,128)} all-to-all(f32[32,5,2,8,128]{4,3,2,1,0:T(8,128)S(1)} %get-tuple-element.15), channel_id=1, replica_groups=mesh['img'=4,'gz'=32] {'gz'}, dimensions={0} | all-to-all | bytes 2621440 | tf_op jit(solution)/shard_map/all_to_all | solution.py:505
  76.1 4.7 %all-to-all-start.2 = ((f32[32,5,2,8,128]{4,3,2,1,0:T(8,128)}), f32[32,5,2,8,128]{4,3,2,1,0:T(8,128)}, u32[]{:S(2)}, u32[]{:S(2)}) async-start(f32[32,5,2,8,128]{4,3,2,1,0:T(8,128)} %copy-done), calls=%async_computation.2 | async-start | bytes 2621440 | tf_op jit(solution)/shard_map/all_to_all | solution.py:506
  80.8 5.3 %inverse.2 = (f32[5,2,128,128]{3,2,1,0:T(8,128)S(1)}, f32[5,2,128,128]{3,2,1,0:T(8,128)S(1)}, f32[2,8,128]{2,1,0:T(8,128)S(1)}) custom-call(f32[32,5,2,8,128]{4,3,2,1,0:T(8,128)} %all_to_all.20.refs_0_, f32[2,5,32,8,128]{4,3,2,1,0:T(8,128)} %get-tuple-element.16.refs_1_, f32[4,5,2,128,128]{4,3,2,1,0:T(8,128)} %refs_2_.3, ...), custom_call_target="tpu_custom_call" | custom-call | flops 2000000000 | bytes 6000000 | tf_op jit(solution)/shard_map/inverse/pallas_call | solution.py:449
  86.1 0.8 copy-done.1
  86.9 0.8 copy-done.3
  87.8 9.8 %all-to-all-done.2.refs_0_ = f32[32,5,2,8,128]{4,3,2,1,0:T(8,128)} async-done(((f32[32,5,2,8,128]{4,3,2,1,0:T(8,128)}), f32[32,5,2,8,128]{4,3,2,1,0:T(8,128)}, u32[]{:S(2)}, u32[]{:S(2)}) %all-to-all-start.2) | async-done | bytes 1310752 | tf_op jit(solution)/shard_map/all_to_all | solution.py:506
  97.6 5.6 %inverse.3 = (f32[2,5,2,128,128]{4,3,2,1,0:T(8,128)S(1)}, f32[2,8,128]{2,1,0:T(8,128)S(1)}) custom-call(f32[32,5,2,8,128]{4,3,2,1,0:T(8,128)} %all-to-all-done.2.refs_0_, f32[2,5,32,8,128]{4,3,2,1,0:T(8,128)} %get-tuple-element.16.refs_1_, f32[4,5,2,128,128]{4,3,2,1,0:T(8,128)} %refs_2_.3, bf16[256,256]{1,0:T(8,128)(2,1)} %constant.20.clone.refs_3_, ...), custom_call_target="tpu_custom_call" | custom-call | flops 2000000000 | bytes 6000000 | tf_op jit(solution)/shard_map/inverse/pallas_call | solution.py:449
  103.2 8.1 %collective-permute-start.1 = (f32[2,5,2,128,128]{4,3,2,1,0:T(8,128)S(1)}, f32[2,5,2,128,128]{4,3,2,1,0:T(8,128)}, u32[]{:S(2)}, u32[]{:S(2)}) collective-permute-start(f32[2,5,2,128,128]{4,3,2,1,0:T(8,128)S(1)} %get-tuple-element.21.upper), channel_id=1, source_target_pairs={{0,32},{32,64},{64,96},{1,33},{33,65},{65,97},{2,34},{34,66},{66,9... | collective-permute-start | bytes 3932168 | tf_op jit(solution)/shard_map/ppermute | solution.py:511
  111.3 1.9 %collective-permute-start = (f32[5,2,128,128]{3,2,1,0:T(8,128)}, f32[5,2,128,128]{3,2,1,0:T(8,128)S(1)}, u32[]{:S(2)}, u32[]{:S(2)}) collective-permute-start(f32[5,2,128,128]{3,2,1,0:T(8,128)} %copy-done.1), channel_id=1, source_target_pairs={{32,0},{64,32},{96,64},{33,1},{65,33},{97,65},{34,2},{66,34},{98,6... | collective-permute-start | bytes 1966088 | tf_op jit(solution)/shard_map/ppermute | solution.py:508
  113.2 1.9 %collective-permute-start.2 = (f32[5,2,128,128]{3,2,1,0:T(8,128)}, f32[5,2,128,128]{3,2,1,0:T(8,128)S(1)}, u32[]{:S(2)}, u32[]{:S(2)}) collective-permute-start(f32[5,2,128,128]{3,2,1,0:T(8,128)} %copy-done.3), channel_id=1, source_target_pairs={{32,0},{64,32},{96,64},{33,1},{65,33},{97,65},{34,2},{66,34},{98,6... | collective-permute-start | bytes 1966088 | tf_op jit(solution)/shard_map/ppermute | solution.py:510
  115.1 9.8 %collective-permute-done.above.a0 = f32[5,2,128,128]{3,2,1,0:T(8,128)S(1)} collective-permute-done((f32[5,2,128,128]{3,2,1,0:T(8,128)}, f32[5,2,128,128]{3,2,1,0:T(8,128)S(1)}, u32[]{:S(2)}, u32[]{:S(2)}) %collective-permute-start) | collective-permute-done | bytes 655392 | tf_op jit(solution)/shard_map/ppermute | solution.py:508
  124.9 0.9 edge.1
  125.7 3.5 %all-to-all-start.3 = ((f32[128,1,128]{2,1,0:T(1,128)}), f32[128,1,128]{2,1,0:T(1,128)S(1)}, u32[]{:S(2)}, u32[]{:S(2)}) async-start(f32[128,1,128]{2,1,0:T(1,128)} %edge.1), calls=%async_computation.3 | async-start | bytes 131072 | tf_op jit(solution)/shard_map/all_to_all | solution.py:513
  129.2 2.7 %collective-permute-done.2.a1 = f32[5,2,128,128]{3,2,1,0:T(8,128)S(1)} collective-permute-done((f32[5,2,128,128]{3,2,1,0:T(8,128)}, f32[5,2,128,128]{3,2,1,0:T(8,128)S(1)}, u32[]{:S(2)}, u32[]{:S(2)}) %collective-permute-start.2) | collective-permute-done | bytes 655392 | tf_op jit(solution)/shard_map/ppermute | solution.py:510
  131.9 0.8 copy-done.5
  132.7 6.2 %all-to-all-done.3.sums = f32[128,1,128]{2,1,0:T(1,128)S(1)} async-done(((f32[128,1,128]{2,1,0:T(1,128)}), f32[128,1,128]{2,1,0:T(1,128)S(1)}, u32[]{:S(2)}, u32[]{:S(2)}) %all-to-all-start.3) | async-done | bytes 65568 | tf_op jit(solution)/shard_map/all_to_all | solution.py:513
  139.0 1.1 copy-done.2
  140.1 1.1 copy-done.4
  141.1 1.1 copy-done.6
  142.2 5.1 %final.1 = f32[4,5,2,128,128]{4,3,2,1,0:T(8,128)} custom-call(s32[4]{0:T(128)S(1)} %copy-done.8, f32[4]{0:T(128)S(1)} %copy-done.9, s32[1]{0:T(128)} %bitcast.where, f32[128,1,128]{2,1,0:T(1,128)S(1)} %all-to-all-done.3.sums, f32[2,5,2,128,128]{4,3,2,1,0:T(8,128)} %collective-permute-done.1.below, f32[5,2,128,128]{3,2,1,0:T(8,128)S(1)} %copy-done.2, ...), custom_call_target="tpu_custom_call" | custom-call | flops 30000000 | bytes 8000000 | tf_op jit(solution)/shard_map/final/pallas_call | solution.py:485
  (15 shorter events, 0.0 us)
Async XLA Ops:
  6.5 44.6 %copy-start.7 = (f32[32,8,128]{2,1,0:T(8,128)S(1)}, f32[32,8,128]{2,1,0:T(8,128)}, u32[]{:S(2)}) copy-start(f32[32,8,128]{2,1,0:T(8,128)} %constant.23.clone.rho_ref) | copy-start | bytes 393220
  6.5 44.6 %all-to-all-start = ((f32[32,2,2,5,8,128]{5,4,3,2,1,0:T(8,128)}), f32[32,2,2,5,8,128]{5,4,3,2,1,0:T(8,128)S(1)}, u32[]{:S(2)}, u32[]{:S(2)}) async-start(f32[32,2,2,5,8,128]{5,4,3,2,1,0:T(8,128)} %get-tuple-element.14), calls=%async_computation | async-start | bytes 5242880 | tf_op jit(solution)/shard_map/all_to_all | solution.py:503
  52.2 23.9 %copy-start = (f32[32,5,2,8,128]{4,3,2,1,0:T(8,128)}, f32[32,5,2,8,128]{4,3,2,1,0:T(8,128)S(1)}, u32[]{:S(2)}) copy-start(f32[32,5,2,8,128]{4,3,2,1,0:T(8,128)S(1)} %get-tuple-element.18) | copy-start | bytes 3932164
  76.1 21.5 %all-to-all-start.2 = ((f32[32,5,2,8,128]{4,3,2,1,0:T(8,128)}), f32[32,5,2,8,128]{4,3,2,1,0:T(8,128)}, u32[]{:S(2)}, u32[]{:S(2)}) async-start(f32[32,5,2,8,128]{4,3,2,1,0:T(8,128)} %copy-done), calls=%async_computation.2 | async-start | bytes 2621440 | tf_op jit(solution)/shard_map/all_to_all | solution.py:506
  86.1 0.8 copy-start.1
  86.9 0.8 copy-start.3
  103.2 35.8 %copy-start.8 = (s32[4]{0:T(128)S(1)}, s32[4]{0:T(128)}, u32[]{:S(2)}) copy-start(s32[4]{0:T(128)} %centre.1) | copy-start | bytes 52
  103.2 35.8 %copy-start.9 = (f32[4]{0:T(128)S(1)}, f32[4]{0:T(128)}, u32[]{:S(2)}) copy-start(f32[4]{0:T(128)} %positions.1) | copy-start | bytes 52
  103.2 35.8 %collective-permute-start.1 = (f32[2,5,2,128,128]{4,3,2,1,0:T(8,128)S(1)}, f32[2,5,2,128,128]{4,3,2,1,0:T(8,128)}, u32[]{:S(2)}, u32[]{:S(2)}) collective-permute-start(f32[2,5,2,128,128]{4,3,2,1,0:T(8,128)S(1)} %get-tuple-element.21.upper), channel_id=1, source_target_pairs={{0,32},{32,64},{64,96},{1,33},{33,65},{65,97},{2,34},{34,66},{66,9... | collective-permute-start | bytes 3932168 | tf_op jit(solution)/shard_map/ppermute | solution.py:511
  111.3 13.6 %collective-permute-start = (f32[5,2,128,128]{3,2,1,0:T(8,128)}, f32[5,2,128,128]{3,2,1,0:T(8,128)S(1)}, u32[]{:S(2)}, u32[]{:S(2)}) collective-permute-start(f32[5,2,128,128]{3,2,1,0:T(8,128)} %copy-done.1), channel_id=1, source_target_pairs={{32,0},{64,32},{96,64},{33,1},{65,33},{97,65},{34,2},{66,34},{98,6... | collective-permute-start | bytes 1966088 | tf_op jit(solution)/shard_map/ppermute | solution.py:508
  113.2 18.7 %collective-permute-start.2 = (f32[5,2,128,128]{3,2,1,0:T(8,128)}, f32[5,2,128,128]{3,2,1,0:T(8,128)S(1)}, u32[]{:S(2)}, u32[]{:S(2)}) collective-permute-start(f32[5,2,128,128]{3,2,1,0:T(8,128)} %copy-done.3), channel_id=1, source_target_pairs={{32,0},{64,32},{96,64},{33,1},{65,33},{97,65},{34,2},{66,34},{98,6... | collective-permute-start | bytes 1966088 | tf_op jit(solution)/shard_map/ppermute | solution.py:510
  125.7 13.2 %all-to-all-start.3 = ((f32[128,1,128]{2,1,0:T(1,128)}), f32[128,1,128]{2,1,0:T(1,128)S(1)}, u32[]{:S(2)}, u32[]{:S(2)}) async-start(f32[128,1,128]{2,1,0:T(1,128)} %edge.1), calls=%async_computation.3 | async-start | bytes 131072 | tf_op jit(solution)/shard_map/all_to_all | solution.py:513
  131.9 0.8 copy-start.5
  139.0 1.1 copy-start.2
  140.1 1.1 copy-start.4
  141.1 1.1 copy-start.6

commit v6 on v4

--- a/solution.py
+++ b/solution.py
@@ -18,6 +18,7 @@
 SMOOTH = 64.0
 EPS = 1e-6
 KEEP = 1.0 - 1.0 / SMOOTH
+SLOTS = 5
 FORWARD_MIB = 60
 SOLVE_MIB = 16
 INVERSE_MIB = 8
@@ -260,12 +261,10 @@
         sums[...] = jnp.zeros_like(sums)
     first = lax.broadcasted_iota(jnp.int32, (16, 8, 128), 1) < 4
 
-    @pl.loop(0, 5)
-    def _(c):
-        weight = jnp.where(c == 0, 0.5, jnp.where(c == 3, -0.5, jnp.where(c == 2, 0.25, -0.25)))
-        weight = weight * (1.0 / SMOOTH)
-        other = jnp.where(c == 1, 0.25 / SMOOTH, 0.0)
-        source = jnp.where(c == 1, 0, jnp.where(c == 2, 4, jnp.where(c == 4, 2, 1)))
+    mixes = ((1, 0.5), (0, -0.25), (4, 0.25), (1, -0.5), (2, -0.25))
+    for c in range(5):
+        source, weight = mixes[c]
+        weight = weight / SMOOTH
         if start is not None:
             last = (start[c, 0], start[c, 1])
         for n, image in enumerate(chosen):
@@ -275,13 +274,16 @@
             w_odd = spec[16:32, pair, c, 1] + keep[pair, c, 16:32]
             if i == 1:
                 p_even, p_odd, w_even, w_odd = p_odd, p_even, w_odd, w_even
-            push(stack, n, 0, jnp.where(first, w_even, w_odd).reshape(128, 128))
-            push(stack, n, 1, jnp.where(first, p_even, p_odd).reshape(128, 128))
-            both = jnp.dot(tx[i], stack[n], preferred_element_type=F32)
+            slot = (c * len(chosen) + n) % SLOTS
+            push(stack, slot, 0, jnp.where(first, w_even, w_odd).reshape(128, 128))
+            push(stack, slot, 1, jnp.where(first, p_even, p_odd).reshape(128, 128))
+            both = jnp.dot(tx[i], stack[slot], preferred_element_type=F32)
             even = KEEP * img[image, c, 0] + times_right(both[:, :128], ty[...])
             odd = times_right(both[:, 128:], ty[...])
-            odd = KEEP * img[image, c, 1] + odd * (1.0 / SMOOTH)
-            odd = odd + (weight * img[image, source, 1] + other * img[image, 3, 1])
+            mix = img[image, source, 1]
+            if c == 1:
+                mix = mix - img[image, 3, 1]
+            odd = KEEP * img[image, c, 1] + odd * (1.0 / SMOOTH) + weight * mix
             out[n][c, 0] = even
             out[n][c, 1] = odd
             if start is not None:
@@ -303,51 +305,87 @@
 
 
 def final_kernel(
-    centre, positions, where, sums, below, s0, s1, upper, a0, a1, out, weights
+    centre,
+    positions,
+    where,
+    sums,
+    below_hbm,
+    s0,
+    s1,
+    upper,
+    a0,
+    a1_hbm,
+    out_hbm,
+    below,
+    a1,
+    out,
+    below_sem,
+    a1_sem,
+    out_sem,
 ):
-    @pl.when(pl.program_id(0) == 0)
-    def _():
-        arc = [jnp.zeros((8, 128), F32)]
-        lane = lax.broadcasted_iota(jnp.int32, (1, 128), 1)
-        for k in range(LOCAL):
-            block = jnp.sum(sums[k * GROUPS : (k + 1) * GROUPS], axis=0)
-            dist = jnp.sqrt(block * (1.0 / CELLS) + EPS)
-            for g in range(4):
-                if k * 4 + g < IMAGES - 1:
-                    value = jnp.sum(jnp.where(lane == g, dist, 0.0), axis=1, keepdims=True)
-                    arc.append(arc[-1] + jnp.broadcast_to(value, (8, 128)))
-        base = where[0] * LOCAL - 2
-        for m in range(LOCAL):
-            c = centre[m]
-            tau = positions[m] * arc[-1]
-
-            def pick(index):
-                value = arc[0]
-                for j in range(1, IMAGES):
-                    value = jnp.where(index == j, arc[j], value)
-                return value
-
-            a, b, d = pick(c - 1), pick(c), pick(c + 1)
-            w = (
-                (tau - b) * (tau - d) / ((a - b) * (a - d)),
-                (tau - a) * (tau - d) / ((b - a) * (b - d)),
-                (tau - a) * (tau - b) / ((d - a) * (d - b)),
-            )
-            for r in range(5):
-                spot = base + m + r
-                value = jnp.zeros((8, 128), F32)
-                for n in range(3):
-                    value = jnp.where(c - 1 + n == spot, w[n], value)
-                weights[m, r] = value
-
-    c = pl.program_id(0)
-    pieces = [below[0, 0], below[1, 0], s0[c], s1[c], upper[0, c], upper[1, c], a0[c], a1[0]]
-    pieces = [p.reshape(32, 8, 128) for p in pieces]
+    def fetch_below(c):
+        return pltpu.make_async_copy(below_hbm.at[:, c], below.at[c], below_sem.at[c])
+
+    def fetch_a1(c):
+        return pltpu.make_async_copy(a1_hbm.at[c], a1.at[c], a1_sem.at[c])
+
+    def store(c):
+        return pltpu.make_async_copy(out.at[c], out_hbm.at[:, c], out_sem.at[c])
+
+    for c in range(5):
+        fetch_below(c).start()
+        fetch_a1(c).start()
+    arc = [jnp.zeros((8, 128), F32)]
+    lane = lax.broadcasted_iota(jnp.int32, (1, 128), 1)
+    for k in range(LOCAL):
+        block = jnp.sum(sums[k * GROUPS : (k + 1) * GROUPS], axis=0)
+        dist = jnp.sqrt(block * (1.0 / CELLS) + EPS)
+        for g in range(4):
+            if k * 4 + g < IMAGES - 1:
+                value = jnp.sum(jnp.where(lane == g, dist, 0.0), axis=1, keepdims=True)
+                arc.append(arc[-1] + jnp.broadcast_to(value, (8, 128)))
+    base = where[0] * LOCAL - 2
+    weights = {}
     for m in range(LOCAL):
-        acc = pieces[m] * weights[m, 0][None]
-        for r in range(1, 5):
-            acc = acc + pieces[m + r] * weights[m, r][None]
-        out[m, 0] = acc.reshape(2, 128, 128)
+        c = centre[m]
+        tau = positions[m] * arc[-1]
+
+        def pick(index):
+            value = arc[0]
+            for j in range(1, IMAGES):
+                value = jnp.where(index == j, arc[j], value)
+            return value
+
+        a, b, d = pick(c - 1), pick(c), pick(c + 1)
+        w = (
+            (tau - b) * (tau - d) / ((a - b) * (a - d)),
+            (tau - a) * (tau - d) / ((b - a) * (b - d)),
+            (tau - a) * (tau - b) / ((d - a) * (d - b)),
+        )
+        for r in range(5):
+            spot = base + m + r
+            value = jnp.zeros((8, 128), F32)
+            for n in range(3):
+                value = jnp.where(c - 1 + n == spot, w[n], value)
+            weights[m, r] = value
+
+    for c in range(5):
+        fetch_below(c).wait()
+        fetch_a1(c).wait()
+        lines = [below.at[c, 0], below.at[c, 1], s0.at[c], s1.at[c]]
+        lines += [upper.at[0, c], upper.at[1, c], a0.at[c], a1.at[c]]
+        for zz in range(2):
+            for n in range(16):
+                rows = slice(8 * n, 8 * n + 8)
+                pieces = [line[zz, rows] for line in lines]
+                for m in range(LOCAL):
+                    acc = pieces[m] * weights[m, 0]
+                    for r in range(1, 5):
+                        acc = acc + pieces[m + r] * weights[m, r]
+                    out[c, m, zz, rows] = acc
+        store(c).start()
+    for c in range(5):
+        store(c).wait()
 
 
 def whole(shape):
@@ -356,6 +394,7 @@
 
 SMEM = pl.BlockSpec(memory_space=pltpu.SMEM)
 VMEM = pl.BlockSpec(memory_space=pltpu.VMEM)
+HBM = pl.BlockSpec(memory_space=pltpu.HBM)
 
 
 def plain(mib):
@@ -438,7 +477,7 @@
         out_shape=out_shape,
         in_specs=[VMEM] * len(args),
         out_specs=(VMEM,) * len(out_shape),
-        scratch_shapes=[pltpu.VMEM((count, 384, 256), BF16)],
+        scratch_shapes=[pltpu.VMEM((SLOTS, 384, 256), BF16)],
         compiler_params=plain(INVERSE_MIB),
         cost_estimate=cost(1_000_000_000 * count, 3_000_000 * count),
         name="inverse",
@@ -458,18 +497,22 @@
 
 
 def final(centre, positions, sums, below, s0, s1, upper, a0, a1):
-    pair = pl.BlockSpec((2, 1, 2, 128, 128), lambda c: (0, c, 0, 0, 0))
-    one = pl.BlockSpec((1, 2, 128, 128), lambda c: (c, 0, 0, 0))
     where = lax.axis_index("img").astype(jnp.int32).reshape(1)
     return pl.pallas_call(
         final_kernel,
         out_shape=jax.ShapeDtypeStruct((4, 5, 2, 128, 128), F32),
-        grid=(5,),
-        in_specs=[SMEM, SMEM, SMEM, VMEM, pair, VMEM, VMEM, VMEM, VMEM, one],
-        out_specs=pl.BlockSpec((4, 1, 2, 128, 128), lambda c: (0, c, 0, 0, 0)),
-        scratch_shapes=[pltpu.VMEM((4, 5, 8, 128), F32)],
-        compiler_params=params(FINAL_MIB),
-        cost_estimate=cost(30000000, 8000000),
+        in_specs=[SMEM, SMEM, SMEM, VMEM, HBM, VMEM, VMEM, VMEM, VMEM, HBM],
+        out_specs=HBM,
+        scratch_shapes=[
+            pltpu.VMEM((5, 2, 2, 128, 128), F32),
+            pltpu.VMEM((5, 2, 128, 128), F32),
+            pltpu.VMEM((5, 4, 2, 128, 128), F32),
+            pltpu.SemaphoreType.DMA((5,)),
+            pltpu.SemaphoreType.DMA((5,)),
+            pltpu.SemaphoreType.DMA((5,)),
+        ],
+        compiler_params=plain(FINAL_MIB),
+        cost_estimate=cost(30_000_000, 8_000_000),
         name="final",
     )(centre, positions, where, sums, below, s0, s1, upper, a0, a1)
 

time: 135 us -> 131 us (0.970)
  Pallas kernels: 18.7 us -> 14.9 us
    pallas_call x2, Pallas kernels: 4.87 us -> 2.82 us  [inverse(): pl.pallas_call(functools.partial(inverse_kernel, chosen=chosen), out_shap...]
    pallas_call x1, Pallas kernels: 5.33 us -> 3.61 us  [final(): pl.pallas_call(final_kernel, out_shape=jax.ShapeDtypeStruct((4, 5, 2, 128...]
where the time goes in v6:
time: 131 us; the launch traced here: 130 us
  waiting for transfers between devices  53.4 us (41%)
  blocking collectives  37.5 us (29%)
  starting transfers between devices  24.4 us (19%)
  Pallas kernels  14.9 us (11%)
    all_to_all x1, blocking collectives, local(): u = lax.all_to_all(u, 'gz', 0, 0, tiled=True)  37.5 us
    all_to_all x1, waiting for transfers between devices, local(): f = lax.all_to_all(f, 'gz', 0, 0, tiled=True)  34.7 us
    all_to_all x1, starting transfers between devices, local(): f = lax.all_to_all(f, 'gz', 0, 0, tiled=True)  9.84 us
    ppermute x1, waiting for transfers between devices, local(): a0 = lax.ppermute(s0, 'img', rows_back)  9.55 us
    ppermute x1, starting transfers between devices, local(): below = lax.ppermute(upper, 'img', rows)  7.19 us
    pallas_call x1, Pallas kernels, forward(): pl.pallas_call(forward_kernel, out_shape=(jax.ShapeDtypeStruct((GROUPS, 2...  6.52 us
    all_to_all x1, waiting for transfers between devices, local(): sums = lax.all_to_all(part, ('img', 'gz'), 0, 0, tiled=True)  6.26 us
    pallas_call x1, Pallas kernels, final(): pl.pallas_call(final_kernel, out_shape=jax.ShapeDtypeStruct((4, 5, 2, 128...  3.61 us
  transfers between devices with their start and end apart: 5, of which 4 were waited for; matrix products, arithmetic and copies ran while one was open for 0% of the time, Pallas kernels for 1%

profile of v6, /device:TPU:1, one launch (start us, length us, event | category | flops | bytes accessed | tf_op | source)
XLA Modules:
  0.0 130.3 jit_solution(9308661943361650539)
XLA Ops:
  0.0 6.5 %forward.1 = (f32[32,2,2,5,8,128]{5,4,3,2,1,0:T(8,128)}, f32[2,5,32,8,128]{4,3,2,1,0:T(8,128)}) custom-call(f32[4,5,2,128,128]{4,3,2,1,0:T(8,128)} %refs_2_.3, bf16[256,256]{1,0:T(8,128)(2,1)} %constant.19.clone.ty, bf16[2,128,384]{2,1,0:T(8,128)(2,1)} %constant.21.clone.tx, f32[32,8,128]{2,1,0:T(8,128)} %constant.23.clone.rho_ref), custom_call_target="tpu_custom_call" | custom-call | flops 3000000000 | bytes 9000000 | tf_op jit(solution)/shard_map/forward/pallas_call | solution.py:415
  6.5 9.8 %all-to-all-start = ((f32[32,2,2,5,8,128]{5,4,3,2,1,0:T(8,128)}), f32[32,2,2,5,8,128]{5,4,3,2,1,0:T(8,128)S(1)}, u32[]{:S(2)}, u32[]{:S(2)}) async-start(f32[32,2,2,5,8,128]{5,4,3,2,1,0:T(8,128)} %get-tuple-element.10), calls=%async_computation | async-start | bytes 5242880 | tf_op jit(solution)/shard_map/all_to_all | solution.py:525
  16.4 34.7 %all-to-all-done.f = f32[32,2,2,5,8,128]{5,4,3,2,1,0:T(8,128)S(1)} async-done(((f32[32,2,2,5,8,128]{5,4,3,2,1,0:T(8,128)}), f32[32,2,2,5,8,128]{5,4,3,2,1,0:T(8,128)S(1)}, u32[]{:S(2)}, u32[]{:S(2)}) %all-to-all-start) | async-done | bytes 2621472 | tf_op jit(solution)/shard_map/all_to_all | solution.py:525
  51.1 1.1 solve.1
  52.2 0.0 copy-start
  52.2 0.0 copy-start.2
  52.3 0.0 copy-start.3
  52.3 37.5 %all_to_all.15.refs_0_ = f32[32,2,5,2,8,128]{5,4,3,2,1,0:T(8,128)S(1)} all-to-all(f32[32,2,5,2,8,128]{5,4,3,2,1,0:T(8,128)S(1)} %solve.1), channel_id=1, replica_groups=mesh['img'=4,'gz'=32] {'gz'}, dimensions={0} | all-to-all | bytes 5242880 | tf_op jit(solution)/shard_map/all_to_all | solution.py:527
  89.7 0.0 copy-done
  89.7 0.0 copy-done.2
  89.8 0.7 inverse.2.refs_5_.s0
  90.5 0.0 copy-start.5
  90.5 0.0 copy-start.6
  90.5 2.1 %inverse.3 = (f32[5,2,128,128]{3,2,1,0:T(8,128)S(1)}, f32[2,5,2,128,128]{4,3,2,1,0:T(8,128)S(1)}, f32[3,8,128]{2,1,0:T(8,128)S(1)}) custom-call(f32[32,2,5,2,8,128]{5,4,3,2,1,0:T(8,128)S(1)} %all_to_all.15.refs_0_, f32[2,5,32,8,128]{4,3,2,1,0:T(8,128)S(1)} %copy-done.1, f32[4,5,2,128,128]{4,3,2,1,0:T(8,128)S(1)} %copy-done, bf16[256,256]{1,0:T(8,128)(2,1)S(1)} %copy-done.3, ...), custom_call_target="tpu_custom_call" | custom-call | flops 3000000000 | bytes 9000000 | tf_op jit(solution)/shard_map/inverse/pallas_call | solution.py:475
  92.6 7.2 %collective-permute-start.1 = (f32[2,5,2,128,128]{4,3,2,1,0:T(8,128)S(1)}, f32[2,5,2,128,128]{4,3,2,1,0:T(8,128)}, u32[]{:S(2)}, u32[]{:S(2)}) collective-permute-start(f32[2,5,2,128,128]{4,3,2,1,0:T(8,128)S(1)} %get-tuple-element.13.upper), channel_id=1, source_target_pairs={{0,32},{32,64},{64,96},{1,33},{33,65},{65,97},{2,34},{34,66},{66,9... | collective-permute-start | bytes 3932168 | tf_op jit(solution)/shard_map/ppermute | solution.py:532
  99.8 1.9 %collective-permute-start = (f32[5,2,128,128]{3,2,1,0:T(8,128)S(1)}, f32[5,2,128,128]{3,2,1,0:T(8,128)S(1)}, u32[]{:S(2)}, u32[]{:S(2)}) collective-permute-start(f32[5,2,128,128]{3,2,1,0:T(8,128)S(1)} %inverse.2.refs_5_.s0), channel_id=1, source_target_pairs={{32,0},{64,32},{96,64},{33,1},{65,33},{97,65},{34,2},{66,34},{98,6... | collective-permute-start | bytes 1966088 | tf_op jit(solution)/shard_map/ppermute | solution.py:529
  101.7 1.9 %collective-permute-start.2 = (f32[5,2,128,128]{3,2,1,0:T(8,128)S(1)}, f32[5,2,128,128]{3,2,1,0:T(8,128)}, u32[]{:S(2)}, u32[]{:S(2)}) collective-permute-start(f32[5,2,128,128]{3,2,1,0:T(8,128)S(1)} %get-tuple-element.14.s1), channel_id=1, source_target_pairs={{32,0},{64,32},{96,64},{33,1},{65,33},{97,65},{34,2},{66,34},{98,6... | collective-permute-start | bytes 1966088 | tf_op jit(solution)/shard_map/ppermute | solution.py:531
  103.7 9.6 %collective-permute-done.above.a0 = f32[5,2,128,128]{3,2,1,0:T(8,128)S(1)} collective-permute-done((f32[5,2,128,128]{3,2,1,0:T(8,128)S(1)}, f32[5,2,128,128]{3,2,1,0:T(8,128)S(1)}, u32[]{:S(2)}, u32[]{:S(2)}) %collective-permute-start) | collective-permute-done | bytes 655392 | tf_op jit(solution)/shard_map/ppermute | solution.py:529
  113.2 0.9 edge.1
  114.1 3.5 %all-to-all-start.2 = ((f32[128,1,128]{2,1,0:T(1,128)}), f32[128,1,128]{2,1,0:T(1,128)S(1)}, u32[]{:S(2)}, u32[]{:S(2)}) async-start(f32[128,1,128]{2,1,0:T(1,128)} %edge.1), calls=%async_computation.2 | async-start | bytes 131072 | tf_op jit(solution)/shard_map/all_to_all | solution.py:534
  117.6 2.8 %collective-permute-done.2.a1_hbm = f32[5,2,128,128]{3,2,1,0:T(8,128)} collective-permute-done((f32[5,2,128,128]{3,2,1,0:T(8,128)S(1)}, f32[5,2,128,128]{3,2,1,0:T(8,128)}, u32[]{:S(2)}, u32[]{:S(2)}) %collective-permute-start.2) | collective-permute-done | bytes 655392 | tf_op jit(solution)/shard_map/ppermute | solution.py:531
  120.4 6.3 %all-to-all-done.2.sums = f32[128,1,128]{2,1,0:T(1,128)S(1)} async-done(((f32[128,1,128]{2,1,0:T(1,128)}), f32[128,1,128]{2,1,0:T(1,128)S(1)}, u32[]{:S(2)}, u32[]{:S(2)}) %all-to-all-start.2) | async-done | bytes 65568 | tf_op jit(solution)/shard_map/all_to_all | solution.py:534
  126.7 0.0 collective-permute-done.1.below_hbm
  126.7 3.6 %final.1 = f32[4,5,2,128,128]{4,3,2,1,0:T(8,128)} custom-call(s32[4]{0:T(128)S(1)} %copy-done.5, f32[4]{0:T(128)S(1)} %copy-done.6, s32[1]{0:T(128)} %bitcast.where, f32[128,1,128]{2,1,0:T(1,128)S(1)} %all-to-all-done.2.sums, f32[2,5,2,128,128]{4,3,2,1,0:T(8,128)} %collective-permute-done.1.below_hbm, f32[5,2,128,128]{3,2,1,0:T(8,128)S(1)} %inverse.2.refs_5_.s0, ...), custom_call_target="tpu_custom_call" | custom-call | flops 30000000 | bytes 8000000 | tf_op jit(solution)/shard_map/final/pallas_call | solution.py:501
  (7 shorter events, 0.0 us)
Async XLA Ops:
  6.5 44.6 %copy-start.4 = (f32[32,8,128]{2,1,0:T(8,128)S(1)}, f32[32,8,128]{2,1,0:T(8,128)}, u32[]{:S(2)}) copy-start(f32[32,8,128]{2,1,0:T(8,128)} %constant.23.clone.rho_ref) | copy-start | bytes 393220
  6.5 44.6 %all-to-all-start = ((f32[32,2,2,5,8,128]{5,4,3,2,1,0:T(8,128)}), f32[32,2,2,5,8,128]{5,4,3,2,1,0:T(8,128)S(1)}, u32[]{:S(2)}, u32[]{:S(2)}) async-start(f32[32,2,2,5,8,128]{5,4,3,2,1,0:T(8,128)} %get-tuple-element.10), calls=%async_computation | async-start | bytes 5242880 | tf_op jit(solution)/shard_map/all_to_all | solution.py:525
  52.2 37.5 %copy-start = (f32[4,5,2,128,128]{4,3,2,1,0:T(8,128)S(1)}, f32[4,5,2,128,128]{4,3,2,1,0:T(8,128)}, u32[]{:S(2)}) copy-start(f32[4,5,2,128,128]{4,3,2,1,0:T(8,128)} %refs_2_.3) | copy-start | bytes 7864324
  52.2 37.5 %copy-start.1 = (f32[2,5,32,8,128]{4,3,2,1,0:T(8,128)S(1)}, f32[2,5,32,8,128]{4,3,2,1,0:T(8,128)}, u32[]{:S(2)}) copy-start(f32[2,5,32,8,128]{4,3,2,1,0:T(8,128)} %get-tuple-element.11.refs_1_) | copy-start | bytes 3932164
  52.2 37.5 %copy-start.2 = (bf16[2,128,384]{2,1,0:T(8,128)(2,1)S(1)}, bf16[2,128,384]{2,1,0:T(8,128)(2,1)}, u32[]{:S(2)}) copy-start(bf16[2,128,384]{2,1,0:T(8,128)(2,1)} %constant.22.clone.refs_4_) | copy-start | bytes 589828
  52.3 37.5 %copy-start.3 = (bf16[256,256]{1,0:T(8,128)(2,1)S(1)}, bf16[256,256]{1,0:T(8,128)(2,1)}, u32[]{:S(2)}) copy-start(bf16[256,256]{1,0:T(8,128)(2,1)} %constant.20.clone.refs_3_) | copy-start | bytes 393220
  90.5 36.2 %copy-start.5 = (s32[4]{0:T(128)S(1)}, s32[4]{0:T(128)}, u32[]{:S(2)}) copy-start(s32[4]{0:T(128)} %centre.1) | copy-start | bytes 52
  90.5 36.2 %copy-start.6 = (f32[4]{0:T(128)S(1)}, f32[4]{0:T(128)}, u32[]{:S(2)}) copy-start(f32[4]{0:T(128)} %positions.1) | copy-start | bytes 52
  92.6 34.1 %collective-permute-start.1 = (f32[2,5,2,128,128]{4,3,2,1,0:T(8,128)S(1)}, f32[2,5,2,128,128]{4,3,2,1,0:T(8,128)}, u32[]{:S(2)}, u32[]{:S(2)}) collective-permute-start(f32[2,5,2,128,128]{4,3,2,1,0:T(8,128)S(1)} %get-tuple-element.13.upper), channel_id=1, source_target_pairs={{0,32},{32,64},{64,96},{1,33},{33,65},{65,97},{2,34},{34,66},{66,9... | collective-permute-start | bytes 3932168 | tf_op jit(solution)/shard_map/ppermute | solution.py:532
  99.8 13.4 %collective-permute-start = (f32[5,2,128,128]{3,2,1,0:T(8,128)S(1)}, f32[5,2,128,128]{3,2,1,0:T(8,128)S(1)}, u32[]{:S(2)}, u32[]{:S(2)}) collective-permute-start(f32[5,2,128,128]{3,2,1,0:T(8,128)S(1)} %inverse.2.refs_5_.s0), channel_id=1, source_target_pairs={{32,0},{64,32},{96,64},{33,1},{65,33},{97,65},{34,2},{66,34},{98,6... | collective-permute-start | bytes 1966088 | tf_op jit(solution)/shard_map/ppermute | solution.py:529
  101.7 18.7 %collective-permute-start.2 = (f32[5,2,128,128]{3,2,1,0:T(8,128)S(1)}, f32[5,2,128,128]{3,2,1,0:T(8,128)}, u32[]{:S(2)}, u32[]{:S(2)}) collective-permute-start(f32[5,2,128,128]{3,2,1,0:T(8,128)S(1)} %get-tuple-element.14.s1), channel_id=1, source_target_pairs={{32,0},{64,32},{96,64},{33,1},{65,33},{97,65},{34,2},{66,34},{98,6... | collective-permute-start | bytes 1966088 | tf_op jit(solution)/shard_map/ppermute | solution.py:531
  114.1 12.6 %all-to-all-start.2 = ((f32[128,1,128]{2,1,0:T(1,128)}), f32[128,1,128]{2,1,0:T(1,128)S(1)}, u32[]{:S(2)}, u32[]{:S(2)}) async-start(f32[128,1,128]{2,1,0:T(1,128)} %edge.1), calls=%async_computation.2 | async-start | bytes 131072 | tf_op jit(solution)/shard_map/all_to_all | solution.py:534

commit v7 on v6

--- a/solution.py
+++ b/solution.py
@@ -19,7 +19,7 @@
 EPS = 1e-6
 KEEP = 1.0 - 1.0 / SMOOTH
 SLOTS = 5
-FORWARD_MIB = 60
+FORWARD_MIB = 56
 SOLVE_MIB = 16
 INVERSE_MIB = 8
 EDGE_MIB = 4
@@ -152,7 +152,9 @@
     stack[slot, 256:384, cols] = h
 
 
-def forward_kernel(img, ty, tx, rho_ref, out, keep, stack, spectrum):
+def forward_kernel(where, img, ty, tx, rho_ref, out, keep, mine, stack, spectrum):
+    pair = pl.program_id(0)
+    mine[...] = rho_ref[where[0]]
     for i in range(2):
         qe = [img[i, c, 0] for c in range(5)]
         qo = [img[i, c, 1] for c in range(5)]
@@ -190,14 +192,13 @@
         ks = add_spread(ys, g, 1.0)
         for c in range(5):
             y = ys[c]
-            out[rows, 0, 0, c] = beta * tile(c, 1) + y
-            out[rows, 1, 0, c] = ks[c]
+            out[rows, 0, pair, c] = beta * tile(c, 1) + y
+            out[rows, 1, pair, c] = ks[c]
             keep[0, c, rows] = back * y
 
 
-def solve_kernel(where, f, rho_ref, out, right, work):
-    del where
-    rho = rho_ref[0]
+def solve_kernel(f, rho_ref, out, right, work):
+    rho = rho_ref[...]
     sigma = rho * rho
     power = sigma
     for _ in range(5):
@@ -412,22 +413,26 @@
 
 
 def forward(images, ty, tx, rho):
+    where = lax.axis_index("gz").astype(jnp.int32).reshape(1)
     return pl.pallas_call(
         forward_kernel,
         out_shape=(
-            jax.ShapeDtypeStruct((GROUPS, 2, 2, 5, 8, 128), F32),
+            pltpu.VMEM((GROUPS, 2, 2, 5, 8, 128), F32),
             jax.ShapeDtypeStruct((2, 5, GROUPS, 8, 128), F32),
+            pltpu.VMEM((8, 128), F32),
         ),
         grid=(2,),
         in_specs=[
+            SMEM,
             pl.BlockSpec((2, 5, 2, 128, 128), lambda p: (p, 0, 0, 0, 0)),
             whole((256, 256)),
             whole((2, 128, 384)),
             whole((GROUPS, 8, 128)),
         ],
         out_specs=(
-            pl.BlockSpec((GROUPS, 2, 1, 5, 8, 128), lambda p: (0, 0, p, 0, 0, 0)),
+            VMEM,
             pl.BlockSpec((1, 5, GROUPS, 8, 128), lambda p: (p, 0, 0, 0, 0)),
+            VMEM,
         ),
         scratch_shapes=[
             pltpu.VMEM((7, 384, 256), BF16),
@@ -436,32 +441,23 @@
         compiler_params=params(FORWARD_MIB),
         cost_estimate=cost(3000000000, 9000000),
         name="forward",
-    )(images, ty, tx, rho)
+    )(where, images, ty, tx, rho)
 
 
 def solve(f, rho):
-    where = lax.axis_index("gz").astype(jnp.int32).reshape(1)
-    result = (GROUPS, 2, 5, 2, 8, 128)
     return pl.pallas_call(
         solve_kernel,
-        out_shape=pltpu.VMEM(result, F32),
-        grid_spec=pltpu.PrefetchScalarGridSpec(
-            num_scalar_prefetch=1,
-            grid=(1,),
-            in_specs=[
-                VMEM,
-                pl.BlockSpec((1, 8, 128), lambda i, w: (w[0], 0, 0)),
-            ],
-            out_specs=VMEM,
-            scratch_shapes=[
-                pltpu.VMEM((GROUPS, 2, 5, 8, 128), F32),
-                pltpu.VMEM((GROUPS, 2, 5, 8, 128), F32),
-            ],
-        ),
-        compiler_params=params(SOLVE_MIB),
-        cost_estimate=cost(20000000, 6000000),
+        out_shape=pltpu.VMEM((GROUPS, 2, 5, 2, 8, 128), F32),
+        in_specs=[VMEM, VMEM],
+        out_specs=VMEM,
+        scratch_shapes=[
+            pltpu.VMEM((GROUPS, 2, 5, 8, 128), F32),
+            pltpu.VMEM((GROUPS, 2, 5, 8, 128), F32),
+        ],
+        compiler_params=plain(SOLVE_MIB),
+        cost_estimate=cost(20_000_000, 6_000_000),
         name="solve",
-    )(where, f, rho)
+    )(f, rho)
 
 
 def inverse(chosen, spec, keep, images, ty, tx, *start):
@@ -487,7 +483,7 @@
 def edge(sums, upper, above):
     return pl.pallas_call(
         edge_kernel,
-        out_shape=jax.ShapeDtypeStruct((128, 1, 128), F32),
+        out_shape=pltpu.VMEM((128, 1, 128), F32),
         in_specs=[VMEM] * 3,
         out_specs=VMEM,
         compiler_params=plain(EDGE_MIB),
@@ -521,9 +517,9 @@
     forward_y, inverse_y, forward_x, inverse_x, rho = (jnp.asarray(t) for t in tables())
     rows = [(i, i + 1) for i in range(LOCAL - 1)]
     rows_back = [(b, a) for a, b in rows]
-    f, keep = forward(images, forward_y, forward_x, rho)
+    f, keep, mine = forward(images, forward_y, forward_x, rho)
     f = lax.all_to_all(f, "gz", 0, 0, tiled=True)
-    u = solve(f, rho)
+    u = solve(f, mine)
     u = lax.all_to_all(u, "gz", 0, 0, tiled=True)
     (s0,) = inverse((0,), u, keep, images, inverse_y, inverse_x)
     a0 = lax.ppermute(s0, "img", rows_back)

time: 131 us -> 127 us (0.969)
  blocking collectives: 37.5 us -> 78.7 us
  waiting for transfers between devices: 53.4 us -> 18.7 us
  starting transfers between devices: 24.4 us -> 15.1 us
    all_to_all x0 -> x1, blocking collectives: none -> 41.9 us  [local(): f = lax.all_to_all(f, 'gz', 0, 0, tiled=True)]
    all_to_all x1 -> x0, waiting for transfers between devices: 34.7 us -> none  [local(): f = lax.all_to_all(f, 'gz', 0, 0, tiled=True)]
    all_to_all x1 -> x0, starting transfers between devices: 9.84 us -> none  [local(): f = lax.all_to_all(f, 'gz', 0, 0, tiled=True)]
  transfers between devices with their start and end apart: 5 -> 4, of which waited for: 4 -> 3; matrix products, arithmetic and copies ran while one was open for 0% -> 0% of each run, Pallas kernels for 1% -> 1%
where the time goes in v7:
time: 127 us
  blocking collectives  78.7 us (62%)
  waiting for transfers between devices  18.7 us (15%)
  starting transfers between devices  15.1 us (12%)
  Pallas kernels  14.3 us (11%)
    all_to_all x1, blocking collectives, local(): f = lax.all_to_all(f, 'gz', 0, 0, tiled=True)  41.9 us
    all_to_all x1, blocking collectives, local(): u = lax.all_to_all(u, 'gz', 0, 0, tiled=True)  36.8 us
    ppermute x1, waiting for transfers between devices, local(): a0 = lax.ppermute(s0, 'img', rows_back)  9.55 us
    ppermute x1, starting transfers between devices, local(): below = lax.ppermute(upper, 'img', rows)  7.76 us
    all_to_all x1, waiting for transfers between devices, local(): sums = lax.all_to_all(part, ('img', 'gz'), 0, 0, tiled=True)  6.26 us
    pallas_call x1, Pallas kernels, forward(): pl.pallas_call(forward_kernel, out_shape=(pltpu.VMEM((GROUPS, 2, 2, 5, 8,...  6 us
    pallas_call x1, Pallas kernels, final(): pl.pallas_call(final_kernel, out_shape=jax.ShapeDtypeStruct((4, 5, 2, 128...  3.61 us
    all_to_all x1, starting transfers between devices, local(): sums = lax.all_to_all(part, ('img', 'gz'), 0, 0, tiled=True)  3.52 us
  transfers between devices with their start and end apart: 4, of which 3 were waited for; matrix products, arithmetic and copies ran while one was open for 0% of the time, Pallas kernels for 1%

profile of v7, /device:TPU:1, one launch (start us, length us, event | category | flops | bytes accessed | tf_op | source)
XLA Modules:
  0.0 127.0 jit_solution(7424516715853259846)
XLA Ops:
  0.0 6.0 %forward.1 = (f32[32,2,2,5,8,128]{5,4,3,2,1,0:T(8,128)S(1)}, f32[2,5,32,8,128]{4,3,2,1,0:T(8,128)}, f32[8,128]{1,0:T(8,128)S(1)}) custom-call(s32[1]{0:T(128)} %bitcast.1.where, f32[4,5,2,128,128]{4,3,2,1,0:T(8,128)} %refs_2_.3, bf16[256,256]{1,0:T(8,128)(2,1)} %constant.19.clone.ty, bf16[2,128,384]{2,1,0:T(8,128)(2,1)} %constant.21.clone.tx, ...), custom_call_target="tpu_custom_call" | custom-call | flops 3000000000 | bytes 9000000 | tf_op jit(solution)/shard_map/forward/pallas_call | solution.py:417
  6.0 41.9 %all_to_all.15.f = f32[32,2,2,5,8,128]{5,4,3,2,1,0:T(8,128)S(1)} all-to-all(f32[32,2,2,5,8,128]{5,4,3,2,1,0:T(8,128)S(1)} %get-tuple-element.11), channel_id=1, replica_groups=mesh['img'=4,'gz'=32] {'gz'}, dimensions={0} | all-to-all | bytes 5242880 | tf_op jit(solution)/shard_map/all_to_all | solution.py:521
  47.9 1.1 solve.1
  49.0 0.0 copy-start
  49.0 0.0 copy-start.1
  49.0 0.0 copy-start.2
  49.0 0.0 copy-start.3
  49.0 36.8 %all_to_all.16.refs_0_ = f32[32,2,5,2,8,128]{5,4,3,2,1,0:T(8,128)S(1)} all-to-all(f32[32,2,5,2,8,128]{5,4,3,2,1,0:T(8,128)S(1)} %solve.1), channel_id=1, replica_groups=mesh['img'=4,'gz'=32] {'gz'}, dimensions={0} | all-to-all | bytes 5242880 | tf_op jit(solution)/shard_map/all_to_all | solution.py:523
  85.9 0.0 copy-done.2
  85.9 0.0 copy-done.3
  85.9 0.7 inverse.2.refs_5_.s0
  86.6 0.0 copy-start.4
  86.6 0.0 copy-start.5
  86.6 2.0 %inverse.3 = (f32[5,2,128,128]{3,2,1,0:T(8,128)S(1)}, f32[2,5,2,128,128]{4,3,2,1,0:T(8,128)S(1)}, f32[3,8,128]{2,1,0:T(8,128)S(1)}) custom-call(f32[32,2,5,2,8,128]{5,4,3,2,1,0:T(8,128)S(1)} %all_to_all.16.refs_0_, f32[2,5,32,8,128]{4,3,2,1,0:T(8,128)S(1)} %copy-done.1, f32[4,5,2,128,128]{4,3,2,1,0:T(8,128)S(1)} %copy-done, bf16[256,256]{1,0:T(8,128)(2,1)S(1)} %copy-done.3, ...), custom_call_target="tpu_custom_call" | custom-call | flops 3000000000 | bytes 9000000 | tf_op jit(solution)/shard_map/inverse/pallas_call | solution.py:471
  88.6 7.8 %collective-permute-start.1 = (f32[2,5,2,128,128]{4,3,2,1,0:T(8,128)S(1)}, f32[2,5,2,128,128]{4,3,2,1,0:T(8,128)}, u32[]{:S(2)}, u32[]{:S(2)}) collective-permute-start(f32[2,5,2,128,128]{4,3,2,1,0:T(8,128)S(1)} %get-tuple-element.15.upper), channel_id=1, source_target_pairs={{0,32},{32,64},{64,96},{1,33},{33,65},{65,97},{2,34},{34,66},{66,9... | collective-permute-start | bytes 3932168 | tf_op jit(solution)/shard_map/ppermute | solution.py:528
  96.4 1.9 %collective-permute-start = (f32[5,2,128,128]{3,2,1,0:T(8,128)S(1)}, f32[5,2,128,128]{3,2,1,0:T(8,128)S(1)}, u32[]{:S(2)}, u32[]{:S(2)}) collective-permute-start(f32[5,2,128,128]{3,2,1,0:T(8,128)S(1)} %inverse.2.refs_5_.s0), channel_id=1, source_target_pairs={{32,0},{64,32},{96,64},{33,1},{65,33},{97,65},{34,2},{66,34},{98,6... | collective-permute-start | bytes 1966088 | tf_op jit(solution)/shard_map/ppermute | solution.py:525
  98.3 1.9 %collective-permute-start.2 = (f32[5,2,128,128]{3,2,1,0:T(8,128)S(1)}, f32[5,2,128,128]{3,2,1,0:T(8,128)}, u32[]{:S(2)}, u32[]{:S(2)}) collective-permute-start(f32[5,2,128,128]{3,2,1,0:T(8,128)S(1)} %get-tuple-element.16.s1), channel_id=1, source_target_pairs={{32,0},{64,32},{96,64},{33,1},{65,33},{97,65},{34,2},{66,34},{98,6... | collective-permute-start | bytes 1966088 | tf_op jit(solution)/shard_map/ppermute | solution.py:527
  100.3 9.6 %collective-permute-done.above.a0 = f32[5,2,128,128]{3,2,1,0:T(8,128)S(1)} collective-permute-done((f32[5,2,128,128]{3,2,1,0:T(8,128)S(1)}, f32[5,2,128,128]{3,2,1,0:T(8,128)S(1)}, u32[]{:S(2)}, u32[]{:S(2)}) %collective-permute-start) | collective-permute-done | bytes 655392 | tf_op jit(solution)/shard_map/ppermute | solution.py:525
  109.8 0.8 edge.1
  110.7 3.5 %all-to-all-start.2 = ((f32[128,1,128]{2,1,0:T(1,128)}), f32[128,1,128]{2,1,0:T(1,128)S(1)}, u32[]{:S(2)}, u32[]{:S(2)}) async-start(f32[128,1,128]{2,1,0:T(1,128)} %edge.1), calls=%async_computation.2 | async-start | bytes 131072 | tf_op jit(solution)/shard_map/all_to_all | solution.py:530
  114.2 2.9 %collective-permute-done.2.a1_hbm = f32[5,2,128,128]{3,2,1,0:T(8,128)} collective-permute-done((f32[5,2,128,128]{3,2,1,0:T(8,128)S(1)}, f32[5,2,128,128]{3,2,1,0:T(8,128)}, u32[]{:S(2)}, u32[]{:S(2)}) %collective-permute-start.2) | collective-permute-done | bytes 655392 | tf_op jit(solution)/shard_map/ppermute | solution.py:527
  117.1 6.3 %all-to-all-done.2.sums = f32[128,1,128]{2,1,0:T(1,128)S(1)} async-done(((f32[128,1,128]{2,1,0:T(1,128)}), f32[128,1,128]{2,1,0:T(1,128)S(1)}, u32[]{:S(2)}, u32[]{:S(2)}) %all-to-all-start.2) | async-done | bytes 65568 | tf_op jit(solution)/shard_map/all_to_all | solution.py:530
  123.3 0.0 collective-permute-done.1.below_hbm
  123.4 3.6 %final.1 = f32[4,5,2,128,128]{4,3,2,1,0:T(8,128)} custom-call(s32[4]{0:T(128)S(1)} %copy-done.4, f32[4]{0:T(128)S(1)} %copy-done.5, s32[1]{0:T(128)} %bitcast.where, f32[128,1,128]{2,1,0:T(1,128)S(1)} %all-to-all-done.2.sums, f32[2,5,2,128,128]{4,3,2,1,0:T(8,128)} %collective-permute-done.1.below_hbm, f32[5,2,128,128]{3,2,1,0:T(8,128)S(1)} %inverse.2.refs_5_.s0, ...), custom_call_target="tpu_custom_call" | custom-call | flops 30000000 | bytes 8000000 | tf_op jit(solution)/shard_map/final/pallas_call | solution.py:497
  (4 shorter events, 0.0 us)
Async XLA Ops:
  49.0 36.9 %copy-start = (f32[4,5,2,128,128]{4,3,2,1,0:T(8,128)S(1)}, f32[4,5,2,128,128]{4,3,2,1,0:T(8,128)}, u32[]{:S(2)}) copy-start(f32[4,5,2,128,128]{4,3,2,1,0:T(8,128)} %refs_2_.3) | copy-start | bytes 7864324
  49.0 36.8 %copy-start.1 = (f32[2,5,32,8,128]{4,3,2,1,0:T(8,128)S(1)}, f32[2,5,32,8,128]{4,3,2,1,0:T(8,128)}, u32[]{:S(2)}) copy-start(f32[2,5,32,8,128]{4,3,2,1,0:T(8,128)} %get-tuple-element.13.refs_1_) | copy-start | bytes 3932164
  49.0 36.8 %copy-start.2 = (bf16[2,128,384]{2,1,0:T(8,128)(2,1)S(1)}, bf16[2,128,384]{2,1,0:T(8,128)(2,1)}, u32[]{:S(2)}) copy-start(bf16[2,128,384]{2,1,0:T(8,128)(2,1)} %constant.22.clone.refs_4_) | copy-start | bytes 589828
  49.0 36.8 %copy-start.3 = (bf16[256,256]{1,0:T(8,128)(2,1)S(1)}, bf16[256,256]{1,0:T(8,128)(2,1)}, u32[]{:S(2)}) copy-start(bf16[256,256]{1,0:T(8,128)(2,1)} %constant.20.clone.refs_3_) | copy-start | bytes 393220
  86.6 36.8 %copy-start.4 = (s32[4]{0:T(128)S(1)}, s32[4]{0:T(128)}, u32[]{:S(2)}) copy-start(s32[4]{0:T(128)} %centre.1) | copy-start | bytes 52
  86.6 36.8 %copy-start.5 = (f32[4]{0:T(128)S(1)}, f32[4]{0:T(128)}, u32[]{:S(2)}) copy-start(f32[4]{0:T(128)} %positions.1) | copy-start | bytes 52
  88.6 34.7 %collective-permute-start.1 = (f32[2,5,2,128,128]{4,3,2,1,0:T(8,128)S(1)}, f32[2,5,2,128,128]{4,3,2,1,0:T(8,128)}, u32[]{:S(2)}, u32[]{:S(2)}) collective-permute-start(f32[2,5,2,128,128]{4,3,2,1,0:T(8,128)S(1)} %get-tuple-element.15.upper), channel_id=1, source_target_pairs={{0,32},{32,64},{64,96},{1,33},{33,65},{65,97},{2,34},{34,66},{66,9... | collective-permute-start | bytes 3932168 | tf_op jit(solution)/shard_map/ppermute | solution.py:528
  96.4 13.4 %collective-permute-start = (f32[5,2,128,128]{3,2,1,0:T(8,128)S(1)}, f32[5,2,128,128]{3,2,1,0:T(8,128)S(1)}, u32[]{:S(2)}, u32[]{:S(2)}) collective-permute-start(f32[5,2,128,128]{3,2,1,0:T(8,128)S(1)} %inverse.2.refs_5_.s0), channel_id=1, source_target_pairs={{32,0},{64,32},{96,64},{33,1},{65,33},{97,65},{34,2},{66,34},{98,6... | collective-permute-start | bytes 1966088 | tf_op jit(solution)/shard_map/ppermute | solution.py:525
  98.3 18.7 %collective-permute-start.2 = (f32[5,2,128,128]{3,2,1,0:T(8,128)S(1)}, f32[5,2,128,128]{3,2,1,0:T(8,128)}, u32[]{:S(2)}, u32[]{:S(2)}) collective-permute-start(f32[5,2,128,128]{3,2,1,0:T(8,128)S(1)} %get-tuple-element.16.s1), channel_id=1, source_target_pairs={{32,0},{64,32},{96,64},{33,1},{65,33},{97,65},{34,2},{66,34},{98,6... | collective-permute-start | bytes 1966088 | tf_op jit(solution)/shard_map/ppermute | solution.py:527
  110.7 12.7 %all-to-all-start.2 = ((f32[128,1,128]{2,1,0:T(1,128)}), f32[128,1,128]{2,1,0:T(1,128)S(1)}, u32[]{:S(2)}, u32[]{:S(2)}) async-start(f32[128,1,128]{2,1,0:T(1,128)} %edge.1), calls=%async_computation.2 | async-start | bytes 131072 | tf_op jit(solution)/shard_map/all_to_all | solution.py:530
